TPU v7x, 256 devices: a whole 4x4x8 slice. The times are simulated.
256 devices in a mesh: context: 32 (over y, z), head: 2 (over core), dp: 4 (over x).
Axes of the slice: x: 4, y: 4, z: 8, core: 2. Of those that a mesh axis runs over, the one named last changes fastest.
Arguments:
- lin_query: float32 [16384, 4096], P(('dp', 'context'), 'head'), parts along dimension 0, may hold values from -6 to 6
- lin_key: float32 [16384, 4096], P(('dp', 'context'), 'head'), parts along dimension 0, may hold values from -6 to 6
- lin_value: float32 [16384, 4096], P(('dp', 'context'), 'head'), parts along dimension 0, may hold values from -6 to 6
- lin_gate: float32 [16384, 4096], P(('dp', 'context'), 'head'), parts along dimension 0, may hold values from -8 to 8
- decay_rate: float32 [32, 16384], P('head', ('dp', 'context')), parts along dimension 1, may hold values from 0 to 1.5, as said below
- norm_gain: float32 [4096], P('head'), may hold values from 0.5 to 1.5
- sm_query: float32 [16384, 4096], P(('dp', 'context'), 'head'), parts along dimension 0, may hold values from -24 to 24
- sm_key: float32 [16384, 512], P(('dp', 'context'), 'head'), parts along dimension 0, may hold values from -24 to 24
- sm_value: float32 [16384, 512], P(('dp', 'context'), 'head'), parts along dimension 0, may hold values from -6 to 6
- doc_lengths: int32 [64], P('dp'), parts along dimension 0, may hold values from 1 to 3072, 4096 in all
Outputs:
- lin_out: float32 [16384, 4096], P(('dp', 'context'), 'head'), parts along dimension 0
- sm_out: float32 [16384, 4096], P(('dp', 'context'), 'head'), parts along dimension 0
There are 4 independent parts, one for each index of `dp`. A program takes and returns all parts, laid end to end along the dimension named above; an argument that names none is the same for every part. Nothing has to cross between parts.
Inputs may be any that keep to these rules, and one draw needn't show every extreme that they name: `doc_lengths`: the 16 lengths sum to 4096 and the longest is exactly 3072. `decay_rate`: positive rates.
All inputs are finite; a program needn't handle non-finite values.
Results may differ from a plain program's by a relative error of at most 0.0003.
Values sent between devices are 32-bit elements; how exact they have to be, the bound alone decides.
No kernel may reach another device: no remote copies, remote signals or barrier semaphores. Data moves between devices by JAX's collectives and lax.ppermute only.
A program may use at most 192 MiB of HBM per device.

v0:
```python
import jax
import jax.numpy as jnp
from jax import lax
from jax.sharding import PartitionSpec as P

HEAD_DIM = 128
ROT_DIM = 64


rope_base = 10000000.0
norm_eps = 1e-05
highest = lax.Precision.HIGHEST


def entering(value, axis, join, neutral):
    count, mine = (lax.axis_size(axis), lax.axis_index(axis))
    pieces = jax.tree.map(lambda part: lax.all_gather(part, axis), value)
    subtotal = jax.tree.map(
        lambda part, zero: jnp.full_like(part, 0) + jnp.asarray(zero, part.dtype), value, neutral
    )

    def turn(position, subtotal):
        longer = join(subtotal, jax.tree.map(lambda part: part[position], pieces))
        return jax.tree.map(lambda new, old: jnp.where(position < mine, new, old), longer, subtotal)

    return lax.fori_loop(0, count - 1, turn, subtotal)


def doc_tables(doc_lengths):
    doc_ends = jnp.cumsum(doc_lengths)
    doc_starts = doc_ends - doc_lengths
    return (doc_starts, doc_ends)


def doc_number(tokens_at, doc_ends):
    return jnp.sum((doc_ends[None, :] <= tokens_at[:, None]).astype(jnp.int32), axis=1)


def doc_begin(tokens_at, doc_starts):
    picked = jnp.where(doc_starts[None, :] <= tokens_at[:, None], doc_starts[None, :], 0)
    return jnp.max(picked, axis=1)


def lightning_block(
    query_heads, key_heads, value_heads, forgetting_factors, first_token, doc_starts, doc_ends
):
    width = query_heads.shape[1]
    tokens_at = first_token + jnp.arange(width, dtype=jnp.int32)
    doc_ids = doc_number(tokens_at, doc_ends)
    begins = doc_begin(tokens_at, doc_starts)
    log_decay = jnp.cumsum(-forgetting_factors, axis=1)
    visible = (doc_ids[:, None] == doc_ids[None, :]) & (tokens_at[:, None] >= tokens_at[None, :])
    spread = jnp.where(visible[None], log_decay[:, :, None] - log_decay[:, None, :], 0.0)
    weight = jnp.where(visible[None], jnp.exp(spread), 0.0)
    scores = jnp.einsum("htd,hsd->hts", query_heads, key_heads, precision=highest) * weight
    intra = jnp.einsum("hts,hsd->htd", scores, value_heads, precision=highest)
    carried_rows = begins < first_token
    block_decay = jnp.where(carried_rows[-1], jnp.exp(log_decay[:, -1]), 0.0)
    in_tail = doc_ids == doc_ids[-1]
    tail_gap = jnp.where(in_tail[None], log_decay[:, -1:] - log_decay, 0.0)
    tail_weight = jnp.where(in_tail[None], jnp.exp(tail_gap), 0.0)
    block_inner = jnp.einsum(
        "htd,hte->hde", key_heads * tail_weight[:, :, None], value_heads, precision=highest
    )
    return (intra, log_decay, carried_rows, block_decay, block_inner)


def carried_term(query_heads, state, log_decay, carried_rows):
    reach_weight = jnp.where(carried_rows[None], jnp.exp(log_decay), 0.0)
    return (
        jnp.einsum("htd,hde->hte", query_heads, state, precision=highest) * reach_weight[:, :, None]
    )


def finish(attention, lin_gate, norm_gain):
    rows_count = attention.shape[0]
    per_head = attention.reshape(rows_count, -1, HEAD_DIM)
    mean_square = jnp.mean(per_head * per_head, axis=-1, keepdims=True)
    normed = (per_head / jnp.sqrt(mean_square + norm_eps)).reshape(rows_count, -1)
    return normed * norm_gain[None, :] * jax.nn.sigmoid(lin_gate)


def rotate(heads_in, positions):
    half = ROT_DIM // 2
    inverse = rope_base ** (-(2.0 * jnp.arange(half, dtype=jnp.float32)) / ROT_DIM)
    angle = positions.astype(jnp.float32)[:, None] * inverse[None, :]
    cosine = jnp.cos(angle)[:, None, :]
    sine = jnp.sin(angle)[:, None, :]
    first_half = heads_in[..., :half]
    second_half = heads_in[..., half:ROT_DIM]
    return jnp.concatenate(
        [
            first_half * cosine - second_half * sine,
            second_half * cosine + first_half * sine,
            heads_in[..., ROT_DIM:],
        ],
        axis=-1,
    )


def combine_states(earlier, later):
    return (earlier[0] * later[0], later[0][:, None, None] * earlier[1] + later[1])


def shards(
    lin_query,
    lin_key,
    lin_value,
    lin_gate,
    decay_rate,
    norm_gain,
    sm_query,
    sm_key,
    sm_value,
    doc_lengths,
):
    rows_here = lin_query.shape[0]
    lin_heads = lin_query.shape[1] // HEAD_DIM
    kv_local = sm_key.shape[1] // HEAD_DIM
    group = lin_heads // kv_local
    first_token = lax.axis_index("context") * rows_here
    doc_starts, doc_ends = doc_tables(doc_lengths)

    def split_heads(matrix):
        return matrix.reshape(rows_here, -1, HEAD_DIM).transpose(1, 0, 2)

    query_heads = split_heads(lin_query)
    intra, log_decay, carried_rows, block_decay, block_inner = lightning_block(
        query_heads,
        split_heads(lin_key),
        split_heads(lin_value),
        decay_rate,
        first_token,
        doc_starts,
        doc_ends,
    )
    identity = (jnp.ones_like(block_decay), jnp.zeros_like(block_inner))
    prior = entering((block_decay, block_inner), "context", combine_states, identity)
    state = prior[1]
    attention = intra + carried_term(query_heads, state, log_decay, carried_rows)
    attention = attention.transpose(1, 0, 2).reshape(rows_here, lin_heads * HEAD_DIM)
    lin_out = finish(attention, lin_gate, norm_gain)
    tokens_at = first_token + jnp.arange(rows_here, dtype=jnp.int32)
    positions = tokens_at - doc_begin(tokens_at, doc_starts)
    row_docs = doc_number(tokens_at, doc_ends)
    first_begin = doc_begin(first_token[None], doc_starts)[0]
    last_token = first_token + rows_here - 1
    queries = rotate(sm_query.reshape(rows_here, lin_heads, HEAD_DIM), positions)
    queries = queries.reshape(rows_here, kv_local, group, HEAD_DIM).transpose(1, 2, 0, 3)
    keys_rot = rotate(sm_key.reshape(rows_here, kv_local, HEAD_DIM), positions).reshape(
        rows_here, kv_local * HEAD_DIM
    )
    stacked = jnp.stack([keys_rot, sm_value])
    scale = HEAD_DIM ** (-0.5)
    start_carry = (
        jnp.full((kv_local, group, rows_here), -1e30, jnp.float32),
        jnp.zeros((kv_local, group, rows_here), jnp.float32),
        jnp.zeros((kv_local, group, rows_here, HEAD_DIM), jnp.float32),
    )
    piece = lax.all_gather(stacked, "context", axis=1, tiled=True)
    start = jnp.int32(0)
    count = piece.shape[1]
    relevant = (start <= last_token) & (start + count - 1 >= first_begin)

    def attend(current):
        top_old, total_old, summed_old = current
        key_index = jnp.arange(count, dtype=jnp.int32)
        key_docs = doc_number(key_index, doc_ends)
        visible = (
            (key_index[None, :] >= 0)
            & (key_docs[None, :] == row_docs[:, None])
            & (key_index[None, :] <= tokens_at[:, None])
        )
        key_rows = piece[0].reshape(count, kv_local, HEAD_DIM)
        value_rows = piece[1].reshape(count, kv_local, HEAD_DIM)
        scores = jnp.einsum("kgqd,nkd->kgqn", queries, key_rows, precision=highest) * scale
        masked = jnp.where(visible[None, None], scores, -jnp.inf)
        top_new = jnp.maximum(top_old, jnp.max(masked, axis=-1))
        weights = jnp.where(visible[None, None], jnp.exp(masked - top_new[..., None]), 0.0)
        total_new = jnp.sum(weights, axis=-1)
        summed_new = jnp.einsum("kgqn,nkd->kgqd", weights, value_rows, precision=highest)
        return (top_new, total_new, summed_new)

    def keep(current):
        return current

    final_carry = lax.cond(relevant, attend, keep, start_carry)
    mixed = final_carry[2] / final_carry[1][..., None]
    sm_out = mixed.transpose(2, 0, 1, 3).reshape(rows_here, lin_heads * HEAD_DIM)
    return (lin_out, sm_out)


def solution(mesh):
    in_specs = (
        P(("dp", "context"), "head"),
        P(("dp", "context"), "head"),
        P(("dp", "context"), "head"),
        P(("dp", "context"), "head"),
        P("head", ("dp", "context")),
        P("head"),
        P(("dp", "context"), "head"),
        P(("dp", "context"), "head"),
        P(("dp", "context"), "head"),
        P("dp"),
    )
    out_specs = (P(("dp", "context"), "head"), P(("dp", "context"), "head"))
    return jax.shard_map(shards, mesh=mesh, in_specs=in_specs, out_specs=out_specs, check_vma=False)
```

profile of v0, /device:TPU:13, one launch (start us, length us, event | category | flops | bytes accessed | tf_op | source)
XLA Modules:
  0.0 410.7 jit_solution(14850499489194038331)
XLA Ops:
  7.2 0.8 copy.87
  8.2 1.3 fusion.22
  9.7 1.0 copy.114
  10.7 1.0 copy.95
  11.9 0.7 pad_maximum_fusion.1
  12.7 0.6 slice.38
  13.2 0.6 broadcast_compare_fusion
  13.9 0.6 slice.36
  14.5 0.7 neg.14
  15.2 1.5 copy.111
  17.0 0.9 slice_reduce_fusion
  18.0 3.4 fusion.15
  21.6 1.4 copy.121
  23.3 1.3 copy.117
  25.3 1.3 dynamic-slice
  27.5 52.9 %all-reduce = f32[512]{0:T(512)S(1)} all-reduce(f32[512]{0:T(512)S(1)} %dynamic-update-slice), channel_id=2, replica_groups=mesh['context'=32,'head'=2,'dp'=4] {'context'}, use_global_device_ids=true, to_apply=%add | all-reduce | flops 512 | bytes 4096
  80.5 1.4 copy.120
  82.2 0.6 multiply_subtract_fusion
  82.9 2.9 pad_maximum_fusion
  85.9 2.5 convolution_multiply_fusion
  88.4 2.0 convolution_bitcast_fusion.1
  90.4 25.3 %all-gather.5.cloned.1.call-done = f32[2,4096,256]{1,2,0:T(8,128)} async-done(((f32[2,128,256]{1,2,0:T(8,128)}), f32[2,4096,256]{1,2,0:T(8,128)}) %all-gather.5.cloned.1.call-update) | async-done | bytes 8388624 | tf_op jit(solution)/shard_map/all_gather | solution.py:160
  115.7 92.2 %conditional.1 = (f32[2,8,128]{2,1,0:T(8,128)S(1)}, f32[2,8,128,128]{3,2,1,0:T(8,128)S(1)}) conditional(s32[]{:T(128)} %convert_element_type.19, () %tuple.31, (s32[16]{0:T(128)S(1)}, s32[128]{0:T(128)S(1)}, s32[]{:T(128)}, s32[128]{0:T(128)S(1)}, f32[2,4096,256]{1,2,0:T(8,128)}, /*index=5*/f32[2,8,128,128]{3,2,1,0:T(8,128)}) %tuple.67), branch_computations={%region_8.9_spmd, %region_9.13_spmd} | conditional | flops 25872230400 | bytes 130107472 | solution.py:187
  116.4 4.0 fusion.23
  120.4 35.2 %fusion = (f32[2,8,128]{2,1,0:T(8,128)S(1)}, f32[2,8,128,4096]{3,2,1,0:T(8,128)}) fusion(pred[128,4096]{1,0:T(8,128)(4,1)S(1)} %fusion.8, f32[2,8,128,128]{3,2,1,0:T(8,128)} %get-tuple-element.111, f32[4096,2,128,1]{0,2,3,1:T(8,128)S(1)} %bitcast.95), kind=kOutput, calls=%fused_computation.2 | convolution fusion | flops 12910065664 | bytes 39329792 | tf_op jit(solution)/shard_map/cond/branch_1_fun/kgqd,nkd->kgqn/dot_general | solution.py:176
  155.6 35.1 %fusion.1 = f32[2,8,128,128]{3,2,1,0:T(8,128)S(1)} fusion(f32[4096,2,128,1]{0,2,3,1:T(8,128)S(1)} %bitcast.103, f32[2,8,128,4096]{3,2,1,0:T(8,128)} %get-tuple-element.158, f32[2,8,128]{2,1,0:T(8,128)S(1)} %broadcast_maximum_fusion, pred[128,4096]{1,0:T(8,128)(4,1)S(1)} %fusion.8), kind=kOutput, calls=%fused_computation.3 | convolution fusion | flops 12918456320 | bytes 39329792 | tf_op jit(solution)/shard_map/cond/branch_1_fun/kgqn,nkd->kgqd/dot_general | solution.py:181
  190.7 16.9 %fusion.2 = f32[2,8,128]{2,1,0:T(8,128)S(1)} fusion(f32[2,8,128,4096]{3,2,1,0:T(8,128)} %get-tuple-element.158, f32[2,8,128]{2,1,0:T(8,128)S(1)} %broadcast_maximum_fusion, pred[128,4096]{1,0:T(8,128)(4,1)S(1)} %fusion.8), kind=kLoop, calls=%fused_computation.4 | loop fusion | flops 41940992 | bytes 34095104 | tf_op jit(solution)/shard_map/cond/branch_1_fun/reduce_sum | solution.py:180
  208.3 0.6 copy.101
  208.9 1.3 copy.144
  210.2 142.4 %all-gather.7.cloned.1.call-done = f32[512,128,128]{2,1,0:T(8,128)} async-done(((f32[16,128,128]{2,1,0:T(8,128)}), f32[512,128,128]{2,1,0:T(8,128)}) %all-gather.7.cloned.1.call-update) | async-done | bytes 33554448 | tf_op jit(solution)/shard_map/all_gather | solution.py:17
  352.6 46.4 %while.14 = (s32[]{:T(128)}, f32[16,128,128]{2,1,0:T(8,128)S(1)}, s32[]{:T(128)}, f32[32,16]{1,0:T(8,128)S(1)}, f32[32,16,128,128]{3,2,1,0:T(8,128)}, /*index=5*/s32[]{:T(128)}, s32[]{:T(128)}) while((s32[]{:T(128)}, f32[16,128,128]{2,1,0:T(8,128)S(1)}, s32[]{:T(128)}, f32[32,16]{1,0:T(8,128)S(1)}, f32[32,16,128,128]{3,2,1,0:T(8,128)}, ...), condition=%wide.region_5.6_spmd.clone, body=%wide.region_4.5_spmd.clone.sunk | while | flops 1048580 | bytes 3146025 | solution.py:26
  352.6 1.5 fusion.35
  354.1 1.5 fusion.35
  355.6 1.5 fusion.35
  357.1 1.5 fusion.35
  358.6 1.5 fusion.35
  360.1 1.5 fusion.35
  361.6 1.5 fusion.35
  363.1 1.5 fusion.35
  364.6 1.5 fusion.35
  366.1 1.5 fusion.35
  367.6 1.5 fusion.35
  369.1 1.5 fusion.35
  370.6 1.5 fusion.35
  372.1 1.5 fusion.35
  373.6 1.5 fusion.35
  375.1 1.5 fusion.35
  376.6 1.5 fusion.35
  378.1 1.5 fusion.35
  379.6 1.5 fusion.35
  381.1 1.5 fusion.35
  382.6 1.5 fusion.35
  384.1 1.5 fusion.35
  385.6 1.5 fusion.35
  387.1 1.5 fusion.35
  388.6 1.5 fusion.35
  390.1 1.5 fusion.35
  391.6 1.5 fusion.35
  393.1 1.5 fusion.35
  394.6 1.5 fusion.35
  396.1 1.5 fusion.35
  397.6 1.5 fusion.35
  399.0 1.9 multiply_reduce_fusion
  401.4 2.5 divide_multiply_fusion
  (71 shorter events, 3.9 us)
Async XLA Ops:
  7.2 78.7 %copy-start = (f32[128,2048]{1,0:T(8,128)S(1)}, f32[128,2048]{1,0:T(8,128)}, u32[]{:S(2)}) copy-start(f32[128,2048]{1,0:T(8,128)} %param.14) | copy-start | bytes 3145732
  7.2 108.5 %all-gather.5.cloned.1.call-start = ((), (), s32[]{:S(2)}) async-start(), calls=%async_computation | async-start | bytes 8650752 | tf_op jit(solution)/shard_map/all_gather | solution.py:160
  12.6 340.0 %all-gather.7.cloned.1.call-start = ((), (), s32[]{:S(2)}) async-start(), calls=%async_computation.1 | async-start | bytes 34603008 | tf_op jit(solution)/shard_map/all_gather | solution.py:17
  16.7 4.8 %copy-start.1 = (f32[128,2048]{0,1:T(8,128)}, f32[128,2048]{0,1:T(8,128)S(1)}, u32[]{:S(2)}) copy-start(f32[128,2048]{0,1:T(8,128)S(1)} %copy.111) | copy-start | bytes 3145732
  115.7 285.7 %copy-start.2 = (f32[2048]{0:T(1024)S(1)}, f32[2048]{0:T(1024)}, u32[]{:S(2)}) copy-start(f32[2048]{0:T(1024)} %param.19) | copy-start | bytes 24580
Sparse Core Ops, SparseCore 0:
  12.7 102.9 all-gather.4
  118.9 233.6 all-gather.6
where the time goes:
time: 415 us; the launch traced here: 411 us
  waiting for transfers between devices  168 us (40%)
  matrix products  80.1 us (19%)
  other arithmetic  74.4 us (18%)
  blocking collectives  52.9 us (13%)
  local copies, waits for them, and re-layouts  18.7 us (5%)
  between operations  15.6 us (4%)
    all_gather x1, waiting for transfers between devices, entering(): pieces = jax.tree.map(lambda part: lax.all_gather(part, axis), value)  142 us
    unnamed x1, blocking collectives  52.9 us
    select_n x31, other arithmetic, turn(): jnp.where(position < mine, new, old)  45.2 us
    dot_general x1, matrix products, attend(): jnp.einsum('kgqd,nkd->kgqn', queries, key_rows, precision=highest) * scale  35.2 us
    dot_general x1, matrix products, attend(): jnp.einsum('kgqn,nkd->kgqd', weights, value_rows, precision=highest)  35.1 us
    all_gather x1, waiting for transfers between devices, shards(): piece = lax.all_gather(stacked, 'context', axis=1, tiled=True)  25.3 us
    reduce_sum x1, other arithmetic, attend(): total_new = jnp.sum(weights, axis=-1)  16.9 us
  transfers between devices with their start and end apart: 2, of which 2 were waited for; matrix products, arithmetic and copies ran while one was open for 29% of the time, Pallas kernels for 0%

commit v1 on v0

v1 whole, which is shorter than its diff:
```python
import functools
import math

import jax
import jax.numpy as jnp
import numpy as np
from jax import lax
from jax.experimental import pallas as pl
from jax.experimental.pallas import tpu as pltpu
from jax.sharding import Mesh, PartitionSpec as P

HEAD_DIM = 128
ROT_DIM = 64
TOK = 128
DOCS = 16
CHUNK = 512
NEG = -1e30
ROPE_BASE = 10000000.0
NORM_EPS = 1e-05
F32 = jnp.float32
BF16 = jnp.bfloat16

INVERSE = np.power(
    ROPE_BASE, -(2.0 * np.arange(ROT_DIM // 2, dtype=np.float64)) / ROT_DIM
).astype(np.float32)

SMEM = pl.BlockSpec(memory_space=pltpu.SMEM)


def built(kernel, out_shape, shapes, scratch=(), flops=1_000_000, moved=1_000_000, limit=20):
    def whole(shape):
        return pl.BlockSpec(shape, lambda i: (0,) * len(shape))

    many = isinstance(out_shape, (tuple, list))
    return pl.pallas_call(
        kernel,
        out_shape=out_shape,
        grid=(1,),
        in_specs=[SMEM] + [whole(shape) for shape in shapes],
        out_specs=[whole(o.shape) for o in out_shape] if many else whole(out_shape.shape),
        scratch_shapes=list(scratch),
        compiler_params=pltpu.CompilerParams(vmem_limit_bytes=limit << 20),
        cost_estimate=pl.CostEstimate(
            flops=flops, bytes_accessed=moved, transcendentals=0
        ),
    )


def call(kernel, out_shape, n_in, **options):
    def run(lengths, *arrays):
        return built(kernel, out_shape, [a.shape for a in arrays], **options)(lengths, *arrays)

    return run


def halves(x):
    high = x.astype(BF16)
    return high, (x - high.astype(F32)).astype(BF16)


def dot(a, b, ca, cb):
    return lax.dot_general(a, b, (((ca,), (cb,)), ((), ())), preferred_element_type=F32)


def dot3(a, b, ca, cb):
    ah, al = halves(a)
    bh, bl = halves(b)
    return dot(ah, bh, ca, cb) + (dot(ah, bl, ca, cb) + dot(al, bh, ca, cb))


def begins_of(lengths_ref, tokens):
    begin = jnp.zeros_like(tokens)
    start = jnp.int32(0)
    for d in range(DOCS - 1):
        start = start + lengths_ref[d]
        begin = jnp.where(tokens >= start, start, begin)
    return begin


def begin_scalar(lengths_ref, token):
    begin = jnp.int32(0)
    start = jnp.int32(0)
    for d in range(DOCS - 1):
        start = start + lengths_ref[d]
        begin = jnp.where(token >= start, start, begin)
    return begin


def block_of():
    return lax.axis_index("y") * lax.axis_size("z") + lax.axis_index("z")


def rope_tables(lengths_ref, inverse_ref, first):
    rows = first + lax.broadcasted_iota(jnp.int32, (TOK, HEAD_DIM), 0)
    lane = lax.broadcasted_iota(jnp.int32, (TOK, HEAD_DIM), 1)
    position = (rows - begins_of(lengths_ref, rows)).astype(F32)
    angle = position * inverse_ref[...]
    rotated = lane < ROT_DIM
    cosine = jnp.where(rotated, jnp.cos(angle), 1.0)
    sine = jnp.sin(angle)
    low = jnp.where(lane < ROT_DIM // 2, -sine, 0.0)
    high = jnp.where(rotated & (lane >= ROT_DIM // 2), sine, 0.0)
    return cosine, low, high


def rotated(x, tables):
    cosine, low, high = tables
    half = ROT_DIM // 2
    return (
        x * cosine
        + pltpu.roll(x, HEAD_DIM - half, 1) * low
        + pltpu.roll(x, half, 1) * high
    )


def kv_kernel(lengths_ref, inverse_ref, key_ref, value_ref, tables_ref, *pieces):
    tables = rope_tables(lengths_ref, inverse_ref, block_of() * TOK)
    for i in range(3):
        tables_ref[i] = tables[i]
    mine = lax.axis_index("y")
    for a in range(2):
        lanes = slice(a * HEAD_DIM, (a + 1) * HEAD_DIM)
        k = rotated(key_ref[:, lanes], tables)
        v = value_ref[:, lanes]
        for r in range(4):
            for b, x in ((0, k), (1, v)):

                @pl.when((mine + r) % 4 == 2 * a + b)
                def _():
                    pieces[r][...] = x


def query_kernel(lengths_ref, tables_ref, query_ref, *pieces):
    tables = [tables_ref[i] for i in range(3)]
    mine = lax.axis_index("y")
    scale = math.log2(math.e) / math.sqrt(HEAD_DIM)
    for r in range(4):
        e = (mine + r) % 4
        for n in range(4):
            at = pl.multiple_of(e * (4 * HEAD_DIM) + n * HEAD_DIM, HEAD_DIM)
            x = query_ref[:, pl.ds(at, HEAD_DIM)]
            pieces[r][:, n * HEAD_DIM : (n + 1) * HEAD_DIM] = rotated(x, tables) * scale


def softmax_kernel(lengths_ref, *refs):
    queries, kv_ref, outs = refs[:4], refs[4], refs[5:9]
    kcat, vcat, qcat, s_ref, m_ref, l_ref, acc_ref = refs[9:]
    z = lax.axis_index("z")
    zs = kv_ref.shape[0]
    e_key = 2 * (lax.axis_index("y") % 2)
    e = e_key + lax.axis_index("head")
    last = 3 * zs + z

    @pl.loop(0, last + 1)
    def _(b):
        at = pl.multiple_of(b * TOK, TOK)
        kh, kl = halves(kv_ref[b % zs, 0, (e_key - b // zs + 4) % 4])
        vh, vl = halves(kv_ref[b % zs, 1, (e_key + 1 - b // zs + 4) % 4])
        kcat[pl.ds(at, TOK), 0:128] = kh
        kcat[pl.ds(at, TOK), 128:256] = kh
        kcat[pl.ds(at, TOK), 256:384] = kl
        vcat[pl.ds(at, TOK), 0:128] = vh
        vcat[pl.ds(at, TOK), 128:256] = vl

    @pl.loop(last + 1, 4 * zs)
    def _(b):
        at = pl.multiple_of(b * TOK, TOK)
        kcat[pl.ds(at, TOK), :] = jnp.zeros((TOK, 384), BF16)
        vcat[pl.ds(at, TOK), :] = jnp.zeros((TOK, 256), BF16)

    for r in range(4):
        block = ((e - r + 4) % 4) * zs + z
        first = block * TOK
        rows = first + lax.broadcasted_iota(jnp.int32, (TOK, CHUNK), 0)
        begin = begins_of(lengths_ref, rows)
        for n in range(4):
            qh, ql = halves(queries[r][:, n * HEAD_DIM : (n + 1) * HEAD_DIM])
            qcat[n * TOK : (n + 1) * TOK, 0:128] = qh
            qcat[n * TOK : (n + 1) * TOK, 128:256] = ql
            qcat[n * TOK : (n + 1) * TOK, 256:384] = qh
        low = begin_scalar(lengths_ref, first) // CHUNK
        high = first // CHUNK + 1
        inner = (begin_scalar(lengths_ref, first + TOK - 1) + CHUNK - 1) // CHUNK
        inner = jnp.minimum(inner, high)
        outer = jnp.maximum(inner, high - 1)
        m_ref[...] = jnp.full_like(m_ref, NEG)
        l_ref[...] = jnp.zeros_like(l_ref)
        acc_ref[...] = jnp.zeros_like(acc_ref)

        def score(j, masked):
            at = pl.multiple_of(j * CHUNK, CHUNK)
            s = dot(qcat[...], kcat[pl.ds(at, CHUNK), :], 1, 1)
            if masked:
                keys = at + lax.broadcasted_iota(jnp.int32, (TOK, CHUNK), 1)
                visible = (keys >= begin) & (keys <= rows)
                s = jnp.where(visible[None], s.reshape(4, TOK, CHUNK), NEG)
                s = s.reshape(4 * TOK, CHUNK)
            s_ref[j] = s
            top = s[:, :HEAD_DIM]
            for i in range(1, CHUNK // HEAD_DIM):
                top = jnp.maximum(top, s[:, i * HEAD_DIM : (i + 1) * HEAD_DIM])
            m_ref[...] = jnp.maximum(m_ref[...], top)

        pl.loop(low, inner)(lambda j: score(j, True))
        pl.loop(inner, outer)(lambda j: score(j, False))
        pl.loop(outer, high)(lambda j: score(j, True))

        top = jnp.max(m_ref[...], axis=1, keepdims=True)
        m_ref[...] = jnp.broadcast_to(top, m_ref.shape)

        @pl.loop(low, high)
        def _(j):
            at = pl.multiple_of(j * CHUNK, CHUNK)
            top = m_ref[...]
            highs, lows, total = [], [], l_ref[...]
            for i in range(CHUNK // HEAD_DIM):
                p = jnp.exp2(s_ref[j, :, i * HEAD_DIM : (i + 1) * HEAD_DIM] - top)
                total = total + p
                ph, pl_ = halves(p)
                highs.append(ph)
                lows.append(pl_)
            l_ref[...] = total
            v = vcat[pl.ds(at, CHUNK), :]
            p = jnp.concatenate(highs + lows, axis=1)
            acc_ref[...] += dot(p, jnp.concatenate([v, v], axis=0), 1, 0)

        total = jnp.sum(l_ref[...], axis=1, keepdims=True)
        mixed = (acc_ref[:, :HEAD_DIM] + acc_ref[:, HEAD_DIM:]) / total
        for n in range(4):
            outs[r][:, n * HEAD_DIM : (n + 1) * HEAD_DIM] = mixed[n * TOK : (n + 1) * TOK]


def place_kernel(lengths_ref, *refs):
    pieces, out_ref = refs[:4], refs[4]
    mine = lax.axis_index("y")
    width = 4 * HEAD_DIM
    for r in range(4):
        at = pl.multiple_of(((mine + r) % 4) * width, width)
        out_ref[:, pl.ds(at, width)] = pieces[r][...]


def thirds(x):
    high = x.astype(BF16)
    rest = x - high.astype(F32)
    mid = rest.astype(BF16)
    return high, mid, (rest - mid.astype(F32)).astype(BF16)


def dot6(a, b, ca, cb):
    ah, am, al = thirds(a)
    bh, bm, bl = thirds(b)
    small = dot(ah, bl, ca, cb) + dot(al, bh, ca, cb) + dot(am, bm, ca, cb)
    return dot(ah, bh, ca, cb) + (dot(ah, bm, ca, cb) + dot(am, bh, ca, cb) + small)


def decay_columns(rate_ref):
    t = lax.broadcasted_iota(jnp.int32, (TOK, TOK), 0)
    s = lax.broadcasted_iota(jnp.int32, (TOK, TOK), 1)
    lower = jnp.where(s <= t, 1.0, 0.0).astype(BF16)
    parts = [dot(lower, x, 1, 1) for x in thirds(-rate_ref[...])]
    return parts[0] + (parts[1] + parts[2])


def decay_rows(rate_ref):
    s = lax.broadcasted_iota(jnp.int32, (TOK, TOK), 0)
    t = lax.broadcasted_iota(jnp.int32, (TOK, TOK), 1)
    upper = jnp.where(s <= t, 1.0, 0.0).astype(BF16)
    parts = [dot(x, upper, 1, 0) for x in thirds(-rate_ref[...])]
    return parts[0] + (parts[1] + parts[2])


def state_kernel(lengths_ref, rate_ref, key_ref, value_ref, out_ref):
    heads = rate_ref.shape[0]
    first = block_of() * TOK
    tail = begin_scalar(lengths_ref, first + TOK - 1)
    columns = decay_columns(rate_ref)
    rows = first + lax.broadcasted_iota(jnp.int32, (TOK, heads), 0)
    end = columns[TOK - 1 : TOK, :]
    weight = jnp.where(
        rows >= tail, jnp.exp(jnp.where(rows >= tail, end - columns, 0.0)), 0.0
    )
    carried = jnp.where(tail < first, jnp.exp(end), 0.0)
    half = HEAD_DIM // 2
    for h in range(heads):
        lanes = slice(h * HEAD_DIM, (h + 1) * HEAD_DIM)
        k = key_ref[:, lanes] * weight[:, h : h + 1]
        inner = dot3(k, value_ref[:, lanes], 0, 0)
        kept = jnp.broadcast_to(carried[:, h : h + 1], (8, HEAD_DIM))
        for i in range(2):
            out_ref[2 * h + i, :half] = inner[i * half : (i + 1) * half]
            out_ref[2 * h + i, half:] = kept


def prefix_kernel(lengths_ref, in_ref, out_ref):
    blocks, half = out_ref.shape[0], out_ref.shape[1]
    state = jnp.zeros(out_ref.shape[1:], F32)
    for i in range(blocks):
        out_ref[i] = state
        if i < blocks - 1:
            state = in_ref[i, half : half + 1, :] * state + in_ref[i, :half, :]


def intra_kernel(lengths_ref, rate_ref, query_ref, key_ref, value_ref, out_ref):
    heads = rate_ref.shape[0]
    first = block_of() * TOK
    columns = decay_columns(rate_ref)
    across = decay_rows(rate_ref)
    t = first + lax.broadcasted_iota(jnp.int32, (TOK, TOK), 0)
    s = first + lax.broadcasted_iota(jnp.int32, (TOK, TOK), 1)
    visible = (s <= t) & (s >= begins_of(lengths_ref, t))
    for h in range(heads):
        lanes = slice(h * HEAD_DIM, (h + 1) * HEAD_DIM)
        gap = jnp.where(visible, columns[:, h : h + 1] - across[h : h + 1, :], 0.0)
        weight = jnp.where(visible, jnp.exp(gap), 0.0)
        scores = dot6(query_ref[:, lanes], key_ref[:, lanes], 1, 1) * weight
        out_ref[:, lanes] = dot3(scores, value_ref[:, lanes], 1, 0)


def finish_kernel(
    lengths_ref, rate_ref, query_ref, state_ref, intra_ref, gate_ref, gain_ref, out_ref
):
    heads = rate_ref.shape[0]
    first = block_of() * TOK
    columns = decay_columns(rate_ref)
    rows = first + lax.broadcasted_iota(jnp.int32, (TOK, heads), 0)
    carried = begins_of(lengths_ref, rows) < first
    reach = jnp.where(carried, jnp.exp(columns), 0.0)
    for h in range(heads):
        lanes = slice(h * HEAD_DIM, (h + 1) * HEAD_DIM)
        x = intra_ref[:, lanes] + dot3(query_ref[:, lanes], state_ref[h], 1, 0) * reach[
            :, h : h + 1
        ]
        mean = jnp.mean(x * x, axis=1, keepdims=True)
        normed = x / jnp.sqrt(mean + NORM_EPS)
        gate = 1.0 / (1.0 + jnp.exp(-gate_ref[:, lanes]))
        out_ref[:, lanes] = normed * gain_ref[:, lanes] * gate


def shards(
    lin_query,
    lin_key,
    lin_value,
    lin_gate,
    decay_rate,
    norm_gain,
    sm_query,
    sm_key,
    sm_value,
    doc_lengths,
):
    rows, width = lin_query.shape
    heads = width // HEAD_DIM
    ys, zs = lax.axis_size("y"), lax.axis_size("z")
    blocks = ys * zs
    group = ("y", "head")
    out = jax.ShapeDtypeStruct
    forth, back = [], []
    for r in range(4):
        pairs = []
        for y in range(ys):
            for h in range(2):
                piece = (y + r) % 4
                pairs.append((2 * y + h, 2 * (2 * h + piece // 2) + piece % 2))
        forth.append(pairs)
        back.append([(b, a) for a, b in pairs])

    inverse = np.zeros((1, HEAD_DIM), np.float32)
    inverse[0, :ROT_DIM] = np.tile(INVERSE, 2)
    tables, *kv_pieces = call(
        kv_kernel,
        [out((3, rows, HEAD_DIM), F32)] + [out((rows, HEAD_DIM), F32)] * 4,
        4,
        moved=800_000,
        limit=60,
    )(doc_lengths, jnp.asarray(inverse), sm_key, sm_value)
    kv_here = [lax.ppermute(p, group, forth[r]) for r, p in enumerate(kv_pieces)]
    kv = lax.all_gather(jnp.stack(kv_here), ("z", "head"), axis=0, tiled=False)
    kv = kv.reshape(zs, 2, ys, rows, HEAD_DIM)

    sliced = call(
        state_kernel,
        out((blocks, HEAD_DIM // 2 + 8, HEAD_DIM), F32),
        4,
        flops=6 * heads * HEAD_DIM**3,
        moved=3_300_000,
        limit=60,
    )(doc_lengths, decay_rate, lin_key, lin_value)
    arrived = lax.all_to_all(sliced, ("y", "z"), 0, 0, tiled=True)

    q_pieces = call(
        query_kernel, [out((rows, 4 * HEAD_DIM), F32)] * 4, 3, moved=2_200_000
    )(doc_lengths, tables, sm_query)
    queries = [lax.ppermute(p, group, forth[r]) for r, p in enumerate(q_pieces)]

    intra = call(
        intra_kernel,
        out((rows, width), F32),
        5,
        flops=12 * heads * HEAD_DIM**3,
        moved=4_200_000,
    )(doc_lengths, decay_rate, lin_query, lin_key, lin_value)

    arrived, intra, *queries = lax.optimization_barrier((arrived, intra, *queries))
    prefixes = call(
        prefix_kernel, out((blocks, HEAD_DIM // 2, HEAD_DIM), F32), 2, moved=2_200_000
    )(doc_lengths, arrived)
    state = lax.all_to_all(prefixes, ("y", "z"), 0, 0, tiled=True)
    state = state.reshape(heads, HEAD_DIM, HEAD_DIM)

    mixed = call(
        softmax_kernel,
        [out((rows, 4 * HEAD_DIM), F32)] * 4,
        6,
        scratch=[
            pltpu.VMEM((blocks * TOK, 384), BF16),
            pltpu.VMEM((blocks * TOK, 256), BF16),
            pltpu.VMEM((4 * TOK, 384), BF16),
            pltpu.VMEM((blocks * TOK // CHUNK, 4 * TOK, CHUNK), F32),
            pltpu.VMEM((4 * TOK, HEAD_DIM), F32),
            pltpu.VMEM((4 * TOK, HEAD_DIM), F32),
            pltpu.VMEM((4 * TOK, 2 * HEAD_DIM), F32),
        ],
        limit=32,
        flops=6 * 50 * 4 * 2 * 128**3,
        moved=6_000_000,
    )(doc_lengths, *queries, kv)
    returned = [lax.ppermute(p, group, back[r]) for r, p in enumerate(mixed)]

    lin_out = call(
        finish_kernel,
        out((rows, width), F32),
        7,
        flops=6 * heads * HEAD_DIM**3,
        moved=5_200_000,
    )(doc_lengths, decay_rate, lin_query, state, intra, lin_gate, norm_gain.reshape(1, width))
    sm_out = call(place_kernel, out((rows, width), F32), 5, moved=2_000_000)(
        doc_lengths, *returned
    )
    return (lin_out, sm_out)


def solution(mesh):
    sizes = mesh.shape
    ring = 4
    inner = Mesh(
        mesh.devices.reshape(ring, sizes["context"] // ring, sizes["head"], sizes["dp"]),
        ("y", "z", "head", "dp"),
    )
    tokens = ("dp", "y", "z")
    wide = P(tokens, "head")
    in_specs = (
        wide,
        wide,
        wide,
        wide,
        P("head", tokens),
        P("head"),
        wide,
        wide,
        wide,
        P("dp"),
    )
    return jax.shard_map(
        shards, mesh=inner, in_specs=in_specs, out_specs=(wide, wide), check_vma=False
    )
```

time: 415 us -> 146 us (0.35)
  waiting for transfers between devices: 168 us -> 28.5 us
  matrix products: 80.1 us -> 0 us
  other arithmetic: 74.4 us -> 0.73 us
  blocking collectives: 52.9 us -> 0 us
  starting transfers between devices: 0.08 us -> 50.2 us
  Pallas kernels: 0 us -> 40.9 us
  local copies, waits for them, and re-layouts: 18.7 us -> 10.7 us
    all_gather x2 -> x1, waiting for transfers between devices: 168 us -> 0.98 us  [shards(): kv = lax.all_gather(jnp.stack(kv_here), ('z', 'head'), axis=0, tiled=False)]
    dot_general x6 -> x0, matrix products: 80.1 us -> none  [the longest x1 35.2 us: attend(): jnp.einsum('kgqd,nkd->kgqn', queries, key_rows, precision=highest) * scale]
    unnamed x1 -> x0, blocking collectives: 52.9 us -> none
    select_n x32 -> x0, other arithmetic: 45.3 us -> none  [the longest x31 45.2 us: turn(): jnp.where(position < mine, new, old)]
    pallas_call x0 -> x8, Pallas kernels: none -> 40.9 us  [run(): built(kernel, out_shape, [a.shape for a in arrays], **options)]
    ppermute x0 -> x12, starting transfers between devices: none -> 31.7 us  [the longest x4 11 us: shards(): queries = [lax.ppermute(p, group, forth[r]) for r, p in enumerate(q_pieces)]]
    all_to_all x0 -> x2, starting transfers between devices: none -> 18.5 us  [the longest x1 9.67 us: shards(): arrived = lax.all_to_all(sliced, ('y', 'z'), 0, 0, tiled=True)]
    reduce_sum x2 -> x0, other arithmetic: 17.1 us -> none  [the longest x1 16.9 us: attend(): total_new = jnp.sum(weights, axis=-1)]
  transfers between devices with their start and end apart: 2 -> 15, of which waited for: 2 -> 8; matrix products, arithmetic and copies ran while one was open for 29% -> 0% of each run, Pallas kernels for 0% -> 25%
where the time goes in v1:
time: 146 us; the launch traced here: 145 us
  starting transfers between devices  50.2 us (34%)
  Pallas kernels  40.9 us (28%)
  waiting for transfers between devices  28.5 us (20%)
  between operations  14.3 us (10%)
  local copies, waits for them, and re-layouts  10.7 us (7%)
    pallas_call x8, Pallas kernels, run(): built(kernel, out_shape, [a.shape for a in arrays], **options)  40.9 us
    all_to_all x1, waiting for transfers between devices, shards(): arrived = lax.all_to_all(sliced, ('y', 'z'), 0, 0, tiled=True)  13.2 us
    ppermute x4, starting transfers between devices, shards(): queries = [lax.ppermute(p, group, forth[r]) for r, p in enumerate(q_pieces)]  11 us
    ppermute x4, starting transfers between devices, shards(): lax.ppermute(p, group, forth[r])  10.8 us
    unnamed x36, local copies, waits for them, and re-layouts  10.7 us
    ppermute x4, starting transfers between devices, shards(): returned = [lax.ppermute(p, group, back[r]) for r, p in enumerate(mixed)]  10 us
    all_to_all x1, starting transfers between devices, shards(): arrived = lax.all_to_all(sliced, ('y', 'z'), 0, 0, tiled=True)  9.67 us
    all_to_all x1, starting transfers between devices, shards(): state = lax.all_to_all(prefixes, ('y', 'z'), 0, 0, tiled=True)  8.79 us
  transfers between devices with their start and end apart: 15, of which 8 were waited for; matrix products, arithmetic and copies ran while one was open for 0% of the time, Pallas kernels for 25%

profile of v1, /device:TPU:13, one launch (start us, length us, event | category | flops | bytes accessed | tf_op | source)
XLA Modules:
  0.0 145.3 jit_solution(5067997025002299029)
XLA Ops:
  7.2 0.0 all-gather.3.cloned.1.call-start
  7.2 2.3 %shard_map.124 = (f32[3,128,128]{2,1,0:T(8,128)}, f32[128,128]{1,0:T(8,128)}, f32[128,128]{1,0:T(8,128)}, f32[128,128]{1,0:T(8,128)}, f32[128,128]{1,0:T(8,128)}) custom-call(s32[16]{0:T(128)} %lengths_ref.15, f32[1,128]{1,0:T(1,128)} %constant.2.clone.inverse_ref, f32[128,256]{1,0:T(8,128)} %key_ref.5, f32[128,256]{1,0:T(8,128)} %value_ref.5), custom_call_target="tpu_custom_call" | custom-call | flops 1000000 | bytes 800000 | tf_op jit(solution)/shard_map/pallas_call | solution.py:51
  9.5 3.8 %collective-permute-start.7 = (f32[128,128]{1,0:T(8,128)}, f32[128,128]{1,0:T(8,128)S(1)}, u32[]{:S(2)}, u32[]{:S(2)}) collective-permute-start(f32[128,128]{1,0:T(8,128)} %get-tuple-element.35), channel_id=1, source_target_pairs={{0,68},{4,196},{64,0},{68,128},{128,4},{132,132},{192,64},{196,192... | collective-permute-start | bytes 196616 | tf_op jit(solution)/shard_map/ppermute | solution.py:376
  13.2 0.9 collective-permute-start.6
  14.2 4.2 %collective-permute-start.5 = (f32[128,128]{1,0:T(8,128)}, f32[128,128]{1,0:T(8,128)S(1)}, u32[]{:S(2)}, u32[]{:S(2)}) collective-permute-start(f32[128,128]{1,0:T(8,128)} %get-tuple-element.33), channel_id=1, source_target_pairs={{0,4},{4,132},{64,64},{68,192},{128,68},{132,196},{192,0},{196,128... | collective-permute-start | bytes 196616 | tf_op jit(solution)/shard_map/ppermute | solution.py:376
  18.3 1.9 %collective-permute-start.4 = (f32[128,128]{1,0:T(8,128)}, f32[128,128]{1,0:T(8,128)S(1)}, u32[]{:S(2)}, u32[]{:S(2)}) collective-permute-start(f32[128,128]{1,0:T(8,128)} %get-tuple-element.32), channel_id=1, source_target_pairs={{0,0},{4,128},{64,4},{68,132},{128,64},{132,192},{192,68},{196,196... | collective-permute-start | bytes 196616 | tf_op jit(solution)/shard_map/ppermute | solution.py:376
  20.3 0.0 collective-permute-done.7
  20.3 0.0 collective-permute-done.6
  20.3 0.0 collective-permute-done.5
  20.3 5.3 %collective-permute-done.4 = f32[128,128]{1,0:T(8,128)S(1)} collective-permute-done((f32[128,128]{1,0:T(8,128)}, f32[128,128]{1,0:T(8,128)S(1)}, u32[]{:S(2)}, u32[]{:S(2)}) %collective-permute-start.4) | collective-permute-done | bytes 65568 | tf_op jit(solution)/shard_map/ppermute | solution.py:376
  25.6 0.7 pad_maximum_fusion
  26.4 0.0 all-gather.3.cloned.1.call-update
  26.4 4.1 %shard_map.122 = f32[32,72,128]{2,1,0:T(8,128)} custom-call(s32[16]{0:T(128)} %lengths_ref.15, f32[16,128]{1,0:T(8,128)} %rate_ref.5, f32[128,2048]{1,0:T(8,128)} %key_ref.4, f32[128,2048]{1,0:T(8,128)} %value_ref.4), custom_call_target="tpu_custom_call" | custom-call | flops 201326592 | bytes 3300000 | tf_op jit(solution)/shard_map/pallas_call | solution.py:51
  30.5 0.0 copy-start.7
  30.5 0.0 copy-start.9
  30.5 9.7 %all-to-all-start = ((f32[32,72,128]{2,1,0:T(8,128)}), f32[32,72,128]{2,1,0:T(8,128)S(1)}, u32[]{:S(2)}, u32[]{:S(2)}) async-start(f32[32,72,128]{2,1,0:T(8,128)} %shard_map.122), calls=%async_computation | async-start | bytes 2359296 | tf_op jit(solution)/shard_map/all_to_all | solution.py:388
  40.2 0.0 copy-start
  40.2 0.0 copy-done.7
  40.2 0.0 copy-done.9
  40.2 0.0 copy-start.5
  40.2 1.3 copy-done.5
  41.5 1.2 shard_map.125
  42.7 3.1 %collective-permute-start = (f32[128,512]{1,0:T(8,128)S(1)}, f32[128,512]{1,0:T(8,128)S(1)}, u32[]{:S(2)}, u32[]{:S(2)}) collective-permute-start(f32[128,512]{1,0:T(8,128)S(1)} %get-tuple-element.22), channel_id=1, source_target_pairs={{0,0},{4,128},{64,4},{68,132},{128,64},{132,192},{192,68},{196,196... | collective-permute-start | bytes 786440 | tf_op jit(solution)/shard_map/ppermute | solution.py:393
  45.8 4.0 %collective-permute-start.1 = (f32[128,512]{1,0:T(8,128)S(1)}, f32[128,512]{1,0:T(8,128)S(1)}, u32[]{:S(2)}, u32[]{:S(2)}) collective-permute-start(f32[128,512]{1,0:T(8,128)S(1)} %get-tuple-element.23), channel_id=1, source_target_pairs={{0,4},{4,132},{64,64},{68,192},{128,68},{132,196},{192,0},{196,128... | collective-permute-start | bytes 786440 | tf_op jit(solution)/shard_map/ppermute | solution.py:393
  49.8 0.1 collective-permute-start.2
  49.9 3.8 %collective-permute-start.3 = (f32[128,512]{1,0:T(8,128)S(1)}, f32[128,512]{1,0:T(8,128)S(1)}, u32[]{:S(2)}, u32[]{:S(2)}) collective-permute-start(f32[128,512]{1,0:T(8,128)S(1)} %get-tuple-element.25), channel_id=1, source_target_pairs={{0,68},{4,196},{64,0},{68,128},{128,4},{132,132},{192,64},{196,192... | collective-permute-start | bytes 786440 | tf_op jit(solution)/shard_map/ppermute | solution.py:393
  53.7 0.0 copy-done.1
  53.7 0.0 copy-done.2
  53.8 0.0 copy-done
  53.8 0.0 copy-done.8
  53.8 6.7 %shard_map.123.intra_ref = f32[128,2048]{1,0:T(8,128)S(1)} custom-call(s32[16]{0:T(128)S(1)} %copy-done.9, f32[16,128]{1,0:T(8,128)S(1)} %copy-done.8, f32[128,2048]{1,0:T(8,128)S(1)} %copy-done.2, f32[128,2048]{1,0:T(8,128)S(1)} %copy-done, f32[128,2048]{1,0:T(8,128)S(1)} %copy-done.1), custom_call_target="tpu_custom_call" | custom-call | flops 402653184 | bytes 4200000 | tf_op jit(solution)/shard_map/pallas_call | solution.py:51
  60.5 0.0 copy-start.3
  60.5 1.0 copy-done.3
  61.4 0.0 collective-permute-done.refs_0_
  61.4 2.4 %collective-permute-done.1.refs_1_ = f32[128,512]{1,0:T(8,128)S(1)} collective-permute-done((f32[128,512]{1,0:T(8,128)S(1)}, f32[128,512]{1,0:T(8,128)S(1)}, u32[]{:S(2)}, u32[]{:S(2)}) %collective-permute-start.1) | collective-permute-done | bytes 262176 | tf_op jit(solution)/shard_map/ppermute | solution.py:393
  63.8 0.7 copy-done.12
  64.6 0.0 collective-permute-done.2.refs_2_
  64.6 0.7 copy-done.14
  65.3 0.8 collective-permute-done.3.refs_3_
  66.1 0.7 copy-done.16
  66.8 13.2 %all-to-all-done.in_ref = f32[32,72,128]{2,1,0:T(8,128)S(1)} async-done(((f32[32,72,128]{2,1,0:T(8,128)}), f32[32,72,128]{2,1,0:T(8,128)S(1)}, u32[]{:S(2)}, u32[]{:S(2)}) %all-to-all-start) | async-done | bytes 1179680 | tf_op jit(solution)/shard_map/all_to_all | solution.py:388
  80.0 1.6 %shard_map.126 = f32[32,64,128]{2,1,0:T(8,128)} custom-call(s32[16]{0:T(128)S(1)} %copy-done.9, f32[32,72,128]{2,1,0:T(8,128)S(1)} %all-to-all-done.in_ref), custom_call_target="tpu_custom_call" | custom-call | flops 1000000 | bytes 2200000 | tf_op jit(solution)/shard_map/pallas_call | solution.py:51
  81.6 8.8 %all-to-all-start.1 = ((f32[32,64,128]{2,1,0:T(8,128)}), f32[32,64,128]{2,1,0:T(8,128)S(1)}, u32[]{:S(2)}, u32[]{:S(2)}) async-start(f32[32,64,128]{2,1,0:T(8,128)} %shard_map.126), calls=%async_computation.1 | async-start | bytes 2097152 | tf_op jit(solution)/shard_map/all_to_all | solution.py:407
  90.4 1.0 all-gather.3.cloned.1.call-done
  91.4 2.2 %copy-done.11 = f32[64,128,128]{2,1,0:T(8,128)S(1)} copy-done((f32[64,128,128]{2,1,0:T(8,128)S(1)}, f32[64,128,128]{2,1,0:T(8,128)}, u32[]{:S(2)}) %copy-start.11) | copy-done | bytes 4194328
  93.5 0.9 copy-done.13
  94.5 0.9 copy-done.15
  95.4 0.9 copy-done.17
  96.4 19.6 %shard_map.128 = (f32[128,512]{1,0:T(8,128)}, f32[128,512]{1,0:T(8,128)}, f32[128,512]{1,0:T(8,128)}, f32[128,512]{1,0:T(8,128)}) custom-call(s32[16]{0:T(128)S(1)} %copy-done.9, f32[128,512]{1,0:T(8,128)S(1)} %collective-permute-done.refs_0_, f32[128,512]{1,0:T(8,128)S(1)} %copy-done.13, f32[128,512]{1,0:T(8,128)S(1)} %copy-done.15, ...), custom_call_target="tpu_custom_call" | custom-call | flops 5033164800 | bytes 6000000 | tf_op jit(solution)/shard_map/pallas_call | solution.py:51
  116.0 4.7 %collective-permute-start.8 = (f32[128,512]{1,0:T(8,128)}, f32[128,512]{1,0:T(8,128)S(1)}, u32[]{:S(2)}, u32[]{:S(2)}) collective-permute-start(f32[128,512]{1,0:T(8,128)} %get-tuple-element.36), channel_id=1, source_target_pairs={{0,0},{128,4},{4,64},{132,68},{64,128},{192,132},{68,192},{196,196... | collective-permute-start | bytes 786440 | tf_op jit(solution)/shard_map/ppermute | solution.py:427
  120.7 1.9 %collective-permute-start.9 = (f32[128,512]{1,0:T(8,128)}, f32[128,512]{1,0:T(8,128)}, u32[]{:S(2)}, u32[]{:S(2)}) collective-permute-start(f32[128,512]{1,0:T(8,128)} %get-tuple-element.37), channel_id=1, source_target_pairs={{4,0},{132,4},{64,64},{192,68},{68,128},{196,132},{0,192},{128,196... | collective-permute-start | bytes 786440 | tf_op jit(solution)/shard_map/ppermute | solution.py:427
  122.6 1.4 collective-permute-start.10
  124.0 2.0 %collective-permute-start.11 = (f32[128,512]{1,0:T(8,128)}, f32[128,512]{1,0:T(8,128)}, u32[]{:S(2)}, u32[]{:S(2)}) collective-permute-start(f32[128,512]{1,0:T(8,128)} %get-tuple-element.39), channel_id=1, source_target_pairs={{68,0},{196,4},{0,64},{128,68},{4,128},{132,132},{64,192},{192,196... | collective-permute-start | bytes 786440 | tf_op jit(solution)/shard_map/ppermute | solution.py:427
  126.0 0.0 all-to-all-done.1
  126.0 0.0 copy-done.4
  126.0 0.0 copy-done.10
  126.1 0.0 copy-start.6
  126.1 1.2 copy-done.6
  127.3 3.3 %shard_map.127 = f32[128,2048]{1,0:T(8,128)} custom-call(s32[16]{0:T(128)S(1)} %copy-done.9, f32[16,128]{1,0:T(8,128)S(1)} %copy-done.8, f32[128,2048]{1,0:T(8,128)S(1)} %copy-done.2, f32[16,128,128]{2,1,0:T(8,128)S(1)} %bitcast.7, f32[128,2048]{1,0:T(8,128)S(1)} %copy-done.4, f32[128,2048]{1,0:T(8,128)S(1)} %copy-done.6, f32[1,2048]{1,0:T(1,128)S(1)} %bitcast.8), custom_call_target="tpu_custom_call" | custom-call | flops 201326592 | bytes 5200000 | tf_op jit(solution)/shard_map/pallas_call | solution.py:51
  130.5 0.0 collective-permute-done.8.refs_0_
  130.5 2.6 %collective-permute-done.9.refs_1_ = f32[128,512]{1,0:T(8,128)} collective-permute-done((f32[128,512]{1,0:T(8,128)}, f32[128,512]{1,0:T(8,128)}, u32[]{:S(2)}, u32[]{:S(2)}) %collective-permute-start.9) | collective-permute-done | bytes 262176 | tf_op jit(solution)/shard_map/ppermute | solution.py:427
  133.1 0.4 collective-permute-done.10.refs_2_
  133.5 2.7 %collective-permute-done.11.refs_3_ = f32[128,512]{1,0:T(8,128)} collective-permute-done((f32[128,512]{1,0:T(8,128)}, f32[128,512]{1,0:T(8,128)}, u32[]{:S(2)}, u32[]{:S(2)}) %collective-permute-start.11) | collective-permute-done | bytes 262176 | tf_op jit(solution)/shard_map/ppermute | solution.py:427
  136.2 2.2 %shard_map.129 = f32[128,2048]{1,0:T(8,128)} custom-call(s32[16]{0:T(128)S(1)} %copy-done.9, f32[128,512]{1,0:T(8,128)S(1)} %collective-permute-done.8.refs_0_, f32[128,512]{1,0:T(8,128)} %collective-permute-done.9.refs_1_, f32[128,512]{1,0:T(8,128)} %collective-permute-done.10.refs_2_, f32[128,512]{1,0:T(8,128)} %collective-permute-done.11.refs_3_), custom_call_target="tpu_custom_call" | custom-call | flops 1000000 | bytes 2000000 | tf_op jit(solution)/shard_map/pallas_call | solution.py:51
  (12 shorter events, 0.0 us)
Async XLA Ops:
  7.2 84.2 %all-gather.3.cloned.1.call-start = ((), (), s32[]{:S(2)}) async-start(), calls=%async_computation.2 | async-start | bytes 4456448 | tf_op jit(solution)/shard_map/all_gather | solution.py:377
  9.5 10.8 %collective-permute-start.7 = (f32[128,128]{1,0:T(8,128)}, f32[128,128]{1,0:T(8,128)S(1)}, u32[]{:S(2)}, u32[]{:S(2)}) collective-permute-start(f32[128,128]{1,0:T(8,128)} %get-tuple-element.35), channel_id=1, source_target_pairs={{0,68},{4,196},{64,0},{68,128},{128,4},{132,132},{192,64},{196,192... | collective-permute-start | bytes 196616 | tf_op jit(solution)/shard_map/ppermute | solution.py:376
  13.2 7.0 %collective-permute-start.6 = (f32[128,128]{1,0:T(8,128)}, f32[128,128]{1,0:T(8,128)S(1)}, u32[]{:S(2)}, u32[]{:S(2)}) collective-permute-start(f32[128,128]{1,0:T(8,128)} %get-tuple-element.34), channel_id=1, source_target_pairs={{0,64},{4,192},{64,68},{68,196},{128,0},{132,128},{192,4},{196,132... | collective-permute-start | bytes 196616 | tf_op jit(solution)/shard_map/ppermute | solution.py:376
  14.2 6.1 %collective-permute-start.5 = (f32[128,128]{1,0:T(8,128)}, f32[128,128]{1,0:T(8,128)S(1)}, u32[]{:S(2)}, u32[]{:S(2)}) collective-permute-start(f32[128,128]{1,0:T(8,128)} %get-tuple-element.33), channel_id=1, source_target_pairs={{0,4},{4,132},{64,64},{68,192},{128,68},{132,196},{192,0},{196,128... | collective-permute-start | bytes 196616 | tf_op jit(solution)/shard_map/ppermute | solution.py:376
  18.3 7.3 %collective-permute-start.4 = (f32[128,128]{1,0:T(8,128)}, f32[128,128]{1,0:T(8,128)S(1)}, u32[]{:S(2)}, u32[]{:S(2)}) collective-permute-start(f32[128,128]{1,0:T(8,128)} %get-tuple-element.32), channel_id=1, source_target_pairs={{0,0},{4,128},{64,4},{68,132},{128,64},{132,192},{192,68},{196,196... | collective-permute-start | bytes 196616 | tf_op jit(solution)/shard_map/ppermute | solution.py:376
  30.5 9.7 %copy-start.7 = (f32[3,128,128]{2,1,0:T(8,128)S(1)}, f32[3,128,128]{2,1,0:T(8,128)}, u32[]{:S(2)}) copy-start(f32[3,128,128]{2,1,0:T(8,128)} %get-tuple-element.21.tables_ref) | copy-start | bytes 589828
  30.5 9.7 %copy-start.9 = (s32[16]{0:T(128)S(1)}, s32[16]{0:T(128)}, u32[]{:S(2)}) copy-start(s32[16]{0:T(128)} %lengths_ref.15) | copy-start | bytes 196
  30.5 23.2 %copy-start.1 = (f32[128,2048]{1,0:T(8,128)S(1)}, f32[128,2048]{1,0:T(8,128)}, u32[]{:S(2)}) copy-start(f32[128,2048]{1,0:T(8,128)} %value_ref.4) | copy-start | bytes 3145732
  30.5 23.2 %copy-start.2 = (f32[128,2048]{1,0:T(8,128)S(1)}, f32[128,2048]{1,0:T(8,128)}, u32[]{:S(2)}) copy-start(f32[128,2048]{1,0:T(8,128)} %query_ref.5) | copy-start | bytes 3145732
  30.5 49.5 %all-to-all-start = ((f32[32,72,128]{2,1,0:T(8,128)}), f32[32,72,128]{2,1,0:T(8,128)S(1)}, u32[]{:S(2)}, u32[]{:S(2)}) async-start(f32[32,72,128]{2,1,0:T(8,128)} %shard_map.122), calls=%async_computation | async-start | bytes 2359296 | tf_op jit(solution)/shard_map/all_to_all | solution.py:388
  40.2 13.6 %copy-start = (f32[128,2048]{1,0:T(8,128)S(1)}, f32[128,2048]{1,0:T(8,128)}, u32[]{:S(2)}) copy-start(f32[128,2048]{1,0:T(8,128)} %key_ref.4) | copy-start | bytes 3145732
  40.2 1.3 copy-start.5
  41.5 12.2 %copy-start.8 = (f32[16,128]{1,0:T(8,128)S(1)}, f32[16,128]{1,0:T(8,128)}, u32[]{:S(2)}) copy-start(f32[16,128]{1,0:T(8,128)} %rate_ref.5) | copy-start | bytes 24580
  42.7 18.7 %collective-permute-start = (f32[128,512]{1,0:T(8,128)S(1)}, f32[128,512]{1,0:T(8,128)S(1)}, u32[]{:S(2)}, u32[]{:S(2)}) collective-permute-start(f32[128,512]{1,0:T(8,128)S(1)} %get-tuple-element.22), channel_id=1, source_target_pairs={{0,0},{4,128},{64,4},{68,132},{128,64},{132,192},{192,68},{196,196... | collective-permute-start | bytes 786440 | tf_op jit(solution)/shard_map/ppermute | solution.py:393
  45.8 18.0 %collective-permute-start.1 = (f32[128,512]{1,0:T(8,128)S(1)}, f32[128,512]{1,0:T(8,128)S(1)}, u32[]{:S(2)}, u32[]{:S(2)}) collective-permute-start(f32[128,512]{1,0:T(8,128)S(1)} %get-tuple-element.23), channel_id=1, source_target_pairs={{0,4},{4,132},{64,64},{68,192},{128,68},{132,196},{192,0},{196,128... | collective-permute-start | bytes 786440 | tf_op jit(solution)/shard_map/ppermute | solution.py:393
  49.8 14.7 %collective-permute-start.2 = (f32[128,512]{1,0:T(8,128)S(1)}, f32[128,512]{1,0:T(8,128)S(1)}, u32[]{:S(2)}, u32[]{:S(2)}) collective-permute-start(f32[128,512]{1,0:T(8,128)S(1)} %get-tuple-element.24), channel_id=1, source_target_pairs={{0,64},{4,192},{64,68},{68,196},{128,0},{132,128},{192,4},{196,132... | collective-permute-start | bytes 786440 | tf_op jit(solution)/shard_map/ppermute | solution.py:393
  49.9 16.2 %collective-permute-start.3 = (f32[128,512]{1,0:T(8,128)S(1)}, f32[128,512]{1,0:T(8,128)S(1)}, u32[]{:S(2)}, u32[]{:S(2)}) collective-permute-start(f32[128,512]{1,0:T(8,128)S(1)} %get-tuple-element.25), channel_id=1, source_target_pairs={{0,68},{4,196},{64,0},{68,128},{128,4},{132,132},{192,64},{196,192... | collective-permute-start | bytes 786440 | tf_op jit(solution)/shard_map/ppermute | solution.py:393
  60.5 1.0 copy-start.3
  63.8 0.7 copy-start.12
  64.6 0.7 copy-start.14
  66.1 0.7 copy-start.16
  81.6 44.4 %all-to-all-start.1 = ((f32[32,64,128]{2,1,0:T(8,128)}), f32[32,64,128]{2,1,0:T(8,128)S(1)}, u32[]{:S(2)}, u32[]{:S(2)}) async-start(f32[32,64,128]{2,1,0:T(8,128)} %shard_map.126), calls=%async_computation.1 | async-start | bytes 2097152 | tf_op jit(solution)/shard_map/all_to_all | solution.py:407
  91.4 2.2 %copy-start.11 = (f32[64,128,128]{2,1,0:T(8,128)S(1)}, f32[64,128,128]{2,1,0:T(8,128)}, u32[]{:S(2)}) copy-start(f32[64,128,128]{2,1,0:T(8,128)} %all-gather.3.cloned.1.call-done) | copy-start | bytes 12582916
  93.5 0.9 copy-start.13
  94.5 0.9 copy-start.15
  95.4 0.9 copy-start.17
  96.4 29.6 %copy-start.4 = (f32[128,2048]{1,0:T(8,128)S(1)}, f32[128,2048]{1,0:T(8,128)}, u32[]{:S(2)}) copy-start(f32[128,2048]{1,0:T(8,128)} %copy-done.3) | copy-start | bytes 3145732
  96.4 29.6 %copy-start.10 = (f32[2048]{0:T(1024)S(1)}, f32[2048]{0:T(1024)}, u32[]{:S(2)}) copy-start(f32[2048]{0:T(1024)} %param.16) | copy-start | bytes 24580
  116.0 14.6 %collective-permute-start.8 = (f32[128,512]{1,0:T(8,128)}, f32[128,512]{1,0:T(8,128)S(1)}, u32[]{:S(2)}, u32[]{:S(2)}) collective-permute-start(f32[128,512]{1,0:T(8,128)} %get-tuple-element.36), channel_id=1, source_target_pairs={{0,0},{128,4},{4,64},{132,68},{64,128},{192,132},{68,192},{196,196... | collective-permute-start | bytes 786440 | tf_op jit(solution)/shard_map/ppermute | solution.py:427
  120.7 12.5 %collective-permute-start.9 = (f32[128,512]{1,0:T(8,128)}, f32[128,512]{1,0:T(8,128)}, u32[]{:S(2)}, u32[]{:S(2)}) collective-permute-start(f32[128,512]{1,0:T(8,128)} %get-tuple-element.37), channel_id=1, source_target_pairs={{4,0},{132,4},{64,64},{192,68},{68,128},{196,132},{0,192},{128,196... | collective-permute-start | bytes 786440 | tf_op jit(solution)/shard_map/ppermute | solution.py:427
  122.6 11.0 %collective-permute-start.10 = (f32[128,512]{1,0:T(8,128)}, f32[128,512]{1,0:T(8,128)}, u32[]{:S(2)}, u32[]{:S(2)}) collective-permute-start(f32[128,512]{1,0:T(8,128)} %get-tuple-element.38), channel_id=1, source_target_pairs={{64,0},{192,4},{68,64},{196,68},{0,128},{128,132},{4,192},{132,196... | collective-permute-start | bytes 786440 | tf_op jit(solution)/shard_map/ppermute | solution.py:427
  124.0 12.2 %collective-permute-start.11 = (f32[128,512]{1,0:T(8,128)}, f32[128,512]{1,0:T(8,128)}, u32[]{:S(2)}, u32[]{:S(2)}) collective-permute-start(f32[128,512]{1,0:T(8,128)} %get-tuple-element.39), channel_id=1, source_target_pairs={{68,0},{196,4},{0,64},{128,68},{4,128},{132,132},{64,192},{192,196... | collective-permute-start | bytes 786440 | tf_op jit(solution)/shard_map/ppermute | solution.py:427
  126.1 1.2 copy-start.6
Sparse Core Ops, SparseCore 0:
  26.5 64.7 all-gather.2

commit v2 on v1

--- a/solution.py
+++ b/solution.py
@@ -14,7 +14,9 @@
 TOK = 128
 DOCS = 16
 CHUNK = 512
+PIECES = (0, 1, -1, 2, -2, 3, -3, 4)
 NEG = -1e30
+QUERIES = 4 * HEAD_DIM
 ROPE_BASE = 10000000.0
 NORM_EPS = 1e-05
 F32 = jnp.float32
@@ -24,10 +26,11 @@
     ROPE_BASE, -(2.0 * np.arange(ROT_DIM // 2, dtype=np.float64)) / ROT_DIM
 ).astype(np.float32)
 
+VMEM = pl.BlockSpec(memory_space=pltpu.VMEM)
 SMEM = pl.BlockSpec(memory_space=pltpu.SMEM)
 
 
-def built(kernel, out_shape, shapes, scratch=(), flops=1_000_000, moved=1_000_000, limit=20):
+def built(kernel, out_shape, shapes, scratch=(), flops=1000, moved=1000, limit=20):
     def whole(shape):
         return pl.BlockSpec(shape, lambda i: (0,) * len(shape))
 
@@ -142,92 +145,133 @@
             pieces[r][:, n * HEAD_DIM : (n + 1) * HEAD_DIM] = rotated(x, tables) * scale
 
 
+def pack(mine, theirs, kcat, vcat):
+    z, zs = lax.axis_index("z"), lax.axis_size("z")
+    core = lax.axis_index("head")
+    e_key = 2 * (lax.axis_index("y") % 2)
+
+    def keep(x, at, keys):
+        high, low = halves(x)
+        if keys:
+            kcat[pl.ds(at, TOK), 0:128] = high
+            kcat[pl.ds(at, TOK), 128:256] = high
+            kcat[pl.ds(at, TOK), 256:384] = low
+        else:
+            vcat[pl.ds(at, TOK), 0:128] = high
+            vcat[pl.ds(at, TOK), 128:256] = low
+
+    def fill(i, own, keys):
+        source = (z - PIECES[i] + zs) % zs
+
+        @pl.loop(0, 4)
+        def _(r):
+            row = (e_key + (0 if keys else 1) - r + 4) % 4
+            at = pl.multiple_of((row * zs + source) * TOK, TOK)
+            if own:
+                x = mine[i][r]
+            elif i < 7:
+                x = theirs[0][i, r]
+            else:
+                x = theirs[1][r]
+            keep(x, at, keys)
+
+    @pl.when(core == 0)
+    def _():
+        for i in range(8):
+            fill(i, True, True)
+            fill(i, False, False)
+
+    @pl.when(core == 1)
+    def _():
+        for i in range(8):
+            fill(i, True, False)
+            fill(i, False, True)
+
+
+def in_pairs(low, high, step):
+    pairs = (high - low) // 2
+
+    @pl.loop(0, pairs)
+    def _(i):
+        step(low + 2 * i)
+        step(low + 2 * i + 1)
+
+    pl.when((high - low) % 2 == 1)(lambda: step(high - 1))
+
+
 def softmax_kernel(lengths_ref, *refs):
-    queries, kv_ref, outs = refs[:4], refs[4], refs[5:9]
-    kcat, vcat, qcat, s_ref, m_ref, l_ref, acc_ref = refs[9:]
-    z = lax.axis_index("z")
-    zs = kv_ref.shape[0]
-    e_key = 2 * (lax.axis_index("y") % 2)
-    e = e_key + lax.axis_index("head")
-    last = 3 * zs + z
-
-    @pl.loop(0, last + 1)
-    def _(b):
-        at = pl.multiple_of(b * TOK, TOK)
-        kh, kl = halves(kv_ref[b % zs, 0, (e_key - b // zs + 4) % 4])
-        vh, vl = halves(kv_ref[b % zs, 1, (e_key + 1 - b // zs + 4) % 4])
-        kcat[pl.ds(at, TOK), 0:128] = kh
-        kcat[pl.ds(at, TOK), 128:256] = kh
-        kcat[pl.ds(at, TOK), 256:384] = kl
-        vcat[pl.ds(at, TOK), 0:128] = vh
-        vcat[pl.ds(at, TOK), 128:256] = vl
-
-    @pl.loop(last + 1, 4 * zs)
-    def _(b):
-        at = pl.multiple_of(b * TOK, TOK)
-        kcat[pl.ds(at, TOK), :] = jnp.zeros((TOK, 384), BF16)
-        vcat[pl.ds(at, TOK), :] = jnp.zeros((TOK, 256), BF16)
-
+    queries, mine, theirs, outs = refs[:4], refs[4:12], refs[12:14], refs[14:18]
+    kcat, vcat = refs[18:20]
+    pack(mine, theirs, kcat, vcat)
     for r in range(4):
-        block = ((e - r + 4) % 4) * zs + z
-        first = block * TOK
-        rows = first + lax.broadcasted_iota(jnp.int32, (TOK, CHUNK), 0)
-        begin = begins_of(lengths_ref, rows)
-        for n in range(4):
-            qh, ql = halves(queries[r][:, n * HEAD_DIM : (n + 1) * HEAD_DIM])
-            qcat[n * TOK : (n + 1) * TOK, 0:128] = qh
-            qcat[n * TOK : (n + 1) * TOK, 128:256] = ql
-            qcat[n * TOK : (n + 1) * TOK, 256:384] = qh
-        low = begin_scalar(lengths_ref, first) // CHUNK
-        high = first // CHUNK + 1
-        inner = (begin_scalar(lengths_ref, first + TOK - 1) + CHUNK - 1) // CHUNK
-        inner = jnp.minimum(inner, high)
-        outer = jnp.maximum(inner, high - 1)
-        m_ref[...] = jnp.full_like(m_ref, NEG)
-        l_ref[...] = jnp.zeros_like(l_ref)
-        acc_ref[...] = jnp.zeros_like(acc_ref)
-
-        def score(j, masked):
-            at = pl.multiple_of(j * CHUNK, CHUNK)
-            s = dot(qcat[...], kcat[pl.ds(at, CHUNK), :], 1, 1)
-            if masked:
-                keys = at + lax.broadcasted_iota(jnp.int32, (TOK, CHUNK), 1)
-                visible = (keys >= begin) & (keys <= rows)
-                s = jnp.where(visible[None], s.reshape(4, TOK, CHUNK), NEG)
-                s = s.reshape(4 * TOK, CHUNK)
-            s_ref[j] = s
-            top = s[:, :HEAD_DIM]
-            for i in range(1, CHUNK // HEAD_DIM):
-                top = jnp.maximum(top, s[:, i * HEAD_DIM : (i + 1) * HEAD_DIM])
-            m_ref[...] = jnp.maximum(m_ref[...], top)
-
-        pl.loop(low, inner)(lambda j: score(j, True))
-        pl.loop(inner, outer)(lambda j: score(j, False))
-        pl.loop(outer, high)(lambda j: score(j, True))
-
-        top = jnp.max(m_ref[...], axis=1, keepdims=True)
-        m_ref[...] = jnp.broadcast_to(top, m_ref.shape)
-
-        @pl.loop(low, high)
-        def _(j):
-            at = pl.multiple_of(j * CHUNK, CHUNK)
-            top = m_ref[...]
-            highs, lows, total = [], [], l_ref[...]
-            for i in range(CHUNK // HEAD_DIM):
-                p = jnp.exp2(s_ref[j, :, i * HEAD_DIM : (i + 1) * HEAD_DIM] - top)
-                total = total + p
-                ph, pl_ = halves(p)
-                highs.append(ph)
-                lows.append(pl_)
-            l_ref[...] = total
-            v = vcat[pl.ds(at, CHUNK), :]
-            p = jnp.concatenate(highs + lows, axis=1)
-            acc_ref[...] += dot(p, jnp.concatenate([v, v], axis=0), 1, 0)
-
-        total = jnp.sum(l_ref[...], axis=1, keepdims=True)
-        mixed = (acc_ref[:, :HEAD_DIM] + acc_ref[:, HEAD_DIM:]) / total
-        for n in range(4):
-            outs[r][:, n * HEAD_DIM : (n + 1) * HEAD_DIM] = mixed[n * TOK : (n + 1) * TOK]
+        attend(r, lengths_ref, queries[r], kcat, vcat, outs[r], *refs[20:])
+
+
+def attend(r, lengths_ref, query_ref, kcat, vcat, out_ref, *scratch):
+    qcat, s_ref, m_ref, l_ref, acc_ref = scratch
+    e = 2 * (lax.axis_index("y") % 2) + lax.axis_index("head")
+    block = ((e - r + 4) % 4) * lax.axis_size("z") + lax.axis_index("z")
+    first = block * TOK
+    for n in range(4):
+        qh, ql = halves(query_ref[:, n * HEAD_DIM : (n + 1) * HEAD_DIM])
+        qcat[n * TOK : (n + 1) * TOK, 0:128] = qh
+        qcat[n * TOK : (n + 1) * TOK, 128:256] = ql
+        qcat[n * TOK : (n + 1) * TOK, 256:384] = qh
+    low = begin_scalar(lengths_ref, first) // CHUNK
+    high = first // CHUNK + 1
+    inner = (begin_scalar(lengths_ref, first + TOK - 1) + CHUNK - 1) // CHUNK
+    inner = jnp.minimum(inner, high)
+    outer = jnp.maximum(inner, high - 1)
+    m_ref[...] = jnp.full_like(m_ref, NEG)
+    l_ref[...] = jnp.zeros_like(l_ref)
+    acc_ref[...] = jnp.zeros_like(acc_ref)
+
+    def score(j, masked):
+        at = pl.multiple_of(j * CHUNK, CHUNK)
+        s = dot(qcat[...], kcat[pl.ds(at, CHUNK), :], 1, 1)
+        if masked:
+            rows = first + lax.broadcasted_iota(jnp.int32, (TOK, CHUNK), 0)
+            keys = at + lax.broadcasted_iota(jnp.int32, (TOK, CHUNK), 1)
+            begin = begins_of(
+                lengths_ref, first + lax.broadcasted_iota(jnp.int32, (TOK, 1), 0)
+            )
+            visible = (keys >= begin) & (keys <= rows)
+            s = jnp.where(visible[None], s.reshape(4, TOK, CHUNK), NEG)
+            s = s.reshape(4 * TOK, CHUNK)
+        s_ref[j] = s
+        top = s[:, :HEAD_DIM]
+        for i in range(1, CHUNK // HEAD_DIM):
+            top = jnp.maximum(top, s[:, i * HEAD_DIM : (i + 1) * HEAD_DIM])
+        m_ref[...] = jnp.maximum(m_ref[...], top)
+
+    pl.loop(low, inner)(lambda j: score(j, True))
+    in_pairs(inner, outer, lambda j: score(j, False))
+    pl.loop(outer, high)(lambda j: score(j, True))
+
+    top = jnp.max(m_ref[...], axis=1, keepdims=True)
+    m_ref[...] = jnp.broadcast_to(top, m_ref.shape)
+
+    def mix(j):
+        at = pl.multiple_of(j * CHUNK, CHUNK)
+        top = m_ref[...]
+        highs, lows, total = [], [], l_ref[...]
+        for i in range(CHUNK // HEAD_DIM):
+            p = jnp.exp2(s_ref[j, :, i * HEAD_DIM : (i + 1) * HEAD_DIM] - top)
+            total = total + p
+            ph, pl_ = halves(p)
+            highs.append(ph)
+            lows.append(pl_)
+        l_ref[...] = total
+        v = vcat[pl.ds(at, CHUNK), :]
+        p = jnp.concatenate(highs + lows, axis=1)
+        acc_ref[...] += dot(p, jnp.concatenate([v, v], axis=0), 1, 0)
+
+    in_pairs(low, high, mix)
+
+    total = jnp.sum(l_ref[...], axis=1, keepdims=True)
+    mixed = (acc_ref[:, :HEAD_DIM] + acc_ref[:, HEAD_DIM:]) / total
+    for n in range(4):
+        out_ref[:, n * HEAD_DIM : (n + 1) * HEAD_DIM] = mixed[n * TOK : (n + 1) * TOK]
 
 
 def place_kernel(lengths_ref, *refs):
@@ -284,7 +328,14 @@
     for h in range(heads):
         lanes = slice(h * HEAD_DIM, (h + 1) * HEAD_DIM)
         k = key_ref[:, lanes] * weight[:, h : h + 1]
-        inner = dot3(k, value_ref[:, lanes], 0, 0)
+        kh, kl = halves(k)
+        vh, vl = halves(value_ref[:, lanes])
+        inner = dot(
+            jnp.concatenate([kh, kh, kl], axis=0),
+            jnp.concatenate([vh, vl, vh], axis=0),
+            0,
+            0,
+        )
         kept = jnp.broadcast_to(carried[:, h : h + 1], (8, HEAD_DIM))
         for i in range(2):
             out_ref[2 * h + i, :half] = inner[i * half : (i + 1) * half]
@@ -364,78 +415,95 @@
         forth.append(pairs)
         back.append([(b, a) for a, b in pairs])
 
+    sliced = call(
+        state_kernel, out((blocks, HEAD_DIM // 2 + 8, HEAD_DIM), F32), 4, limit=60
+    )(doc_lengths, decay_rate, lin_key, lin_value)
+    arrived = lax.all_to_all(sliced, ("y", "z"), 0, 0, tiled=True)
+
     inverse = np.zeros((1, HEAD_DIM), np.float32)
     inverse[0, :ROT_DIM] = np.tile(INVERSE, 2)
+    sm_key, sliced = lax.optimization_barrier((sm_key, sliced))
     tables, *kv_pieces = call(
         kv_kernel,
         [out((3, rows, HEAD_DIM), F32)] + [out((rows, HEAD_DIM), F32)] * 4,
         4,
-        moved=800_000,
         limit=60,
     )(doc_lengths, jnp.asarray(inverse), sm_key, sm_value)
     kv_here = [lax.ppermute(p, group, forth[r]) for r, p in enumerate(kv_pieces)]
-    kv = lax.all_gather(jnp.stack(kv_here), ("z", "head"), axis=0, tiled=False)
-    kv = kv.reshape(zs, 2, ys, rows, HEAD_DIM)
-
-    sliced = call(
-        state_kernel,
-        out((blocks, HEAD_DIM // 2 + 8, HEAD_DIM), F32),
-        4,
-        flops=6 * heads * HEAD_DIM**3,
-        moved=3_300_000,
-        limit=60,
-    )(doc_lengths, decay_rate, lin_key, lin_value)
-    arrived = lax.all_to_all(sliced, ("y", "z"), 0, 0, tiled=True)
-
-    q_pieces = call(
-        query_kernel, [out((rows, 4 * HEAD_DIM), F32)] * 4, 3, moved=2_200_000
-    )(doc_lengths, tables, sm_query)
-    queries = [lax.ppermute(p, group, forth[r]) for r, p in enumerate(q_pieces)]
-
-    intra = call(
-        intra_kernel,
-        out((rows, width), F32),
-        5,
-        flops=12 * heads * HEAD_DIM**3,
-        moved=4_200_000,
-    )(doc_lengths, decay_rate, lin_query, lin_key, lin_value)
-
-    arrived, intra, *queries = lax.optimization_barrier((arrived, intra, *queries))
-    prefixes = call(
-        prefix_kernel, out((blocks, HEAD_DIM // 2, HEAD_DIM), F32), 2, moved=2_200_000
-    )(doc_lengths, arrived)
+
+    up = [(i, (i + 1) % zs) for i in range(zs)]
+    down = [(b, a) for a, b in up]
+    own = jnp.stack(kv_here)
+    up1 = lax.ppermute(own, "z", up)
+    down1 = lax.ppermute(own, "z", down)
+
+    sm_query, own = lax.optimization_barrier((sm_query, own))
+    q_pieces = call(query_kernel, [out((rows, QUERIES), F32)] * 4, 3, limit=60)(
+        doc_lengths, tables, sm_query
+    )
+    up1, down1, arrived, *second = lax.optimization_barrier(
+        (up1, down1, arrived, *q_pieces[2:])
+    )
+    q_pieces = [*q_pieces[:2], *second]
+    here = [lax.ppermute(p, group, forth[r]) for r, p in enumerate(q_pieces)]
+    up2 = lax.ppermute(up1, "z", up)
+    down2 = lax.ppermute(down1, "z", down)
+    prefixes = call(prefix_kernel, out((blocks, HEAD_DIM // 2, HEAD_DIM), F32), 2)(
+        doc_lengths, arrived
+    )
+    up2, down2, prefixes, lin_query, *here = lax.optimization_barrier(
+        (up2, down2, prefixes, lin_query, *here)
+    )
+    intra = call(intra_kernel, out((rows, width), F32), 5)(
+        doc_lengths, decay_rate, lin_query, lin_key, lin_value
+    )
+    up3 = lax.ppermute(up2, "z", up)
+    down3 = lax.ppermute(down2, "z", down)
+    up3, down3, prefixes, intra = lax.optimization_barrier((up3, down3, prefixes, intra))
+    up4 = lax.ppermute(up3, "z", up)
+    cross = [
+        (2 * i + c, 2 * ((i - 1) % zs) + 1 - c) for i in range(zs) for c in range(2)
+    ]
+    theirs4 = lax.ppermute(down3, ("z", "head"), cross)
+    near = [own, up1, down1, up2, down2, up3, down3]
+    theirs = lax.ppermute(jnp.stack(near), "head", [(0, 1), (1, 0)])
+
     state = lax.all_to_all(prefixes, ("y", "z"), 0, 0, tiled=True)
     state = state.reshape(heads, HEAD_DIM, HEAD_DIM)
 
+    keys = blocks * TOK
     mixed = call(
         softmax_kernel,
         [out((rows, 4 * HEAD_DIM), F32)] * 4,
-        6,
+        15,
         scratch=[
-            pltpu.VMEM((blocks * TOK, 384), BF16),
-            pltpu.VMEM((blocks * TOK, 256), BF16),
+            pltpu.VMEM((keys, 384), BF16),
+            pltpu.VMEM((keys, 256), BF16),
             pltpu.VMEM((4 * TOK, 384), BF16),
-            pltpu.VMEM((blocks * TOK // CHUNK, 4 * TOK, CHUNK), F32),
+            pltpu.VMEM((keys // CHUNK, 4 * TOK, CHUNK), F32),
             pltpu.VMEM((4 * TOK, HEAD_DIM), F32),
             pltpu.VMEM((4 * TOK, HEAD_DIM), F32),
             pltpu.VMEM((4 * TOK, 2 * HEAD_DIM), F32),
         ],
-        limit=32,
-        flops=6 * 50 * 4 * 2 * 128**3,
-        moved=6_000_000,
-    )(doc_lengths, *queries, kv)
+        limit=60,
+        flops=400_000_000_000,
+        moved=8_000_000,
+    )(
+        doc_lengths, *here, *near, up4, theirs, theirs4
+    )
     returned = [lax.ppermute(p, group, back[r]) for r, p in enumerate(mixed)]
 
-    lin_out = call(
-        finish_kernel,
-        out((rows, width), F32),
-        7,
-        flops=6 * heads * HEAD_DIM**3,
-        moved=5_200_000,
-    )(doc_lengths, decay_rate, lin_query, state, intra, lin_gate, norm_gain.reshape(1, width))
-    sm_out = call(place_kernel, out((rows, width), F32), 5, moved=2_000_000)(
-        doc_lengths, *returned
-    )
+    lin_out = call(finish_kernel, out((rows, width), F32), 7, limit=60)(
+        doc_lengths,
+        decay_rate,
+        lin_query,
+        state,
+        intra,
+        lin_gate,
+        norm_gain.reshape(1, width),
+    )
+    lin_out, *returned = lax.optimization_barrier((lin_out, *returned))
+    sm_out = call(place_kernel, out((rows, width), F32), 5)(doc_lengths, *returned)
     return (lin_out, sm_out)
 
 

time: 146 us -> 133 us (0.911)
  starting transfers between devices: 50.2 us -> 65.5 us
  waiting for transfers between devices: 28.5 us -> 13.4 us
  between operations: 14.3 us -> 1.04 us
  Pallas kernels: 40.9 us -> 44.6 us
  local copies, waits for them, and re-layouts: 10.7 us -> 8.32 us
    ppermute x4 -> x13, starting transfers between devices: 11 us -> 25.9 us  [the longest x4 12.4 us: shards(): here = [lax.ppermute(p, group, forth[r]) for r, p in enumerate(q_pieces)]]
    all_to_all x1, waiting for transfers between devices: 13.2 us -> 0.01 us  [shards(): arrived = lax.all_to_all(sliced, ('y', 'z'), 0, 0, tiled=True)]
    pallas_call x8, Pallas kernels: 40.9 us -> 44.6 us  [run(): built(kernel, out_shape, [a.shape for a in arrays], **options)]
    unnamed x36 -> x48, local copies, waits for them, and re-layouts: 10.7 us -> 7.59 us
    all_to_all x1, starting transfers between devices: 9.67 us -> 11.1 us  [shards(): arrived = lax.all_to_all(sliced, ('y', 'z'), 0, 0, tiled=True)]
    ppermute x4 -> x13, waiting for transfers between devices: 3.24 us -> 3.42 us  [the longest x4 2.34 us: shards(): here = [lax.ppermute(p, group, forth[r]) for r, p in enumerate(q_pieces)]]
  transfers between devices with their start and end apart: 15 -> 23, of which waited for: 8 -> 7; matrix products, arithmetic and copies ran while one was open for 0% -> 3% of each run, Pallas kernels for 25% -> 29%
where the time goes in v2:
time: 133 us
  starting transfers between devices  65.5 us (49%)
  Pallas kernels  44.6 us (34%)
  waiting for transfers between devices  13.4 us (10%)
  local copies, waits for them, and re-layouts  8.32 us (6%)
    pallas_call x8, Pallas kernels, run(): built(kernel, out_shape, [a.shape for a in arrays], **options)  44.6 us
    ppermute x4, starting transfers between devices, shards(): here = [lax.ppermute(p, group, forth[r]) for r, p in enumerate(q_pieces)]  12.4 us
    all_to_all x1, starting transfers between devices, shards(): arrived = lax.all_to_all(sliced, ('y', 'z'), 0, 0, tiled=True)  11.1 us
    ppermute x4, starting transfers between devices, shards(): lax.ppermute(p, group, forth[r])  10.6 us
    ppermute x4, starting transfers between devices, shards(): returned = [lax.ppermute(p, group, back[r]) for r, p in enumerate(mixed)]  9.92 us
    all_to_all x1, starting transfers between devices, shards(): state = lax.all_to_all(prefixes, ('y', 'z'), 0, 0, tiled=True)  7.95 us
    unnamed x48, local copies, waits for them, and re-layouts  7.59 us
    ppermute x4, waiting for transfers between devices, shards(): lax.ppermute(p, group, forth[r])  5.58 us
  transfers between devices with their start and end apart: 23, of which 7 were waited for; matrix products, arithmetic and copies ran while one was open for 3% of the time, Pallas kernels for 29%

profile of v2, /device:TPU:13, one launch (start us, length us, event | category | flops | bytes accessed | tf_op | source)
XLA Modules:
  0.0 132.8 jit_solution(16003648613158269245)
XLA Ops:
  0.6 4.2 %shard_map.122 = f32[32,72,128]{2,1,0:T(8,128)} custom-call(s32[16]{0:T(128)} %lengths_ref.15, f32[16,128]{1,0:T(8,128)} %rate_ref.5, f32[128,2048]{1,0:T(8,128)} %key_ref.4, f32[128,2048]{1,0:T(8,128)} %value_ref.5), custom_call_target="tpu_custom_call" | custom-call | flops 1000 | bytes 1000 | tf_op jit(solution)/shard_map/pallas_call | solution.py:54
  4.9 11.1 %all-to-all-start = ((f32[32,72,128]{2,1,0:T(8,128)}), f32[32,72,128]{2,1,0:T(8,128)S(1)}, u32[]{:S(2)}, u32[]{:S(2)}) async-start(f32[32,72,128]{2,1,0:T(8,128)} %shard_map.122), calls=%async_computation | async-start | bytes 2359296 | tf_op jit(solution)/shard_map/all_to_all | solution.py:421
  16.0 0.0 copy-start.5
  16.0 2.3 %shard_map.123 = (f32[3,128,128]{2,1,0:T(8,128)}, f32[128,128]{1,0:T(8,128)}, f32[128,128]{1,0:T(8,128)}, f32[128,128]{1,0:T(8,128)}, f32[128,128]{1,0:T(8,128)}) custom-call(s32[16]{0:T(128)} %lengths_ref.15, f32[1,128]{1,0:T(1,128)} %constant.2.clone.inverse_ref, f32[128,256]{1,0:T(8,128)} %key_ref.3, f32[128,256]{1,0:T(8,128)} %value_ref.4), custom_call_target="tpu_custom_call" | custom-call | flops 1000 | bytes 1000 | tf_op jit(solution)/shard_map/pallas_call | solution.py:54
  18.3 4.2 %collective-permute-start.3 = (f32[128,128]{1,0:T(8,128)}, f32[128,128]{1,0:T(8,128)S(1)}, u32[]{:S(2)}, u32[]{:S(2)}) collective-permute-start(f32[128,128]{1,0:T(8,128)} %get-tuple-element.44), channel_id=1, source_target_pairs={{0,68},{4,196},{64,0},{68,128},{128,4},{132,132},{192,64},{196,192... | collective-permute-start | bytes 196616 | tf_op jit(solution)/shard_map/ppermute | solution.py:432
  22.5 0.8 collective-permute-start.2
  23.4 3.6 %collective-permute-start.1 = (f32[128,128]{1,0:T(8,128)}, f32[128,128]{1,0:T(8,128)S(1)}, u32[]{:S(2)}, u32[]{:S(2)}) collective-permute-start(f32[128,128]{1,0:T(8,128)} %get-tuple-element.42), channel_id=1, source_target_pairs={{0,4},{4,132},{64,64},{68,192},{128,68},{132,196},{192,0},{196,128... | collective-permute-start | bytes 196616 | tf_op jit(solution)/shard_map/ppermute | solution.py:432
  27.0 1.9 %collective-permute-start = (f32[128,128]{1,0:T(8,128)}, f32[128,128]{1,0:T(8,128)S(1)}, u32[]{:S(2)}, u32[]{:S(2)}) collective-permute-start(f32[128,128]{1,0:T(8,128)} %get-tuple-element.41), channel_id=1, source_target_pairs={{0,0},{4,128},{64,4},{68,132},{128,64},{132,192},{192,68},{196,196... | collective-permute-start | bytes 196616 | tf_op jit(solution)/shard_map/ppermute | solution.py:432
  28.9 0.0 collective-permute-done.3
  28.9 0.0 collective-permute-done.2
  28.9 0.9 collective-permute-done.1
  29.8 4.7 %collective-permute-done = f32[128,128]{1,0:T(8,128)S(1)} collective-permute-done((f32[128,128]{1,0:T(8,128)}, f32[128,128]{1,0:T(8,128)S(1)}, u32[]{:S(2)}, u32[]{:S(2)}) %collective-permute-start) | collective-permute-done | bytes 65568 | tf_op jit(solution)/shard_map/ppermute | solution.py:432
  34.5 3.1 %collective-permute-start.4 = (f32[4,128,128]{2,1,0:T(8,128)S(1)}, f32[4,128,128]{2,1,0:T(8,128)S(1)}, u32[]{:S(2)}, u32[]{:S(2)}) collective-permute-start(f32[4,128,128]{2,1,0:T(8,128)S(1)} %pad_maximum_fusion.refs_4_), channel_id=1, source_target_pairs={{0,8},{8,16},{16,24},{24,32},{32,40},{40,48},{48,56},{56,0},{1,9},... | collective-permute-start | bytes 786440 | tf_op jit(solution)/shard_map/ppermute | solution.py:437
  37.6 0.6 collective-permute-start.5
  38.2 2.8 %shard_map.124 = (f32[128,512]{1,0:T(8,128)}, f32[128,512]{1,0:T(8,128)}, f32[128,512]{1,0:T(8,128)}, f32[128,512]{1,0:T(8,128)}) custom-call(s32[16]{0:T(128)} %lengths_ref.15, f32[3,128,128]{2,1,0:T(8,128)} %get-tuple-element.45.tables_ref, f32[128,2048]{1,0:T(8,128)} %query_ref), custom_call_target="tpu_custom_call" | custom-call | flops 1000 | bytes 1000 | tf_op jit(solution)/shard_map/pallas_call | solution.py:54
  40.9 1.9 %collective-permute-start.8 = (f32[128,512]{1,0:T(8,128)}, f32[128,512]{1,0:T(8,128)S(1)}, u32[]{:S(2)}, u32[]{:S(2)}) collective-permute-start(f32[128,512]{1,0:T(8,128)} %get-tuple-element.52), channel_id=1, source_target_pairs={{0,0},{4,128},{64,4},{68,132},{128,64},{132,192},{192,68},{196,196... | collective-permute-start | bytes 786440 | tf_op jit(solution)/shard_map/ppermute | solution.py:448
  42.8 5.1 %collective-permute-start.9 = (f32[128,512]{1,0:T(8,128)}, f32[128,512]{1,0:T(8,128)S(1)}, u32[]{:S(2)}, u32[]{:S(2)}) collective-permute-start(f32[128,512]{1,0:T(8,128)} %get-tuple-element.53), channel_id=1, source_target_pairs={{0,4},{4,132},{64,64},{68,192},{128,68},{132,196},{192,0},{196,128... | collective-permute-start | bytes 786440 | tf_op jit(solution)/shard_map/ppermute | solution.py:448
  48.0 0.7 bitcast_dynamic-update-slice_fusion.6
  48.7 1.1 collective-permute-done.4.refs_5_
  49.8 0.0 copy-start
  49.8 0.0 copy-start.1
  49.8 0.0 copy-start.2
  49.8 0.0 copy-start.4
  49.8 0.1 collective-permute-start.6
  49.9 2.7 %collective-permute-start.7 = (f32[4,128,128]{2,1,0:T(8,128)S(1)}, f32[4,128,128]{2,1,0:T(8,128)S(1)}, u32[]{:S(2)}, u32[]{:S(2)}) collective-permute-start(f32[4,128,128]{2,1,0:T(8,128)S(1)} %collective-permute-done.5.refs_6_), channel_id=1, source_target_pairs={{8,0},{16,8},{24,16},{32,24},{40,32},{48,40},{56,48},{0,56},{9,1},... | collective-permute-start | bytes 786440 | tf_op jit(solution)/shard_map/ppermute | solution.py:450
  52.6 1.7 %collective-permute-start.10 = (f32[128,512]{1,0:T(8,128)}, f32[128,512]{1,0:T(8,128)S(1)}, u32[]{:S(2)}, u32[]{:S(2)}) collective-permute-start(f32[128,512]{1,0:T(8,128)} %get-tuple-element.54), channel_id=1, source_target_pairs={{0,64},{4,192},{64,68},{68,196},{128,0},{132,128},{192,4},{196,132... | collective-permute-start | bytes 786440 | tf_op jit(solution)/shard_map/ppermute | solution.py:448
  54.3 3.7 %collective-permute-start.11 = (f32[128,512]{1,0:T(8,128)}, f32[128,512]{1,0:T(8,128)S(1)}, u32[]{:S(2)}, u32[]{:S(2)}) collective-permute-start(f32[128,512]{1,0:T(8,128)} %get-tuple-element.55), channel_id=1, source_target_pairs={{0,68},{4,196},{64,0},{68,128},{128,4},{132,132},{192,64},{196,192... | collective-permute-start | bytes 786440 | tf_op jit(solution)/shard_map/ppermute | solution.py:448
  58.0 0.7 bitcast_dynamic-update-slice_fusion.5
  58.7 1.6 %shard_map.125 = f32[32,64,128]{2,1,0:T(8,128)} custom-call(s32[16]{0:T(128)S(1)} %copy-done.5, f32[32,72,128]{2,1,0:T(8,128)S(1)} %all-to-all-done.in_ref), custom_call_target="tpu_custom_call" | custom-call | flops 1000 | bytes 1000 | tf_op jit(solution)/shard_map/pallas_call | solution.py:54
  60.3 0.7 bitcast_dynamic-update-slice_fusion.4
  61.0 0.0 collective-permute-done.9.refs_1_
  61.0 0.0 collective-permute-done.6.refs_7_
  61.1 0.0 collective-permute-done.10.refs_2_
  61.1 2.3 %collective-permute-done.11.refs_3_ = f32[128,512]{1,0:T(8,128)S(1)} collective-permute-done((f32[128,512]{1,0:T(8,128)}, f32[128,512]{1,0:T(8,128)S(1)}, u32[]{:S(2)}, u32[]{:S(2)}) %collective-permute-start.11) | collective-permute-done | bytes 262176 | tf_op jit(solution)/shard_map/ppermute | solution.py:448
  63.4 2.7 %collective-permute-start.13 = (f32[4,128,128]{2,1,0:T(8,128)S(1)}, f32[4,128,128]{2,1,0:T(8,128)S(1)}, u32[]{:S(2)}, u32[]{:S(2)}) collective-permute-start(f32[4,128,128]{2,1,0:T(8,128)S(1)} %collective-permute-done.7.refs_8_), channel_id=1, source_target_pairs={{8,0},{16,8},{24,16},{32,24},{40,32},{48,40},{56,48},{0,56},{9,1},... | collective-permute-start | bytes 786440 | tf_op jit(solution)/shard_map/ppermute | solution.py:461
  66.1 0.7 bitcast_dynamic-update-slice_fusion.3
  66.9 6.7 %shard_map.126.intra_ref = f32[128,2048]{1,0:T(8,128)S(1)} custom-call(s32[16]{0:T(128)S(1)} %copy-done.5, f32[16,128]{1,0:T(8,128)S(1)} %copy-done.4, f32[128,2048]{1,0:T(8,128)S(1)} %copy-done.2, f32[128,2048]{1,0:T(8,128)S(1)} %copy-done, f32[128,2048]{1,0:T(8,128)S(1)} %copy-done.1), custom_call_target="tpu_custom_call" | custom-call | flops 1000 | bytes 1000 | tf_op jit(solution)/shard_map/pallas_call | solution.py:54
  73.6 1.0 copy-done.3
  74.6 0.7 bitcast_dynamic-update-slice_fusion.2
  75.3 0.0 collective-permute-done.12.refs_9_
  75.3 0.0 collective-permute-done.13.refs_10_
  75.3 0.8 bitcast_dynamic-update-slice_fusion.1
  76.2 0.7 bitcast_dynamic-update-slice_fusion
  76.9 1.6 %collective-permute-start.15 = (f32[7,4,128,128]{3,2,1,0:T(8,128)}, f32[7,4,128,128]{3,2,1,0:T(8,128)S(1)}, u32[]{:S(2)}, u32[]{:S(2)}) collective-permute-start(f32[7,4,128,128]{3,2,1,0:T(8,128)} %bitcast_dynamic-update-slice_fusion), channel_id=1, source_target_pairs={{0,4},{4,0},{1,5},{5,1},{2,6},{6,2},{3,7},{7,3},{8,12},{12,8},{9,1... | collective-permute-start | bytes 5505032 | tf_op jit(solution)/shard_map/ppermute | solution.py:469
  78.4 0.0 collective-permute-start.14
  78.4 2.8 %collective-permute-start.16 = (f32[4,128,128]{2,1,0:T(8,128)S(1)}, f32[4,128,128]{2,1,0:T(8,128)S(1)}, u32[]{:S(2)}, u32[]{:S(2)}) collective-permute-start(f32[4,128,128]{2,1,0:T(8,128)S(1)} %collective-permute-done.13.refs_10_), channel_id=1, source_target_pairs={{0,60},{4,56},{8,4},{12,0},{16,12},{20,8},{24,20},{28,16},{32,28},... | collective-permute-start | bytes 786440 | tf_op jit(solution)/shard_map/ppermute | solution.py:467
  81.3 8.0 %all-to-all-start.1 = ((f32[32,64,128]{2,1,0:T(8,128)}), f32[32,64,128]{2,1,0:T(8,128)}, u32[]{:S(2)}, u32[]{:S(2)}) async-start(f32[32,64,128]{2,1,0:T(8,128)} %shard_map.125), calls=%async_computation.1 | async-start | bytes 2097152 | tf_op jit(solution)/shard_map/all_to_all | solution.py:471
  89.2 0.0 collective-permute-done.14.refs_11_
  89.3 0.0 collective-permute-done.16.refs_13_
  89.3 0.7 copy-done.19
  90.0 0.1 copy-done.20
  90.1 1.3 copy-done.14
  91.4 20.6 %shard_map.128 = (f32[128,512]{1,0:T(8,128)}, f32[128,512]{1,0:T(8,128)}, f32[128,512]{1,0:T(8,128)}, f32[128,512]{1,0:T(8,128)}) custom-call(s32[16]{0:T(128)} %lengths_ref.15, f32[128,512]{1,0:T(8,128)} %copy-done.15, f32[128,512]{1,0:T(8,128)} %copy-done.16, f32[128,512]{1,0:T(8,128)} %copy-done.17, f32[128,512]{1,0:T(8,128)} %copy-done.18, ...), custom_call_target="tpu_custom_call" | custom-call | flops 399999991808 | bytes 8000000 | tf_op jit(solution)/shard_map/pallas_call | solution.py:54
  112.0 3.9 %collective-permute-start.17 = (f32[128,512]{1,0:T(8,128)}, f32[128,512]{1,0:T(8,128)S(1)}, u32[]{:S(2)}, u32[]{:S(2)}) collective-permute-start(f32[128,512]{1,0:T(8,128)} %get-tuple-element.69), channel_id=1, source_target_pairs={{0,0},{128,4},{4,64},{132,68},{64,128},{192,132},{68,192},{196,196... | collective-permute-start | bytes 786440 | tf_op jit(solution)/shard_map/ppermute | solution.py:494
  115.9 1.9 %collective-permute-start.18 = (f32[128,512]{1,0:T(8,128)}, f32[128,512]{1,0:T(8,128)S(1)}, u32[]{:S(2)}, u32[]{:S(2)}) collective-permute-start(f32[128,512]{1,0:T(8,128)} %get-tuple-element.70), channel_id=1, source_target_pairs={{4,0},{132,4},{64,64},{192,68},{68,128},{196,132},{0,192},{128,196... | collective-permute-start | bytes 786440 | tf_op jit(solution)/shard_map/ppermute | solution.py:494
  117.8 0.1 collective-permute-start.19
  117.9 4.0 %collective-permute-start.20 = (f32[128,512]{1,0:T(8,128)}, f32[128,512]{1,0:T(8,128)S(1)}, u32[]{:S(2)}, u32[]{:S(2)}) collective-permute-start(f32[128,512]{1,0:T(8,128)} %get-tuple-element.72), channel_id=1, source_target_pairs={{68,0},{196,4},{0,64},{128,68},{4,128},{132,132},{64,192},{192,196... | collective-permute-start | bytes 786440 | tf_op jit(solution)/shard_map/ppermute | solution.py:494
  121.9 0.0 all-to-all-done.1
  121.9 0.0 copy-start.6
  121.9 4.9 %shard_map.127 = f32[128,2048]{1,0:T(8,128)} custom-call(s32[16]{0:T(128)} %lengths_ref.15, f32[16,128]{1,0:T(8,128)} %rate_ref.5, f32[128,2048]{1,0:T(8,128)} %query_ref.2, f32[16,128,128]{2,1,0:T(8,128)} %bitcast.4.state_ref, f32[128,2048]{1,0:T(8,128)} %copy-done.3, f32[128,2048]{1,0:T(8,128)} %gate_ref.1, f32[1,2048]{1,0:T(1,128)} %bitcast.24), custom_call_target="tpu_custom_call" | custom-call | flops 1000 | bytes 1000 | tf_op jit(solution)/shard_map/pallas_call | solution.py:54
  126.8 1.4 %collective-permute-done.18.refs_1_ = f32[128,512]{1,0:T(8,128)S(1)} collective-permute-done((f32[128,512]{1,0:T(8,128)}, f32[128,512]{1,0:T(8,128)S(1)}, u32[]{:S(2)}, u32[]{:S(2)}) %collective-permute-start.18) | collective-permute-done | bytes 262176 | tf_op jit(solution)/shard_map/ppermute | solution.py:494
  128.3 1.0 collective-permute-done.19.refs_2_
  129.3 1.9 %collective-permute-done.20.refs_3_ = f32[128,512]{1,0:T(8,128)S(1)} collective-permute-done((f32[128,512]{1,0:T(8,128)}, f32[128,512]{1,0:T(8,128)S(1)}, u32[]{:S(2)}, u32[]{:S(2)}) %collective-permute-start.20) | collective-permute-done | bytes 262176 | tf_op jit(solution)/shard_map/ppermute | solution.py:494
  131.2 1.6 %shard_map.129 = f32[128,2048]{1,0:T(8,128)} custom-call(s32[16]{0:T(128)S(1)} %copy-done.6, f32[128,512]{1,0:T(8,128)S(1)} %collective-permute-done.17.refs_0_, f32[128,512]{1,0:T(8,128)S(1)} %collective-permute-done.18.refs_1_, f32[128,512]{1,0:T(8,128)S(1)} %collective-permute-done.19.refs_2_, f32[128,512]{1,0:T(8,128)S(1)} %collective-permute-done.20.refs_3_), custom_call_target="tpu_custom_call" | custom-call | flops 1000 | bytes 1000 | tf_op jit(solution)/shard_map/pallas_call | solution.py:54
  (40 shorter events, 0.1 us)
Async XLA Ops:
  4.9 44.9 %all-to-all-start = ((f32[32,72,128]{2,1,0:T(8,128)}), f32[32,72,128]{2,1,0:T(8,128)S(1)}, u32[]{:S(2)}, u32[]{:S(2)}) async-start(f32[32,72,128]{2,1,0:T(8,128)} %shard_map.122), calls=%async_computation | async-start | bytes 2359296 | tf_op jit(solution)/shard_map/all_to_all | solution.py:421
  16.0 42.7 %copy-start.5 = (s32[16]{0:T(128)S(1)}, s32[16]{0:T(128)}, u32[]{:S(2)}) copy-start(s32[16]{0:T(128)} %lengths_ref.15) | copy-start | bytes 196
  18.3 10.6 %collective-permute-start.3 = (f32[128,128]{1,0:T(8,128)}, f32[128,128]{1,0:T(8,128)S(1)}, u32[]{:S(2)}, u32[]{:S(2)}) collective-permute-start(f32[128,128]{1,0:T(8,128)} %get-tuple-element.44), channel_id=1, source_target_pairs={{0,68},{4,196},{64,0},{68,128},{128,4},{132,132},{192,64},{196,192... | collective-permute-start | bytes 196616 | tf_op jit(solution)/shard_map/ppermute | solution.py:432
  22.5 6.4 %collective-permute-start.2 = (f32[128,128]{1,0:T(8,128)}, f32[128,128]{1,0:T(8,128)S(1)}, u32[]{:S(2)}, u32[]{:S(2)}) collective-permute-start(f32[128,128]{1,0:T(8,128)} %get-tuple-element.43), channel_id=1, source_target_pairs={{0,64},{4,192},{64,68},{68,196},{128,0},{132,128},{192,4},{196,132... | collective-permute-start | bytes 196616 | tf_op jit(solution)/shard_map/ppermute | solution.py:432
  23.4 6.5 %collective-permute-start.1 = (f32[128,128]{1,0:T(8,128)}, f32[128,128]{1,0:T(8,128)S(1)}, u32[]{:S(2)}, u32[]{:S(2)}) collective-permute-start(f32[128,128]{1,0:T(8,128)} %get-tuple-element.42), channel_id=1, source_target_pairs={{0,4},{4,132},{64,64},{68,192},{128,68},{132,196},{192,0},{196,128... | collective-permute-start | bytes 196616 | tf_op jit(solution)/shard_map/ppermute | solution.py:432
  27.0 7.5 %collective-permute-start = (f32[128,128]{1,0:T(8,128)}, f32[128,128]{1,0:T(8,128)S(1)}, u32[]{:S(2)}, u32[]{:S(2)}) collective-permute-start(f32[128,128]{1,0:T(8,128)} %get-tuple-element.41), channel_id=1, source_target_pairs={{0,0},{4,128},{64,4},{68,132},{128,64},{132,192},{192,68},{196,196... | collective-permute-start | bytes 196616 | tf_op jit(solution)/shard_map/ppermute | solution.py:432
  34.5 25.8 %copy-start.7 = (f32[4,128,128]{2,1,0:T(8,128)}, f32[4,128,128]{2,1,0:T(8,128)S(1)}, u32[]{:S(2)}) copy-start(f32[4,128,128]{2,1,0:T(8,128)S(1)} %pad_maximum_fusion.refs_4_) | copy-start | bytes 786436
  34.5 15.2 %collective-permute-start.4 = (f32[4,128,128]{2,1,0:T(8,128)S(1)}, f32[4,128,128]{2,1,0:T(8,128)S(1)}, u32[]{:S(2)}, u32[]{:S(2)}) collective-permute-start(f32[4,128,128]{2,1,0:T(8,128)S(1)} %pad_maximum_fusion.refs_4_), channel_id=1, source_target_pairs={{0,8},{8,16},{16,24},{24,32},{32,40},{40,48},{48,56},{56,0},{1,9},... | collective-permute-start | bytes 786440 | tf_op jit(solution)/shard_map/ppermute | solution.py:437
  37.6 12.2 %collective-permute-start.5 = (f32[4,128,128]{2,1,0:T(8,128)S(1)}, f32[4,128,128]{2,1,0:T(8,128)S(1)}, u32[]{:S(2)}, u32[]{:S(2)}) collective-permute-start(f32[4,128,128]{2,1,0:T(8,128)S(1)} %pad_maximum_fusion.refs_4_), channel_id=1, source_target_pairs={{8,0},{16,8},{24,16},{32,24},{40,32},{48,40},{56,48},{0,56},{9,1},... | collective-permute-start | bytes 786440 | tf_op jit(solution)/shard_map/ppermute | solution.py:438
  40.9 13.4 %collective-permute-start.8 = (f32[128,512]{1,0:T(8,128)}, f32[128,512]{1,0:T(8,128)S(1)}, u32[]{:S(2)}, u32[]{:S(2)}) collective-permute-start(f32[128,512]{1,0:T(8,128)} %get-tuple-element.52), channel_id=1, source_target_pairs={{0,0},{4,128},{64,4},{68,132},{128,64},{132,192},{192,68},{196,196... | collective-permute-start | bytes 786440 | tf_op jit(solution)/shard_map/ppermute | solution.py:448
  42.8 18.2 %collective-permute-start.9 = (f32[128,512]{1,0:T(8,128)}, f32[128,512]{1,0:T(8,128)S(1)}, u32[]{:S(2)}, u32[]{:S(2)}) collective-permute-start(f32[128,512]{1,0:T(8,128)} %get-tuple-element.53), channel_id=1, source_target_pairs={{0,4},{4,132},{64,64},{68,192},{128,68},{132,196},{192,0},{196,128... | collective-permute-start | bytes 786440 | tf_op jit(solution)/shard_map/ppermute | solution.py:448
  49.8 17.0 %copy-start.8 = (f32[4,128,128]{2,1,0:T(8,128)}, f32[4,128,128]{2,1,0:T(8,128)S(1)}, u32[]{:S(2)}) copy-start(f32[4,128,128]{2,1,0:T(8,128)S(1)} %collective-permute-done.4.refs_5_) | copy-start | bytes 786436
  49.8 17.0 %copy-start.9 = (f32[4,128,128]{2,1,0:T(8,128)}, f32[4,128,128]{2,1,0:T(8,128)S(1)}, u32[]{:S(2)}) copy-start(f32[4,128,128]{2,1,0:T(8,128)S(1)} %collective-permute-done.5.refs_6_) | copy-start | bytes 786436
  49.8 17.0 %copy-start = (f32[128,2048]{1,0:T(8,128)S(1)}, f32[128,2048]{1,0:T(8,128)}, u32[]{:S(2)}) copy-start(f32[128,2048]{1,0:T(8,128)} %key_ref.4) | copy-start | bytes 3145732
  49.8 17.0 %copy-start.1 = (f32[128,2048]{1,0:T(8,128)S(1)}, f32[128,2048]{1,0:T(8,128)}, u32[]{:S(2)}) copy-start(f32[128,2048]{1,0:T(8,128)} %value_ref.5) | copy-start | bytes 3145732
  49.8 17.0 %copy-start.2 = (f32[128,2048]{1,0:T(8,128)S(1)}, f32[128,2048]{1,0:T(8,128)}, u32[]{:S(2)}) copy-start(f32[128,2048]{1,0:T(8,128)} %query_ref.2) | copy-start | bytes 3145732
  49.8 17.0 %copy-start.4 = (f32[16,128]{1,0:T(8,128)S(1)}, f32[16,128]{1,0:T(8,128)}, u32[]{:S(2)}) copy-start(f32[16,128]{1,0:T(8,128)} %rate_ref.5) | copy-start | bytes 24580
  49.8 11.2 %collective-permute-start.6 = (f32[4,128,128]{2,1,0:T(8,128)S(1)}, f32[4,128,128]{2,1,0:T(8,128)S(1)}, u32[]{:S(2)}, u32[]{:S(2)}) collective-permute-start(f32[4,128,128]{2,1,0:T(8,128)S(1)} %collective-permute-done.4.refs_5_), channel_id=1, source_target_pairs={{0,8},{8,16},{16,24},{24,32},{32,40},{40,48},{48,56},{56,0},{1,9},... | collective-permute-start | bytes 786440 | tf_op jit(solution)/shard_map/ppermute | solution.py:449
  49.9 11.1 %collective-permute-start.7 = (f32[4,128,128]{2,1,0:T(8,128)S(1)}, f32[4,128,128]{2,1,0:T(8,128)S(1)}, u32[]{:S(2)}, u32[]{:S(2)}) collective-permute-start(f32[4,128,128]{2,1,0:T(8,128)S(1)} %collective-permute-done.5.refs_6_), channel_id=1, source_target_pairs={{8,0},{16,8},{24,16},{32,24},{40,32},{48,40},{56,48},{0,56},{9,1},... | collective-permute-start | bytes 786440 | tf_op jit(solution)/shard_map/ppermute | solution.py:450
  52.6 8.5 %collective-permute-start.10 = (f32[128,512]{1,0:T(8,128)}, f32[128,512]{1,0:T(8,128)S(1)}, u32[]{:S(2)}, u32[]{:S(2)}) collective-permute-start(f32[128,512]{1,0:T(8,128)} %get-tuple-element.54), channel_id=1, source_target_pairs={{0,64},{4,192},{64,68},{68,196},{128,0},{132,128},{192,4},{196,132... | collective-permute-start | bytes 786440 | tf_op jit(solution)/shard_map/ppermute | solution.py:448
  54.3 12.5 %copy-start.15 = (f32[128,512]{1,0:T(8,128)}, f32[128,512]{1,0:T(8,128)S(1)}, u32[]{:S(2)}) copy-start(f32[128,512]{1,0:T(8,128)S(1)} %collective-permute-done.8.refs_0_) | copy-start | bytes 786436
  54.3 9.1 %collective-permute-start.11 = (f32[128,512]{1,0:T(8,128)}, f32[128,512]{1,0:T(8,128)S(1)}, u32[]{:S(2)}, u32[]{:S(2)}) collective-permute-start(f32[128,512]{1,0:T(8,128)} %get-tuple-element.55), channel_id=1, source_target_pairs={{0,68},{4,196},{64,0},{68,128},{128,4},{132,132},{192,64},{196,192... | collective-permute-start | bytes 786440 | tf_op jit(solution)/shard_map/ppermute | solution.py:448
  61.0 12.5 %copy-start.16 = (f32[128,512]{1,0:T(8,128)}, f32[128,512]{1,0:T(8,128)S(1)}, u32[]{:S(2)}) copy-start(f32[128,512]{1,0:T(8,128)S(1)} %collective-permute-done.9.refs_1_) | copy-start | bytes 786436
  61.0 12.5 %copy-start.10 = (f32[4,128,128]{2,1,0:T(8,128)}, f32[4,128,128]{2,1,0:T(8,128)S(1)}, u32[]{:S(2)}) copy-start(f32[4,128,128]{2,1,0:T(8,128)S(1)} %collective-permute-done.6.refs_7_) | copy-start | bytes 786436
  61.1 12.5 %copy-start.11 = (f32[4,128,128]{2,1,0:T(8,128)}, f32[4,128,128]{2,1,0:T(8,128)S(1)}, u32[]{:S(2)}) copy-start(f32[4,128,128]{2,1,0:T(8,128)S(1)} %collective-permute-done.7.refs_8_) | copy-start | bytes 786436
  61.1 12.5 %copy-start.17 = (f32[128,512]{1,0:T(8,128)}, f32[128,512]{1,0:T(8,128)S(1)}, u32[]{:S(2)}) copy-start(f32[128,512]{1,0:T(8,128)S(1)} %collective-permute-done.10.refs_2_) | copy-start | bytes 786436
  63.4 10.2 %copy-start.18 = (f32[128,512]{1,0:T(8,128)}, f32[128,512]{1,0:T(8,128)S(1)}, u32[]{:S(2)}) copy-start(f32[128,512]{1,0:T(8,128)S(1)} %collective-permute-done.11.refs_3_) | copy-start | bytes 786436
  63.4 11.9 %collective-permute-start.12 = (f32[4,128,128]{2,1,0:T(8,128)S(1)}, f32[4,128,128]{2,1,0:T(8,128)S(1)}, u32[]{:S(2)}, u32[]{:S(2)}) collective-permute-start(f32[4,128,128]{2,1,0:T(8,128)S(1)} %collective-permute-done.6.refs_7_), channel_id=1, source_target_pairs={{0,8},{8,16},{16,24},{24,32},{32,40},{40,48},{48,56},{56,0},{1,9},... | collective-permute-start | bytes 786440 | tf_op jit(solution)/shard_map/ppermute | solution.py:460
  63.4 11.9 %collective-permute-start.13 = (f32[4,128,128]{2,1,0:T(8,128)S(1)}, f32[4,128,128]{2,1,0:T(8,128)S(1)}, u32[]{:S(2)}, u32[]{:S(2)}) collective-permute-start(f32[4,128,128]{2,1,0:T(8,128)S(1)} %collective-permute-done.7.refs_8_), channel_id=1, source_target_pairs={{8,0},{16,8},{24,16},{32,24},{40,32},{48,40},{56,48},{0,56},{9,1},... | collective-permute-start | bytes 786440 | tf_op jit(solution)/shard_map/ppermute | solution.py:461
  73.6 1.0 copy-start.3
  75.3 14.0 %copy-start.12 = (f32[4,128,128]{2,1,0:T(8,128)}, f32[4,128,128]{2,1,0:T(8,128)S(1)}, u32[]{:S(2)}) copy-start(f32[4,128,128]{2,1,0:T(8,128)S(1)} %collective-permute-done.12.refs_9_) | copy-start | bytes 786436
  75.3 14.0 %copy-start.13 = (f32[4,128,128]{2,1,0:T(8,128)}, f32[4,128,128]{2,1,0:T(8,128)S(1)}, u32[]{:S(2)}) copy-start(f32[4,128,128]{2,1,0:T(8,128)S(1)} %collective-permute-done.13.refs_10_) | copy-start | bytes 786436
  76.9 12.4 %collective-permute-start.15 = (f32[7,4,128,128]{3,2,1,0:T(8,128)}, f32[7,4,128,128]{3,2,1,0:T(8,128)S(1)}, u32[]{:S(2)}, u32[]{:S(2)}) collective-permute-start(f32[7,4,128,128]{3,2,1,0:T(8,128)} %bitcast_dynamic-update-slice_fusion), channel_id=1, source_target_pairs={{0,4},{4,0},{1,5},{5,1},{2,6},{6,2},{3,7},{7,3},{8,12},{12,8},{9,1... | collective-permute-start | bytes 5505032 | tf_op jit(solution)/shard_map/ppermute | solution.py:469
  78.4 10.8 %collective-permute-start.14 = (f32[4,128,128]{2,1,0:T(8,128)S(1)}, f32[4,128,128]{2,1,0:T(8,128)S(1)}, u32[]{:S(2)}, u32[]{:S(2)}) collective-permute-start(f32[4,128,128]{2,1,0:T(8,128)S(1)} %collective-permute-done.12.refs_9_), channel_id=1, source_target_pairs={{0,8},{8,16},{16,24},{24,32},{32,40},{40,48},{48,56},{56,0},{1,9},... | collective-permute-start | bytes 786440 | tf_op jit(solution)/shard_map/ppermute | solution.py:463
  78.4 10.8 %collective-permute-start.16 = (f32[4,128,128]{2,1,0:T(8,128)S(1)}, f32[4,128,128]{2,1,0:T(8,128)S(1)}, u32[]{:S(2)}, u32[]{:S(2)}) collective-permute-start(f32[4,128,128]{2,1,0:T(8,128)S(1)} %collective-permute-done.13.refs_10_), channel_id=1, source_target_pairs={{0,60},{4,56},{8,4},{12,0},{16,12},{20,8},{24,20},{28,16},{32,28},... | collective-permute-start | bytes 786440 | tf_op jit(solution)/shard_map/ppermute | solution.py:467
  81.3 40.6 %all-to-all-start.1 = ((f32[32,64,128]{2,1,0:T(8,128)}), f32[32,64,128]{2,1,0:T(8,128)}, u32[]{:S(2)}, u32[]{:S(2)}) async-start(f32[32,64,128]{2,1,0:T(8,128)} %shard_map.125), calls=%async_computation.1 | async-start | bytes 2097152 | tf_op jit(solution)/shard_map/all_to_all | solution.py:471
  89.3 0.7 copy-start.19
  89.3 0.8 copy-start.20
  90.1 1.3 copy-start.14
  112.0 14.9 %collective-permute-start.17 = (f32[128,512]{1,0:T(8,128)}, f32[128,512]{1,0:T(8,128)S(1)}, u32[]{:S(2)}, u32[]{:S(2)}) collective-permute-start(f32[128,512]{1,0:T(8,128)} %get-tuple-element.69), channel_id=1, source_target_pairs={{0,0},{128,4},{4,64},{132,68},{64,128},{192,132},{68,192},{196,196... | collective-permute-start | bytes 786440 | tf_op jit(solution)/shard_map/ppermute | solution.py:494
  115.9 12.4 %collective-permute-start.18 = (f32[128,512]{1,0:T(8,128)}, f32[128,512]{1,0:T(8,128)S(1)}, u32[]{:S(2)}, u32[]{:S(2)}) collective-permute-start(f32[128,512]{1,0:T(8,128)} %get-tuple-element.70), channel_id=1, source_target_pairs={{4,0},{132,4},{64,64},{192,68},{68,128},{196,132},{0,192},{128,196... | collective-permute-start | bytes 786440 | tf_op jit(solution)/shard_map/ppermute | solution.py:494
  117.8 11.5 %collective-permute-start.19 = (f32[128,512]{1,0:T(8,128)}, f32[128,512]{1,0:T(8,128)S(1)}, u32[]{:S(2)}, u32[]{:S(2)}) collective-permute-start(f32[128,512]{1,0:T(8,128)} %get-tuple-element.71), channel_id=1, source_target_pairs={{64,0},{192,4},{68,64},{196,68},{0,128},{128,132},{4,192},{132,196... | collective-permute-start | bytes 786440 | tf_op jit(solution)/shard_map/ppermute | solution.py:494
  117.9 13.3 %collective-permute-start.20 = (f32[128,512]{1,0:T(8,128)}, f32[128,512]{1,0:T(8,128)S(1)}, u32[]{:S(2)}, u32[]{:S(2)}) collective-permute-start(f32[128,512]{1,0:T(8,128)} %get-tuple-element.72), channel_id=1, source_target_pairs={{68,0},{196,4},{0,64},{128,68},{4,128},{132,132},{64,192},{192,196... | collective-permute-start | bytes 786440 | tf_op jit(solution)/shard_map/ppermute | solution.py:494
  121.9 9.3 %copy-start.6 = (s32[16]{0:T(128)S(1)}, s32[16]{0:T(128)}, u32[]{:S(2)}) copy-start(s32[16]{0:T(128)} %lengths_ref.15) | copy-start | bytes 196

commit v3 on v2

--- a/solution.py
+++ b/solution.py
@@ -16,7 +16,8 @@
 CHUNK = 512
 PIECES = (0, 1, -1, 2, -2, 3, -3, 4)
 NEG = -1e30
-QUERIES = 4 * HEAD_DIM
+GROUP = 8
+QUERIES = GROUP * HEAD_DIM
 ROPE_BASE = 10000000.0
 NORM_EPS = 1e-05
 F32 = jnp.float32
@@ -93,6 +94,14 @@
     return lax.axis_index("y") * lax.axis_size("z") + lax.axis_index("z")
 
 
+def sent_in(r):
+    return (lax.axis_index("y") // 2 + r) % 2
+
+
+def row_of(r, core):
+    return 2 * ((lax.axis_index("y") - r + 2) % 2) + core
+
+
 def rope_tables(lengths_ref, inverse_ref, first):
     rows = first + lax.broadcasted_iota(jnp.int32, (TOK, HEAD_DIM), 0)
     lane = lax.broadcasted_iota(jnp.int32, (TOK, HEAD_DIM), 1)
@@ -120,27 +129,18 @@
     tables = rope_tables(lengths_ref, inverse_ref, block_of() * TOK)
     for i in range(3):
         tables_ref[i] = tables[i]
-    mine = lax.axis_index("y")
-    for a in range(2):
-        lanes = slice(a * HEAD_DIM, (a + 1) * HEAD_DIM)
-        k = rotated(key_ref[:, lanes], tables)
-        v = value_ref[:, lanes]
-        for r in range(4):
-            for b, x in ((0, k), (1, v)):
-
-                @pl.when((mine + r) % 4 == 2 * a + b)
-                def _():
-                    pieces[r][...] = x
+    for r in range(2):
+        at = pl.multiple_of(sent_in(r) * HEAD_DIM, HEAD_DIM)
+        pieces[r][:, :HEAD_DIM] = rotated(key_ref[:, pl.ds(at, HEAD_DIM)], tables)
+        pieces[r][:, HEAD_DIM:] = value_ref[:, pl.ds(at, HEAD_DIM)]
 
 
 def query_kernel(lengths_ref, tables_ref, query_ref, *pieces):
     tables = [tables_ref[i] for i in range(3)]
-    mine = lax.axis_index("y")
     scale = math.log2(math.e) / math.sqrt(HEAD_DIM)
-    for r in range(4):
-        e = (mine + r) % 4
-        for n in range(4):
-            at = pl.multiple_of(e * (4 * HEAD_DIM) + n * HEAD_DIM, HEAD_DIM)
+    for r in range(2):
+        for n in range(GROUP):
+            at = pl.multiple_of(sent_in(r) * QUERIES + n * HEAD_DIM, HEAD_DIM)
             x = query_ref[:, pl.ds(at, HEAD_DIM)]
             pieces[r][:, n * HEAD_DIM : (n + 1) * HEAD_DIM] = rotated(x, tables) * scale
 
@@ -148,71 +148,40 @@
 def pack(mine, theirs, kcat, vcat):
     z, zs = lax.axis_index("z"), lax.axis_size("z")
     core = lax.axis_index("head")
-    e_key = 2 * (lax.axis_index("y") % 2)
-
-    def keep(x, at, keys):
-        high, low = halves(x)
-        if keys:
-            kcat[pl.ds(at, TOK), 0:128] = high
-            kcat[pl.ds(at, TOK), 128:256] = high
-            kcat[pl.ds(at, TOK), 256:384] = low
-        else:
-            vcat[pl.ds(at, TOK), 0:128] = high
-            vcat[pl.ds(at, TOK), 128:256] = low
-
-    def fill(i, own, keys):
+    for i in range(8):
         source = (z - PIECES[i] + zs) % zs
-
-        @pl.loop(0, 4)
-        def _(r):
-            row = (e_key + (0 if keys else 1) - r + 4) % 4
-            at = pl.multiple_of((row * zs + source) * TOK, TOK)
-            if own:
-                x = mine[i][r]
-            elif i < 7:
-                x = theirs[0][i, r]
-            else:
-                x = theirs[1][r]
-            keep(x, at, keys)
-
-    @pl.when(core == 0)
-    def _():
-        for i in range(8):
-            fill(i, True, True)
-            fill(i, False, False)
-
-    @pl.when(core == 1)
-    def _():
-        for i in range(8):
-            fill(i, True, False)
-            fill(i, False, True)
-
-
-def in_pairs(low, high, step):
-    pairs = (high - low) // 2
-
-    @pl.loop(0, pairs)
-    def _(i):
-        step(low + 2 * i)
-        step(low + 2 * i + 1)
-
-    pl.when((high - low) % 2 == 1)(lambda: step(high - 1))
+        for own in (True, False):
+            for r in range(2):
+                if own:
+                    x = mine[i][r]
+                elif i < 7:
+                    x = theirs[0][i, r]
+                else:
+                    x = theirs[1][r]
+                row = row_of(r, core if own else 1 - core)
+                at = pl.multiple_of((row * zs + source) * TOK, TOK)
+                high, low = halves(x[:, :HEAD_DIM])
+                kcat[pl.ds(at, TOK), 0:128] = high
+                kcat[pl.ds(at, TOK), 128:256] = high
+                kcat[pl.ds(at, TOK), 256:384] = low
+                high, low = halves(x[:, HEAD_DIM:])
+                vcat[pl.ds(at, TOK), 0:128] = high
+                vcat[pl.ds(at, TOK), 128:256] = low
 
 
 def softmax_kernel(lengths_ref, *refs):
-    queries, mine, theirs, outs = refs[:4], refs[4:12], refs[12:14], refs[14:18]
-    kcat, vcat = refs[18:20]
+    queries, mine, theirs, outs = refs[:2], refs[2:10], refs[10:12], refs[12:14]
+    kcat, vcat = refs[14:16]
     pack(mine, theirs, kcat, vcat)
-    for r in range(4):
-        attend(r, lengths_ref, queries[r], kcat, vcat, outs[r], *refs[20:])
+    for r in range(2):
+        attend(r, lengths_ref, queries[r], kcat, vcat, outs[r], *refs[16:])
 
 
 def attend(r, lengths_ref, query_ref, kcat, vcat, out_ref, *scratch):
     qcat, s_ref, m_ref, l_ref, acc_ref = scratch
-    e = 2 * (lax.axis_index("y") % 2) + lax.axis_index("head")
-    block = ((e - r + 4) % 4) * lax.axis_size("z") + lax.axis_index("z")
+    block = row_of(r, lax.axis_index("head")) * lax.axis_size("z") + lax.axis_index("z")
     first = block * TOK
-    for n in range(4):
+    for n in range(GROUP):
         qh, ql = halves(query_ref[:, n * HEAD_DIM : (n + 1) * HEAD_DIM])
         qcat[n * TOK : (n + 1) * TOK, 0:128] = qh
         qcat[n * TOK : (n + 1) * TOK, 128:256] = ql
@@ -236,8 +205,8 @@
                 lengths_ref, first + lax.broadcasted_iota(jnp.int32, (TOK, 1), 0)
             )
             visible = (keys >= begin) & (keys <= rows)
-            s = jnp.where(visible[None], s.reshape(4, TOK, CHUNK), NEG)
-            s = s.reshape(4 * TOK, CHUNK)
+            s = jnp.where(visible[None], s.reshape(GROUP, TOK, CHUNK), NEG)
+            s = s.reshape(GROUP * TOK, CHUNK)
         s_ref[j] = s
         top = s[:, :HEAD_DIM]
         for i in range(1, CHUNK // HEAD_DIM):
@@ -245,7 +214,7 @@
         m_ref[...] = jnp.maximum(m_ref[...], top)
 
     pl.loop(low, inner)(lambda j: score(j, True))
-    in_pairs(inner, outer, lambda j: score(j, False))
+    pl.loop(inner, outer)(lambda j: score(j, False))
     pl.loop(outer, high)(lambda j: score(j, True))
 
     top = jnp.max(m_ref[...], axis=1, keepdims=True)
@@ -266,21 +235,19 @@
         p = jnp.concatenate(highs + lows, axis=1)
         acc_ref[...] += dot(p, jnp.concatenate([v, v], axis=0), 1, 0)
 
-    in_pairs(low, high, mix)
+    pl.loop(low, high)(mix)
 
     total = jnp.sum(l_ref[...], axis=1, keepdims=True)
     mixed = (acc_ref[:, :HEAD_DIM] + acc_ref[:, HEAD_DIM:]) / total
-    for n in range(4):
+    for n in range(GROUP):
         out_ref[:, n * HEAD_DIM : (n + 1) * HEAD_DIM] = mixed[n * TOK : (n + 1) * TOK]
 
 
 def place_kernel(lengths_ref, *refs):
-    pieces, out_ref = refs[:4], refs[4]
-    mine = lax.axis_index("y")
-    width = 4 * HEAD_DIM
-    for r in range(4):
-        at = pl.multiple_of(((mine + r) % 4) * width, width)
-        out_ref[:, pl.ds(at, width)] = pieces[r][...]
+    pieces, out_ref = refs[:2], refs[2]
+    for r in range(2):
+        at = pl.multiple_of(sent_in(r) * QUERIES, QUERIES)
+        out_ref[:, pl.ds(at, QUERIES)] = pieces[r][...]
 
 
 def thirds(x):
@@ -293,8 +260,12 @@
 def dot6(a, b, ca, cb):
     ah, am, al = thirds(a)
     bh, bm, bl = thirds(b)
-    small = dot(ah, bl, ca, cb) + dot(al, bh, ca, cb) + dot(am, bm, ca, cb)
-    return dot(ah, bh, ca, cb) + (dot(ah, bm, ca, cb) + dot(am, bh, ca, cb) + small)
+    return dot(
+        jnp.concatenate([ah, am, ah, al, am, ah], axis=ca),
+        jnp.concatenate([bl, bm, bm, bh, bh, bh], axis=cb),
+        ca,
+        cb,
+    )
 
 
 def decay_columns(rate_ref):
@@ -364,7 +335,11 @@
         gap = jnp.where(visible, columns[:, h : h + 1] - across[h : h + 1, :], 0.0)
         weight = jnp.where(visible, jnp.exp(gap), 0.0)
         scores = dot6(query_ref[:, lanes], key_ref[:, lanes], 1, 1) * weight
-        out_ref[:, lanes] = dot3(scores, value_ref[:, lanes], 1, 0)
+        sh, sl = halves(scores)
+        vh, vl = halves(value_ref[:, lanes])
+        out_ref[:, lanes] = dot(
+            jnp.concatenate([sh, sl, sh], axis=1), jnp.concatenate([vh, vh, vl], axis=0), 1, 0
+        )
 
 
 def finish_kernel(
@@ -406,12 +381,12 @@
     group = ("y", "head")
     out = jax.ShapeDtypeStruct
     forth, back = [], []
-    for r in range(4):
-        pairs = []
-        for y in range(ys):
-            for h in range(2):
-                piece = (y + r) % 4
-                pairs.append((2 * y + h, 2 * (2 * h + piece // 2) + piece % 2))
+    for r in range(2):
+        pairs = [
+            (2 * y + h, 2 * (2 * h + (y // 2 + r) % 2) + y % 2)
+            for y in range(ys)
+            for h in range(2)
+        ]
         forth.append(pairs)
         back.append([(b, a) for a, b in pairs])
 
@@ -425,7 +400,7 @@
     sm_key, sliced = lax.optimization_barrier((sm_key, sliced))
     tables, *kv_pieces = call(
         kv_kernel,
-        [out((3, rows, HEAD_DIM), F32)] + [out((rows, HEAD_DIM), F32)] * 4,
+        [out((3, rows, HEAD_DIM), F32)] + [out((rows, 2 * HEAD_DIM), F32)] * 2,
         4,
         limit=60,
     )(doc_lengths, jnp.asarray(inverse), sm_key, sm_value)
@@ -437,29 +412,24 @@
     up1 = lax.ppermute(own, "z", up)
     down1 = lax.ppermute(own, "z", down)
 
-    sm_query, own = lax.optimization_barrier((sm_query, own))
-    q_pieces = call(query_kernel, [out((rows, QUERIES), F32)] * 4, 3, limit=60)(
+    sm_query, lin_query, own = lax.optimization_barrier((sm_query, lin_query, own))
+    q_pieces = call(query_kernel, [out((rows, QUERIES), F32)] * 2, 3, limit=60)(
         doc_lengths, tables, sm_query
     )
-    up1, down1, arrived, *second = lax.optimization_barrier(
-        (up1, down1, arrived, *q_pieces[2:])
-    )
-    q_pieces = [*q_pieces[:2], *second]
     here = [lax.ppermute(p, group, forth[r]) for r, p in enumerate(q_pieces)]
+    intra = call(intra_kernel, out((rows, width), F32), 5)(
+        doc_lengths, decay_rate, lin_query, lin_key, lin_value
+    )
+    up1, down1, arrived, intra = lax.optimization_barrier((up1, down1, arrived, intra))
     up2 = lax.ppermute(up1, "z", up)
     down2 = lax.ppermute(down1, "z", down)
     prefixes = call(prefix_kernel, out((blocks, HEAD_DIM // 2, HEAD_DIM), F32), 2)(
         doc_lengths, arrived
     )
-    up2, down2, prefixes, lin_query, *here = lax.optimization_barrier(
-        (up2, down2, prefixes, lin_query, *here)
-    )
-    intra = call(intra_kernel, out((rows, width), F32), 5)(
-        doc_lengths, decay_rate, lin_query, lin_key, lin_value
-    )
+    up2, down2, prefixes, *here = lax.optimization_barrier((up2, down2, prefixes, *here))
     up3 = lax.ppermute(up2, "z", up)
     down3 = lax.ppermute(down2, "z", down)
-    up3, down3, prefixes, intra = lax.optimization_barrier((up3, down3, prefixes, intra))
+    up3, down3, prefixes = lax.optimization_barrier((up3, down3, prefixes))
     up4 = lax.ppermute(up3, "z", up)
     cross = [
         (2 * i + c, 2 * ((i - 1) % zs) + 1 - c) for i in range(zs) for c in range(2)
@@ -474,16 +444,16 @@
     keys = blocks * TOK
     mixed = call(
         softmax_kernel,
-        [out((rows, 4 * HEAD_DIM), F32)] * 4,
-        15,
+        [out((rows, QUERIES), F32)] * 2,
+        13,
         scratch=[
             pltpu.VMEM((keys, 384), BF16),
             pltpu.VMEM((keys, 256), BF16),
-            pltpu.VMEM((4 * TOK, 384), BF16),
-            pltpu.VMEM((keys // CHUNK, 4 * TOK, CHUNK), F32),
-            pltpu.VMEM((4 * TOK, HEAD_DIM), F32),
-            pltpu.VMEM((4 * TOK, HEAD_DIM), F32),
-            pltpu.VMEM((4 * TOK, 2 * HEAD_DIM), F32),
+            pltpu.VMEM((GROUP * TOK, 384), BF16),
+            pltpu.VMEM((keys // CHUNK, GROUP * TOK, CHUNK), F32),
+            pltpu.VMEM((GROUP * TOK, HEAD_DIM), F32),
+            pltpu.VMEM((GROUP * TOK, HEAD_DIM), F32),
+            pltpu.VMEM((GROUP * TOK, 2 * HEAD_DIM), F32),
         ],
         limit=60,
         flops=400_000_000_000,
@@ -493,7 +463,7 @@
     )
     returned = [lax.ppermute(p, group, back[r]) for r, p in enumerate(mixed)]
 
-    lin_out = call(finish_kernel, out((rows, width), F32), 7, limit=60)(
+    lin_out = call(finish_kernel, out((rows, width), F32), 7)(
         doc_lengths,
         decay_rate,
         lin_query,
@@ -503,7 +473,7 @@
         norm_gain.reshape(1, width),
     )
     lin_out, *returned = lax.optimization_barrier((lin_out, *returned))
-    sm_out = call(place_kernel, out((rows, width), F32), 5)(doc_lengths, *returned)
+    sm_out = call(place_kernel, out((rows, width), F32), 3)(doc_lengths, *returned)
     return (lin_out, sm_out)
 
 

time: 133 us -> 124 us (0.932); the launches traced: 133 us -> 121 us
  starting transfers between devices: 65.5 us -> 43.2 us
  waiting for transfers between devices: 13.4 us -> 26.1 us
  Pallas kernels: 44.6 us -> 41.4 us
  local copies, waits for them, and re-layouts: 8.32 us -> 9.71 us
    ppermute x4 -> x2, starting transfers between devices: 12.4 us -> 3.78 us  [shards(): here = [lax.ppermute(p, group, forth[r]) for r, p in enumerate(q_pieces)]]
    ppermute x4 -> x2, starting transfers between devices: 9.92 us -> 2 us  [shards(): returned = [lax.ppermute(p, group, back[r]) for r, p in enumerate(mixed)]]
    ppermute x4 -> x2, waiting for transfers between devices: 4.38 us -> 11 us  [shards(): returned = [lax.ppermute(p, group, back[r]) for r, p in enumerate(mixed)]]
    ppermute x4 -> x2, starting transfers between devices: 10.6 us -> 4.32 us  [shards(): lax.ppermute(p, group, forth[r])]
    pallas_call x8, Pallas kernels: 44.6 us -> 41.4 us  [run(): built(kernel, out_shape, [a.shape for a in arrays], **options)]
    ppermute x4 -> x2, waiting for transfers between devices: 2.34 us -> 0.01 us  [shards(): here = [lax.ppermute(p, group, forth[r]) for r, p in enumerate(q_pieces)]]
    ppermute x1, waiting for transfers between devices: 0.01 us -> 2.33 us  [shards(): up3 = lax.ppermute(up2, 'z', up)]
    ppermute x1, waiting for transfers between devices: 1.06 us -> 3.31 us  [shards(): up1 = lax.ppermute(own, 'z', up)]
  transfers between devices with their start and end apart: 23 -> 17, of which waited for: 7 -> 9; matrix products, arithmetic and copies ran while one was open for 3% -> 4% of each run, Pallas kernels for 29% -> 29%
where the time goes in v3:
time: 124 us; the launch traced here: 121 us
  starting transfers between devices  43.2 us (35%)
  Pallas kernels  41.4 us (33%)
  waiting for transfers between devices  26.1 us (21%)
  local copies, waits for them, and re-layouts  9.71 us (8%)
    pallas_call x8, Pallas kernels, run(): built(kernel, out_shape, [a.shape for a in arrays], **options)  41.4 us
    all_to_all x1, starting transfers between devices, shards(): arrived = lax.all_to_all(sliced, ('y', 'z'), 0, 0, tiled=True)  11.1 us
    ppermute x2, waiting for transfers between devices, shards(): returned = [lax.ppermute(p, group, back[r]) for r, p in enumerate(mixed)]  11 us
    unnamed x46, local copies, waits for them, and re-layouts  9 us
    all_to_all x1, starting transfers between devices, shards(): state = lax.all_to_all(prefixes, ('y', 'z'), 0, 0, tiled=True)  7.71 us
    ppermute x2, waiting for transfers between devices, shards(): lax.ppermute(p, group, forth[r])  7.38 us
    ppermute x2, starting transfers between devices, shards(): lax.ppermute(p, group, forth[r])  4.32 us
    ppermute x2, starting transfers between devices, shards(): here = [lax.ppermute(p, group, forth[r]) for r, p in enumerate(q_pieces)]  3.78 us
  transfers between devices with their start and end apart: 17, of which 9 were waited for; matrix products, arithmetic and copies ran while one was open for 4% of the time, Pallas kernels for 29%

profile of v3, /device:TPU:13, one launch (start us, length us, event | category | flops | bytes accessed | tf_op | source)
XLA Modules:
  0.0 121.4 jit_solution(7787342025234570381)
XLA Ops:
  0.6 4.3 %shard_map.122 = f32[32,72,128]{2,1,0:T(8,128)} custom-call(s32[16]{0:T(128)} %lengths_ref.15, f32[16,128]{1,0:T(8,128)} %rate_ref.5, f32[128,2048]{1,0:T(8,128)} %key_ref.4, f32[128,2048]{1,0:T(8,128)} %value_ref.5), custom_call_target="tpu_custom_call" | custom-call | flops 1000 | bytes 1000 | tf_op jit(solution)/shard_map/pallas_call | solution.py:55
  4.9 11.1 %all-to-all-start = ((f32[32,72,128]{2,1,0:T(8,128)}), f32[32,72,128]{2,1,0:T(8,128)S(1)}, u32[]{:S(2)}, u32[]{:S(2)}) async-start(f32[32,72,128]{2,1,0:T(8,128)} %shard_map.122), calls=%async_computation | async-start | bytes 2359296 | tf_op jit(solution)/shard_map/all_to_all | solution.py:396
  16.0 0.0 copy-start
  16.1 0.0 copy-start.1
  16.1 0.0 copy-start.7
  16.1 0.0 copy-start.9
  16.1 2.2 %shard_map.123 = (f32[3,128,128]{2,1,0:T(8,128)}, f32[128,256]{1,0:T(8,128)}, f32[128,256]{1,0:T(8,128)}) custom-call(s32[16]{0:T(128)} %lengths_ref.15, f32[1,128]{1,0:T(1,128)} %constant.2.clone.inverse_ref, f32[128,256]{1,0:T(8,128)} %key_ref.3, f32[128,256]{1,0:T(8,128)} %value_ref.4), custom_call_target="tpu_custom_call" | custom-call | flops 1000 | bytes 1000 | tf_op jit(solution)/shard_map/pallas_call | solution.py:55
  18.3 1.8 %collective-permute-start.1 = (f32[128,256]{1,0:T(8,128)}, f32[128,256]{1,0:T(8,128)S(1)}, u32[]{:S(2)}, u32[]{:S(2)}) collective-permute-start(f32[128,256]{1,0:T(8,128)} %get-tuple-element.30), channel_id=1, source_target_pairs={{0,64},{4,192},{64,68},{68,196},{128,0},{132,128},{192,4},{196,132... | collective-permute-start | bytes 393224 | tf_op jit(solution)/shard_map/ppermute | solution.py:407
  20.2 2.5 %collective-permute-start = (f32[128,256]{1,0:T(8,128)}, f32[128,256]{1,0:T(8,128)S(1)}, u32[]{:S(2)}, u32[]{:S(2)}) collective-permute-start(f32[128,256]{1,0:T(8,128)} %get-tuple-element.29), channel_id=1, source_target_pairs={{0,0},{4,128},{64,4},{68,132},{128,64},{132,192},{192,68},{196,196... | collective-permute-start | bytes 393224 | tf_op jit(solution)/shard_map/ppermute | solution.py:407
  22.7 0.7 collective-permute-done.1
  23.3 6.7 %collective-permute-done = f32[128,256]{1,0:T(8,128)S(1)} collective-permute-done((f32[128,256]{1,0:T(8,128)}, f32[128,256]{1,0:T(8,128)S(1)}, u32[]{:S(2)}, u32[]{:S(2)}) %collective-permute-start) | collective-permute-done | bytes 131104 | tf_op jit(solution)/shard_map/ppermute | solution.py:407
  30.1 0.0 copy-start.12
  30.1 1.0 collective-permute-start.2
  31.1 1.7 %collective-permute-start.3 = (f32[2,128,256]{2,1,0:T(8,128)S(1)}, f32[2,128,256]{2,1,0:T(8,128)}, u32[]{:S(2)}, u32[]{:S(2)}) collective-permute-start(f32[2,128,256]{2,1,0:T(8,128)S(1)} %pad_maximum_fusion.refs_2_), channel_id=1, source_target_pairs={{8,0},{16,8},{24,16},{32,24},{40,32},{48,40},{56,48},{0,56},{9,1},... | collective-permute-start | bytes 786440 | tf_op jit(solution)/shard_map/ppermute | solution.py:413
  32.8 2.9 %shard_map.126 = (f32[128,1024]{1,0:T(8,128)}, f32[128,1024]{1,0:T(8,128)}) custom-call(s32[16]{0:T(128)} %lengths_ref.15, f32[3,128,128]{2,1,0:T(8,128)} %get-tuple-element.35.tables_ref, f32[128,2048]{1,0:T(8,128)} %query_ref.1), custom_call_target="tpu_custom_call" | custom-call | flops 1000 | bytes 1000 | tf_op jit(solution)/shard_map/pallas_call | solution.py:55
  35.7 3.7 %collective-permute-start.6 = (f32[128,1024]{1,0:T(8,128)}, f32[128,1024]{1,0:T(8,128)}, u32[]{:S(2)}, u32[]{:S(2)}) collective-permute-start(f32[128,1024]{1,0:T(8,128)} %get-tuple-element.37), channel_id=1, source_target_pairs={{0,0},{4,128},{64,4},{68,132},{128,64},{132,192},{192,68},{196,196... | collective-permute-start | bytes 1572872 | tf_op jit(solution)/shard_map/ppermute | solution.py:419
  39.4 0.1 collective-permute-start.7
  39.5 0.7 bitcast_dynamic-update-slice_fusion.6
  40.3 0.0 copy-start.2
  40.3 1.2 %copy-done.2 = f32[128,2048]{1,0:T(8,128)S(1)} copy-done((f32[128,2048]{1,0:T(8,128)S(1)}, f32[128,2048]{1,0:T(8,128)}, u32[]{:S(2)}) %copy-start.2) | copy-done | bytes 1048600
  41.5 3.8 %shard_map.124.intra_ref = f32[128,2048]{1,0:T(8,128)S(1)} custom-call(s32[16]{0:T(128)S(1)} %copy-done.9, f32[16,128]{1,0:T(8,128)S(1)} %copy-done.7, f32[128,2048]{1,0:T(8,128)S(1)} %copy-done.2, f32[128,2048]{1,0:T(8,128)S(1)} %copy-done, f32[128,2048]{1,0:T(8,128)S(1)} %copy-done.1), custom_call_target="tpu_custom_call" | custom-call | flops 1000 | bytes 1000 | tf_op jit(solution)/shard_map/pallas_call | solution.py:55
  45.3 0.0 copy-start.4
  45.3 1.0 copy-done.4
  46.3 3.3 %collective-permute-done.2.refs_3_ = f32[2,128,256]{2,1,0:T(8,128)S(1)} collective-permute-done((f32[2,128,256]{2,1,0:T(8,128)S(1)}, f32[2,128,256]{2,1,0:T(8,128)S(1)}, u32[]{:S(2)}, u32[]{:S(2)}) %collective-permute-start.2) | collective-permute-done | bytes 262176 | tf_op jit(solution)/shard_map/ppermute | solution.py:412
  49.6 0.0 collective-permute-done.3.refs_4_
  49.6 0.0 all-to-all-done.in_ref
  49.6 0.2 collective-permute-start.4
  49.8 2.6 %collective-permute-start.5 = (f32[2,128,256]{2,1,0:T(8,128)}, f32[2,128,256]{2,1,0:T(8,128)S(1)}, u32[]{:S(2)}, u32[]{:S(2)}) collective-permute-start(f32[2,128,256]{2,1,0:T(8,128)} %collective-permute-done.3.refs_4_), channel_id=1, source_target_pairs={{8,0},{16,8},{24,16},{32,24},{40,32},{48,40},{56,48},{0,56},{9,1},... | collective-permute-start | bytes 786440 | tf_op jit(solution)/shard_map/ppermute | solution.py:425
  52.4 0.7 bitcast_dynamic-update-slice_fusion.5
  53.1 1.6 %shard_map.125 = f32[32,64,128]{2,1,0:T(8,128)} custom-call(s32[16]{0:T(128)S(1)} %copy-done.9, f32[32,72,128]{2,1,0:T(8,128)S(1)} %all-to-all-done.in_ref), custom_call_target="tpu_custom_call" | custom-call | flops 1000 | bytes 1000 | tf_op jit(solution)/shard_map/pallas_call | solution.py:55
  54.7 1.7 %bitcast_dynamic-update-slice_fusion.4 = f32[7,2,128,256]{3,2,1,0:T(8,128)} fusion(f32[7,2,128,256]{3,2,1,0:T(8,128)} %bitcast_dynamic-update-slice_fusion.5, f32[2,128,256]{2,1,0:T(8,128)} %collective-permute-done.3.refs_4_), kind=kLoop, calls=%fused_computation.5 | loop fusion | bytes 524288
  56.4 0.0 collective-permute-done.6.refs_0_
  56.4 0.0 collective-permute-done.7.refs_1_
  56.4 0.9 collective-permute-done.4.refs_5_
  57.3 0.0 collective-permute-done.5.refs_6_
  57.3 1.8 %collective-permute-start.8 = (f32[2,128,256]{2,1,0:T(8,128)S(1)}, f32[2,128,256]{2,1,0:T(8,128)S(1)}, u32[]{:S(2)}, u32[]{:S(2)}) collective-permute-start(f32[2,128,256]{2,1,0:T(8,128)S(1)} %collective-permute-done.4.refs_5_), channel_id=1, source_target_pairs={{0,8},{8,16},{16,24},{24,32},{32,40},{40,48},{48,56},{56,0},{1,9},... | collective-permute-start | bytes 786440 | tf_op jit(solution)/shard_map/ppermute | solution.py:430
  59.1 0.9 collective-permute-start.9
  60.0 0.7 bitcast_dynamic-update-slice_fusion.3
  60.7 0.7 bitcast_dynamic-update-slice_fusion.2
  61.5 2.3 %collective-permute-done.8.refs_7_ = f32[2,128,256]{2,1,0:T(8,128)S(1)} collective-permute-done((f32[2,128,256]{2,1,0:T(8,128)S(1)}, f32[2,128,256]{2,1,0:T(8,128)S(1)}, u32[]{:S(2)}, u32[]{:S(2)}) %collective-permute-start.8) | collective-permute-done | bytes 262176 | tf_op jit(solution)/shard_map/ppermute | solution.py:430
  63.8 0.9 collective-permute-done.9.refs_8_
  64.6 0.8 bitcast_dynamic-update-slice_fusion.1
  65.4 0.7 bitcast_dynamic-update-slice_fusion
  66.1 3.2 %collective-permute-start.11 = (f32[7,2,128,256]{3,2,1,0:T(8,128)}, f32[7,2,128,256]{3,2,1,0:T(8,128)}, u32[]{:S(2)}, u32[]{:S(2)}) collective-permute-start(f32[7,2,128,256]{3,2,1,0:T(8,128)} %bitcast_dynamic-update-slice_fusion), channel_id=1, source_target_pairs={{0,4},{4,0},{1,5},{5,1},{2,6},{6,2},{3,7},{7,3},{8,12},{12,8},{9,1... | collective-permute-start | bytes 5505032 | tf_op jit(solution)/shard_map/ppermute | solution.py:439
  69.3 1.7 %collective-permute-start.10 = (f32[2,128,256]{2,1,0:T(8,128)S(1)}, f32[2,128,256]{2,1,0:T(8,128)S(1)}, u32[]{:S(2)}, u32[]{:S(2)}) collective-permute-start(f32[2,128,256]{2,1,0:T(8,128)S(1)} %collective-permute-done.8.refs_7_), channel_id=1, source_target_pairs={{0,8},{8,16},{16,24},{24,32},{32,40},{40,48},{48,56},{56,0},{1,9},... | collective-permute-start | bytes 786440 | tf_op jit(solution)/shard_map/ppermute | solution.py:433
  71.0 1.2 collective-permute-start.12
  72.2 7.7 %all-to-all-start.1 = ((f32[32,64,128]{2,1,0:T(8,128)}), f32[32,64,128]{2,1,0:T(8,128)}, u32[]{:S(2)}, u32[]{:S(2)}) async-start(f32[32,64,128]{2,1,0:T(8,128)} %shard_map.125), calls=%async_computation.1 | async-start | bytes 2097152 | tf_op jit(solution)/shard_map/all_to_all | solution.py:441
  79.9 0.0 collective-permute-done.10.refs_9_
  79.9 0.0 collective-permute-done.12.refs_11_
  79.9 0.7 copy-done.18
  80.6 0.7 copy-done.19
  81.4 0.0 collective-permute-done.11.refs_10_
  81.4 0.0 copy-start.6
  81.4 0.0 copy-start.8
  81.4 0.0 copy-start.10
  81.4 0.0 copy-start.11
  81.4 20.3 %shard_map.128 = (f32[128,1024]{1,0:T(8,128)}, f32[128,1024]{1,0:T(8,128)}) custom-call(s32[16]{0:T(128)} %lengths_ref.15, f32[128,1024]{1,0:T(8,128)} %collective-permute-done.6.refs_0_, f32[128,1024]{1,0:T(8,128)} %collective-permute-done.7.refs_1_, f32[2,128,256]{2,1,0:T(8,128)} %copy-done.12, f32[2,128,256]{2,1,0:T(8,128)} %copy-done.13, ...), custom_call_target="tpu_custom_call" | custom-call | flops 399999991808 | bytes 8000000 | tf_op jit(solution)/shard_map/pallas_call | solution.py:55
  101.8 1.9 %collective-permute-start.13 = (f32[128,1024]{1,0:T(8,128)}, f32[128,1024]{1,0:T(8,128)}, u32[]{:S(2)}, u32[]{:S(2)}) collective-permute-start(f32[128,1024]{1,0:T(8,128)} %get-tuple-element.49), channel_id=1, source_target_pairs={{0,0},{128,4},{4,64},{132,68},{64,128},{192,132},{68,192},{196,196... | collective-permute-start | bytes 1572872 | tf_op jit(solution)/shard_map/ppermute | solution.py:464
  103.7 0.1 collective-permute-start.14
  103.8 0.3 all-to-all-done.1
  104.2 4.0 %shard_map.127 = f32[128,2048]{1,0:T(8,128)} custom-call(s32[16]{0:T(128)S(1)} %copy-done.10, f32[16,128]{1,0:T(8,128)S(1)} %copy-done.8, f32[128,2048]{1,0:T(8,128)S(1)} %copy-done.3, f32[16,128,128]{2,1,0:T(8,128)} %bitcast.2.state_ref, f32[128,2048]{1,0:T(8,128)S(1)} %copy-done.5, f32[128,2048]{1,0:T(8,128)S(1)} %copy-done.6, f32[1,2048]{1,0:T(1,128)S(1)} %bitcast.18), custom_call_target="tpu_custom_call" | custom-call | flops 1000 | bytes 1000 | tf_op jit(solution)/shard_map/pallas_call | solution.py:55
  108.1 6.9 %collective-permute-done.13.refs_0_ = f32[128,1024]{1,0:T(8,128)} collective-permute-done((f32[128,1024]{1,0:T(8,128)}, f32[128,1024]{1,0:T(8,128)}, u32[]{:S(2)}, u32[]{:S(2)}) %collective-permute-start.13) | collective-permute-done | bytes 524320 | tf_op jit(solution)/shard_map/ppermute | solution.py:464
  115.0 4.1 %collective-permute-done.14.refs_1_ = f32[128,1024]{1,0:T(8,128)} collective-permute-done((f32[128,1024]{1,0:T(8,128)}, f32[128,1024]{1,0:T(8,128)}, u32[]{:S(2)}, u32[]{:S(2)}) %collective-permute-start.14) | collective-permute-done | bytes 524320 | tf_op jit(solution)/shard_map/ppermute | solution.py:464
  119.1 2.3 %shard_map.129 = f32[128,2048]{1,0:T(8,128)} custom-call(s32[16]{0:T(128)S(1)} %copy-done.10, f32[128,1024]{1,0:T(8,128)} %collective-permute-done.13.refs_0_, f32[128,1024]{1,0:T(8,128)} %collective-permute-done.14.refs_1_), custom_call_target="tpu_custom_call" | custom-call | flops 1000 | bytes 1000 | tf_op jit(solution)/shard_map/pallas_call | solution.py:55
  (26 shorter events, 0.1 us)
Async XLA Ops:
  4.9 44.7 %all-to-all-start = ((f32[32,72,128]{2,1,0:T(8,128)}), f32[32,72,128]{2,1,0:T(8,128)S(1)}, u32[]{:S(2)}, u32[]{:S(2)}) async-start(f32[32,72,128]{2,1,0:T(8,128)} %shard_map.122), calls=%async_computation | async-start | bytes 2359296 | tf_op jit(solution)/shard_map/all_to_all | solution.py:396
  16.0 24.2 %copy-start = (f32[128,2048]{1,0:T(8,128)S(1)}, f32[128,2048]{1,0:T(8,128)}, u32[]{:S(2)}) copy-start(f32[128,2048]{1,0:T(8,128)} %key_ref.4) | copy-start | bytes 3145732
  16.1 24.2 %copy-start.1 = (f32[128,2048]{1,0:T(8,128)S(1)}, f32[128,2048]{1,0:T(8,128)}, u32[]{:S(2)}) copy-start(f32[128,2048]{1,0:T(8,128)} %value_ref.5) | copy-start | bytes 3145732
  16.1 24.2 %copy-start.7 = (f32[16,128]{1,0:T(8,128)S(1)}, f32[16,128]{1,0:T(8,128)}, u32[]{:S(2)}) copy-start(f32[16,128]{1,0:T(8,128)} %rate_ref.5) | copy-start | bytes 24580
  16.1 24.2 %copy-start.9 = (s32[16]{0:T(128)S(1)}, s32[16]{0:T(128)}, u32[]{:S(2)}) copy-start(s32[16]{0:T(128)} %lengths_ref.15) | copy-start | bytes 196
  18.3 5.0 %collective-permute-start.1 = (f32[128,256]{1,0:T(8,128)}, f32[128,256]{1,0:T(8,128)S(1)}, u32[]{:S(2)}, u32[]{:S(2)}) collective-permute-start(f32[128,256]{1,0:T(8,128)} %get-tuple-element.30), channel_id=1, source_target_pairs={{0,64},{4,192},{64,68},{68,196},{128,0},{132,128},{192,4},{196,132... | collective-permute-start | bytes 393224 | tf_op jit(solution)/shard_map/ppermute | solution.py:407
  20.2 9.9 %collective-permute-start = (f32[128,256]{1,0:T(8,128)}, f32[128,256]{1,0:T(8,128)S(1)}, u32[]{:S(2)}, u32[]{:S(2)}) collective-permute-start(f32[128,256]{1,0:T(8,128)} %get-tuple-element.29), channel_id=1, source_target_pairs={{0,0},{4,128},{64,4},{68,132},{128,64},{132,192},{192,68},{196,196... | collective-permute-start | bytes 393224 | tf_op jit(solution)/shard_map/ppermute | solution.py:407
  30.1 15.3 %copy-start.12 = (f32[2,128,256]{2,1,0:T(8,128)}, f32[2,128,256]{2,1,0:T(8,128)S(1)}, u32[]{:S(2)}) copy-start(f32[2,128,256]{2,1,0:T(8,128)S(1)} %pad_maximum_fusion.refs_2_) | copy-start | bytes 786436
  30.1 19.5 %collective-permute-start.2 = (f32[2,128,256]{2,1,0:T(8,128)S(1)}, f32[2,128,256]{2,1,0:T(8,128)S(1)}, u32[]{:S(2)}, u32[]{:S(2)}) collective-permute-start(f32[2,128,256]{2,1,0:T(8,128)S(1)} %pad_maximum_fusion.refs_2_), channel_id=1, source_target_pairs={{0,8},{8,16},{16,24},{24,32},{32,40},{40,48},{48,56},{56,0},{1,9},... | collective-permute-start | bytes 786440 | tf_op jit(solution)/shard_map/ppermute | solution.py:412
  31.1 18.5 %collective-permute-start.3 = (f32[2,128,256]{2,1,0:T(8,128)S(1)}, f32[2,128,256]{2,1,0:T(8,128)}, u32[]{:S(2)}, u32[]{:S(2)}) collective-permute-start(f32[2,128,256]{2,1,0:T(8,128)S(1)} %pad_maximum_fusion.refs_2_), channel_id=1, source_target_pairs={{8,0},{16,8},{24,16},{32,24},{40,32},{48,40},{56,48},{0,56},{9,1},... | collective-permute-start | bytes 786440 | tf_op jit(solution)/shard_map/ppermute | solution.py:413
  35.7 20.6 %collective-permute-start.6 = (f32[128,1024]{1,0:T(8,128)}, f32[128,1024]{1,0:T(8,128)}, u32[]{:S(2)}, u32[]{:S(2)}) collective-permute-start(f32[128,1024]{1,0:T(8,128)} %get-tuple-element.37), channel_id=1, source_target_pairs={{0,0},{4,128},{64,4},{68,132},{128,64},{132,192},{192,68},{196,196... | collective-permute-start | bytes 1572872 | tf_op jit(solution)/shard_map/ppermute | solution.py:419
  39.4 16.9 %collective-permute-start.7 = (f32[128,1024]{1,0:T(8,128)}, f32[128,1024]{1,0:T(8,128)}, u32[]{:S(2)}, u32[]{:S(2)}) collective-permute-start(f32[128,1024]{1,0:T(8,128)} %get-tuple-element.38), channel_id=1, source_target_pairs={{0,64},{4,192},{64,68},{68,196},{128,0},{132,128},{192,4},{196,132... | collective-permute-start | bytes 1572872 | tf_op jit(solution)/shard_map/ppermute | solution.py:419
  40.3 1.2 %copy-start.2 = (f32[128,2048]{1,0:T(8,128)S(1)}, f32[128,2048]{1,0:T(8,128)}, u32[]{:S(2)}) copy-start(f32[128,2048]{1,0:T(8,128)} %query_ref.2) | copy-start | bytes 3145732
  45.3 1.0 copy-start.4
  49.6 31.7 %copy-start.13 = (f32[2,128,256]{2,1,0:T(8,128)}, f32[2,128,256]{2,1,0:T(8,128)S(1)}, u32[]{:S(2)}) copy-start(f32[2,128,256]{2,1,0:T(8,128)S(1)} %collective-permute-done.2.refs_3_) | copy-start | bytes 786436
  49.6 7.6 %collective-permute-start.4 = (f32[2,128,256]{2,1,0:T(8,128)S(1)}, f32[2,128,256]{2,1,0:T(8,128)S(1)}, u32[]{:S(2)}, u32[]{:S(2)}) collective-permute-start(f32[2,128,256]{2,1,0:T(8,128)S(1)} %collective-permute-done.2.refs_3_), channel_id=1, source_target_pairs={{0,8},{8,16},{16,24},{24,32},{32,40},{40,48},{48,56},{56,0},{1,9},... | collective-permute-start | bytes 786440 | tf_op jit(solution)/shard_map/ppermute | solution.py:424
  49.8 7.5 %collective-permute-start.5 = (f32[2,128,256]{2,1,0:T(8,128)}, f32[2,128,256]{2,1,0:T(8,128)S(1)}, u32[]{:S(2)}, u32[]{:S(2)}) collective-permute-start(f32[2,128,256]{2,1,0:T(8,128)} %collective-permute-done.3.refs_4_), channel_id=1, source_target_pairs={{8,0},{16,8},{24,16},{32,24},{40,32},{48,40},{56,48},{0,56},{9,1},... | collective-permute-start | bytes 786440 | tf_op jit(solution)/shard_map/ppermute | solution.py:425
  57.3 14.9 %copy-start.14 = (f32[2,128,256]{2,1,0:T(8,128)}, f32[2,128,256]{2,1,0:T(8,128)S(1)}, u32[]{:S(2)}) copy-start(f32[2,128,256]{2,1,0:T(8,128)S(1)} %collective-permute-done.4.refs_5_) | copy-start | bytes 786436
  57.3 14.9 %copy-start.15 = (f32[2,128,256]{2,1,0:T(8,128)}, f32[2,128,256]{2,1,0:T(8,128)S(1)}, u32[]{:S(2)}) copy-start(f32[2,128,256]{2,1,0:T(8,128)S(1)} %collective-permute-done.5.refs_6_) | copy-start | bytes 786436
  57.3 6.5 %collective-permute-start.8 = (f32[2,128,256]{2,1,0:T(8,128)S(1)}, f32[2,128,256]{2,1,0:T(8,128)S(1)}, u32[]{:S(2)}, u32[]{:S(2)}) collective-permute-start(f32[2,128,256]{2,1,0:T(8,128)S(1)} %collective-permute-done.4.refs_5_), channel_id=1, source_target_pairs={{0,8},{8,16},{16,24},{24,32},{32,40},{40,48},{48,56},{56,0},{1,9},... | collective-permute-start | bytes 786440 | tf_op jit(solution)/shard_map/ppermute | solution.py:430
  59.1 5.5 %collective-permute-start.9 = (f32[2,128,256]{2,1,0:T(8,128)S(1)}, f32[2,128,256]{2,1,0:T(8,128)S(1)}, u32[]{:S(2)}, u32[]{:S(2)}) collective-permute-start(f32[2,128,256]{2,1,0:T(8,128)S(1)} %collective-permute-done.5.refs_6_), channel_id=1, source_target_pairs={{8,0},{16,8},{24,16},{32,24},{40,32},{48,40},{56,48},{0,56},{9,1},... | collective-permute-start | bytes 786440 | tf_op jit(solution)/shard_map/ppermute | solution.py:431
  63.8 16.1 %copy-start.16 = (f32[2,128,256]{2,1,0:T(8,128)}, f32[2,128,256]{2,1,0:T(8,128)S(1)}, u32[]{:S(2)}) copy-start(f32[2,128,256]{2,1,0:T(8,128)S(1)} %collective-permute-done.8.refs_7_) | copy-start | bytes 786436
  64.6 15.3 %copy-start.17 = (f32[2,128,256]{2,1,0:T(8,128)}, f32[2,128,256]{2,1,0:T(8,128)S(1)}, u32[]{:S(2)}) copy-start(f32[2,128,256]{2,1,0:T(8,128)S(1)} %collective-permute-done.9.refs_8_) | copy-start | bytes 786436
  66.1 15.3 %collective-permute-start.11 = (f32[7,2,128,256]{3,2,1,0:T(8,128)}, f32[7,2,128,256]{3,2,1,0:T(8,128)}, u32[]{:S(2)}, u32[]{:S(2)}) collective-permute-start(f32[7,2,128,256]{3,2,1,0:T(8,128)} %bitcast_dynamic-update-slice_fusion), channel_id=1, source_target_pairs={{0,4},{4,0},{1,5},{5,1},{2,6},{6,2},{3,7},{7,3},{8,12},{12,8},{9,1... | collective-permute-start | bytes 5505032 | tf_op jit(solution)/shard_map/ppermute | solution.py:439
  69.3 10.6 %collective-permute-start.10 = (f32[2,128,256]{2,1,0:T(8,128)S(1)}, f32[2,128,256]{2,1,0:T(8,128)S(1)}, u32[]{:S(2)}, u32[]{:S(2)}) collective-permute-start(f32[2,128,256]{2,1,0:T(8,128)S(1)} %collective-permute-done.8.refs_7_), channel_id=1, source_target_pairs={{0,8},{8,16},{16,24},{24,32},{32,40},{40,48},{48,56},{56,0},{1,9},... | collective-permute-start | bytes 786440 | tf_op jit(solution)/shard_map/ppermute | solution.py:433
  71.0 8.9 %collective-permute-start.12 = (f32[2,128,256]{2,1,0:T(8,128)S(1)}, f32[2,128,256]{2,1,0:T(8,128)S(1)}, u32[]{:S(2)}, u32[]{:S(2)}) collective-permute-start(f32[2,128,256]{2,1,0:T(8,128)S(1)} %collective-permute-done.9.refs_8_), channel_id=1, source_target_pairs={{0,60},{4,56},{8,4},{12,0},{16,12},{20,8},{24,20},{28,16},{32,28},... | collective-permute-start | bytes 786440 | tf_op jit(solution)/shard_map/ppermute | solution.py:437
  72.2 32.0 %all-to-all-start.1 = ((f32[32,64,128]{2,1,0:T(8,128)}), f32[32,64,128]{2,1,0:T(8,128)}, u32[]{:S(2)}, u32[]{:S(2)}) async-start(f32[32,64,128]{2,1,0:T(8,128)} %shard_map.125), calls=%async_computation.1 | async-start | bytes 2097152 | tf_op jit(solution)/shard_map/all_to_all | solution.py:441
  79.9 0.7 copy-start.18
  80.6 0.7 copy-start.19
  81.4 22.8 %copy-start.3 = (f32[128,2048]{1,0:T(8,128)S(1)}, f32[128,2048]{1,0:T(8,128)}, u32[]{:S(2)}) copy-start(f32[128,2048]{1,0:T(8,128)} %query_ref.2) | copy-start | bytes 3145732
  81.4 22.8 %copy-start.5 = (f32[128,2048]{1,0:T(8,128)S(1)}, f32[128,2048]{1,0:T(8,128)}, u32[]{:S(2)}) copy-start(f32[128,2048]{1,0:T(8,128)} %copy-done.4) | copy-start | bytes 3145732
  81.4 22.8 %copy-start.6 = (f32[128,2048]{1,0:T(8,128)S(1)}, f32[128,2048]{1,0:T(8,128)}, u32[]{:S(2)}) copy-start(f32[128,2048]{1,0:T(8,128)} %gate_ref.1) | copy-start | bytes 3145732
  81.4 22.7 %copy-start.8 = (f32[16,128]{1,0:T(8,128)S(1)}, f32[16,128]{1,0:T(8,128)}, u32[]{:S(2)}) copy-start(f32[16,128]{1,0:T(8,128)} %rate_ref.5) | copy-start | bytes 24580
  81.4 22.7 %copy-start.10 = (s32[16]{0:T(128)S(1)}, s32[16]{0:T(128)}, u32[]{:S(2)}) copy-start(s32[16]{0:T(128)} %lengths_ref.15) | copy-start | bytes 196
  81.4 22.7 %copy-start.11 = (f32[2048]{0:T(1024)S(1)}, f32[2048]{0:T(1024)}, u32[]{:S(2)}) copy-start(f32[2048]{0:T(1024)} %param.16) | copy-start | bytes 24580
  101.8 13.3 %collective-permute-start.13 = (f32[128,1024]{1,0:T(8,128)}, f32[128,1024]{1,0:T(8,128)}, u32[]{:S(2)}, u32[]{:S(2)}) collective-permute-start(f32[128,1024]{1,0:T(8,128)} %get-tuple-element.49), channel_id=1, source_target_pairs={{0,0},{128,4},{4,64},{132,68},{64,128},{192,132},{68,192},{196,196... | collective-permute-start | bytes 1572872 | tf_op jit(solution)/shard_map/ppermute | solution.py:464
  103.7 15.4 %collective-permute-start.14 = (f32[128,1024]{1,0:T(8,128)}, f32[128,1024]{1,0:T(8,128)}, u32[]{:S(2)}, u32[]{:S(2)}) collective-permute-start(f32[128,1024]{1,0:T(8,128)} %get-tuple-element.50), channel_id=1, source_target_pairs={{64,0},{192,4},{68,64},{196,68},{0,128},{128,132},{4,192},{132,196... | collective-permute-start | bytes 1572872 | tf_op jit(solution)/shard_map/ppermute | solution.py:464

commit v4 on v3

--- a/solution.py
+++ b/solution.py
@@ -48,6 +48,24 @@
             flops=flops, bytes_accessed=moved, transcendentals=0
         ),
     )
+
+
+def halved(kernel, out, out_axis, arrays, axes):
+    def half(shape, axis):
+        block = tuple(n // 2 if d == axis else n for d, n in enumerate(shape))
+        return pl.BlockSpec(
+            block, lambda i: tuple(i if d == axis else 0 for d in range(len(shape)))
+        )
+
+    return pl.pallas_call(
+        kernel,
+        out_shape=out,
+        grid=(2,),
+        in_specs=[SMEM] + [half(a.shape, axis) for a, axis in zip(arrays[1:], axes)],
+        out_specs=half(out.shape, out_axis),
+        compiler_params=pltpu.CompilerParams(vmem_limit_bytes=60 << 20),
+        cost_estimate=pl.CostEstimate(flops=1000, bytes_accessed=1000, transcendentals=0),
+    )(*arrays)
 
 
 def call(kernel, out_shape, n_in, **options):
@@ -390,9 +408,13 @@
         forth.append(pairs)
         back.append([(b, a) for a, b in pairs])
 
-    sliced = call(
-        state_kernel, out((blocks, HEAD_DIM // 2 + 8, HEAD_DIM), F32), 4, limit=60
-    )(doc_lengths, decay_rate, lin_key, lin_value)
+    sliced = halved(
+        state_kernel,
+        out((blocks, HEAD_DIM // 2 + 8, HEAD_DIM), F32),
+        0,
+        (doc_lengths, decay_rate, lin_key, lin_value),
+        (0, 1, 1),
+    )
     arrived = lax.all_to_all(sliced, ("y", "z"), 0, 0, tiled=True)
 
     inverse = np.zeros((1, HEAD_DIM), np.float32)
@@ -463,14 +485,20 @@
     )
     returned = [lax.ppermute(p, group, back[r]) for r, p in enumerate(mixed)]
 
-    lin_out = call(finish_kernel, out((rows, width), F32), 7)(
-        doc_lengths,
-        decay_rate,
-        lin_query,
-        state,
-        intra,
-        lin_gate,
-        norm_gain.reshape(1, width),
+    lin_out = halved(
+        finish_kernel,
+        out((rows, width), F32),
+        1,
+        (
+            doc_lengths,
+            decay_rate,
+            lin_query,
+            state,
+            intra,
+            lin_gate,
+            norm_gain.reshape(1, width),
+        ),
+        (0, 1, 0, 1, 1, 1),
     )
     lin_out, *returned = lax.optimization_barrier((lin_out, *returned))
     sm_out = call(place_kernel, out((rows, width), F32), 3)(doc_lengths, *returned)

time: 124 us -> 121 us (0.976)
  the two profiles are of different devices: /device:TPU:13 before, /device:TPU:3 now
where the time goes in v4:
time: 121 us; the launch traced here: 120 us
  starting transfers between devices  50.4 us (42%)
  Pallas kernels  40.3 us (33%)
  waiting for transfers between devices  19.7 us (16%)
  local copies, waits for them, and re-layouts  9.04 us (7%)
    pallas_call x6, Pallas kernels, run(): built(kernel, out_shape, [a.shape for a in arrays], **options)  32.5 us
    all_to_all x1, starting transfers between devices, shards(): arrived = lax.all_to_all(sliced, ('y', 'z'), 0, 0, tiled=True)  11.2 us
    ppermute x2, waiting for transfers between devices, shards(): returned = [lax.ppermute(p, group, back[r]) for r, p in enumerate(mixed)]  8.7 us
    unnamed x36, local copies, waits for them, and re-layouts  8.33 us
    all_to_all x1, starting transfers between devices, shards(): state = lax.all_to_all(prefixes, ('y', 'z'), 0, 0, tiled=True)  7.94 us
    pallas_call x2, Pallas kernels, halved(): pl.pallas_call(kernel, out_shape=out, grid=(2,), in_specs=[SMEM] + [half(...  7.76 us
    ppermute x2, starting transfers between devices, shards(): lax.ppermute(p, group, forth[r])  5.99 us
    ppermute x2, waiting for transfers between devices, shards(): lax.ppermute(p, group, forth[r])  5.91 us
  transfers between devices with their start and end apart: 17, of which 7 were waited for; matrix products, arithmetic and copies ran while one was open for 4% of the time, Pallas kernels for 29%

profile of v4, /device:TPU:3, one launch (start us, length us, event | category | flops | bytes accessed | tf_op | source)
XLA Modules:
  0.0 120.2 jit_solution(8513319127322554803)
XLA Ops:
  0.6 3.6 %shard_map.122 = f32[32,72,128]{2,1,0:T(8,128)} custom-call(s32[16]{0:T(128)} %lengths_ref.15, f32[16,128]{1,0:T(8,128)} %rate_ref.5, f32[128,2048]{1,0:T(8,128)} %key_ref.4, f32[128,2048]{1,0:T(8,128)} %value_ref.5), custom_call_target="tpu_custom_call" | custom-call | flops 1000 | bytes 1000 | tf_op jit(solution)/shard_map/pallas_call | solution.py:60
  4.2 11.2 %all-to-all-start = ((f32[32,72,128]{2,1,0:T(8,128)}), f32[32,72,128]{2,1,0:T(8,128)S(1)}, u32[]{:S(2)}, u32[]{:S(2)}) async-start(f32[32,72,128]{2,1,0:T(8,128)} %shard_map.122), calls=%async_computation | async-start | bytes 2359296 | tf_op jit(solution)/shard_map/all_to_all | solution.py:418
  15.4 0.0 copy-start
  15.5 0.0 copy-start.1
  15.5 0.0 copy-start.4
  15.5 0.0 copy-start.5
  15.5 2.2 %shard_map.123 = (f32[3,128,128]{2,1,0:T(8,128)}, f32[128,256]{1,0:T(8,128)}, f32[128,256]{1,0:T(8,128)}) custom-call(s32[16]{0:T(128)} %lengths_ref.15, f32[1,128]{1,0:T(1,128)} %constant.2.clone.inverse_ref, f32[128,256]{1,0:T(8,128)} %key_ref.3, f32[128,256]{1,0:T(8,128)} %value_ref.4), custom_call_target="tpu_custom_call" | custom-call | flops 1000 | bytes 1000 | tf_op jit(solution)/shard_map/pallas_call | solution.py:73
  17.7 3.6 %collective-permute-start.1 = (f32[128,256]{1,0:T(8,128)}, f32[128,256]{1,0:T(8,128)S(1)}, u32[]{:S(2)}, u32[]{:S(2)}) collective-permute-start(f32[128,256]{1,0:T(8,128)} %get-tuple-element.30), channel_id=1, source_target_pairs={{0,64},{4,192},{64,68},{68,196},{128,0},{132,128},{192,4},{196,132... | collective-permute-start | bytes 393224 | tf_op jit(solution)/shard_map/ppermute | solution.py:429
  21.3 2.4 %collective-permute-start = (f32[128,256]{1,0:T(8,128)}, f32[128,256]{1,0:T(8,128)S(1)}, u32[]{:S(2)}, u32[]{:S(2)}) collective-permute-start(f32[128,256]{1,0:T(8,128)} %get-tuple-element.29), channel_id=1, source_target_pairs={{0,0},{4,128},{64,4},{68,132},{128,64},{132,192},{192,68},{196,196... | collective-permute-start | bytes 393224 | tf_op jit(solution)/shard_map/ppermute | solution.py:429
  23.7 3.9 %collective-permute-done.1 = f32[128,256]{1,0:T(8,128)S(1)} collective-permute-done((f32[128,256]{1,0:T(8,128)}, f32[128,256]{1,0:T(8,128)S(1)}, u32[]{:S(2)}, u32[]{:S(2)}) %collective-permute-start.1) | collective-permute-done | bytes 131104 | tf_op jit(solution)/shard_map/ppermute | solution.py:429
  27.6 2.0 %collective-permute-done = f32[128,256]{1,0:T(8,128)S(1)} collective-permute-done((f32[128,256]{1,0:T(8,128)}, f32[128,256]{1,0:T(8,128)S(1)}, u32[]{:S(2)}, u32[]{:S(2)}) %collective-permute-start) | collective-permute-done | bytes 131104 | tf_op jit(solution)/shard_map/ppermute | solution.py:429
  29.7 0.0 copy-start.7
  29.7 0.8 collective-permute-start.2
  30.5 2.5 %collective-permute-start.3 = (f32[2,128,256]{2,1,0:T(8,128)S(1)}, f32[2,128,256]{2,1,0:T(8,128)}, u32[]{:S(2)}, u32[]{:S(2)}) collective-permute-start(f32[2,128,256]{2,1,0:T(8,128)S(1)} %pad_maximum_fusion.refs_2_), channel_id=1, source_target_pairs={{8,0},{16,8},{24,16},{32,24},{40,32},{48,40},{56,48},{0,56},{9,1},... | collective-permute-start | bytes 786440 | tf_op jit(solution)/shard_map/ppermute | solution.py:435
  33.0 2.9 %shard_map.126 = (f32[128,1024]{1,0:T(8,128)}, f32[128,1024]{1,0:T(8,128)}) custom-call(s32[16]{0:T(128)} %lengths_ref.15, f32[3,128,128]{2,1,0:T(8,128)} %get-tuple-element.35.tables_ref, f32[128,2048]{1,0:T(8,128)} %query_ref.1), custom_call_target="tpu_custom_call" | custom-call | flops 1000 | bytes 1000 | tf_op jit(solution)/shard_map/pallas_call | solution.py:73
  35.9 4.3 %collective-permute-start.6 = (f32[128,1024]{1,0:T(8,128)}, f32[128,1024]{1,0:T(8,128)}, u32[]{:S(2)}, u32[]{:S(2)}) collective-permute-start(f32[128,1024]{1,0:T(8,128)} %get-tuple-element.37), channel_id=1, source_target_pairs={{0,0},{4,128},{64,4},{68,132},{128,64},{132,192},{192,68},{196,196... | collective-permute-start | bytes 1572872 | tf_op jit(solution)/shard_map/ppermute | solution.py:441
  40.2 0.8 collective-permute-start.7
  41.0 0.7 bitcast_dynamic-update-slice_fusion.6
  41.7 0.0 copy-done
  41.7 0.0 copy-done.1
  41.7 0.0 copy-done.4
  41.7 0.0 copy-start.2
  41.7 1.2 %copy-done.2 = f32[128,2048]{1,0:T(8,128)S(1)} copy-done((f32[128,2048]{1,0:T(8,128)S(1)}, f32[128,2048]{1,0:T(8,128)}, u32[]{:S(2)}) %copy-start.2) | copy-done | bytes 1048600
  43.0 3.8 %shard_map.124.intra_ref = f32[128,2048]{1,0:T(8,128)S(1)} custom-call(s32[16]{0:T(128)S(1)} %copy-done.5, f32[16,128]{1,0:T(8,128)S(1)} %copy-done.4, f32[128,2048]{1,0:T(8,128)S(1)} %copy-done.2, f32[128,2048]{1,0:T(8,128)S(1)} %copy-done, f32[128,2048]{1,0:T(8,128)S(1)} %copy-done.1), custom_call_target="tpu_custom_call" | custom-call | flops 1000 | bytes 1000 | tf_op jit(solution)/shard_map/pallas_call | solution.py:73
  46.8 1.0 copy-done.3
  47.8 1.4 %collective-permute-done.2.refs_3_ = f32[2,128,256]{2,1,0:T(8,128)S(1)} collective-permute-done((f32[2,128,256]{2,1,0:T(8,128)S(1)}, f32[2,128,256]{2,1,0:T(8,128)S(1)}, u32[]{:S(2)}, u32[]{:S(2)}) %collective-permute-start.2) | collective-permute-done | bytes 262176 | tf_op jit(solution)/shard_map/ppermute | solution.py:434
  49.2 0.0 collective-permute-done.3.refs_4_
  49.2 0.0 all-to-all-done.in_ref
  49.2 0.1 collective-permute-start.4
  49.3 2.7 %collective-permute-start.5 = (f32[2,128,256]{2,1,0:T(8,128)}, f32[2,128,256]{2,1,0:T(8,128)S(1)}, u32[]{:S(2)}, u32[]{:S(2)}) collective-permute-start(f32[2,128,256]{2,1,0:T(8,128)} %collective-permute-done.3.refs_4_), channel_id=1, source_target_pairs={{8,0},{16,8},{24,16},{32,24},{40,32},{48,40},{56,48},{0,56},{9,1},... | collective-permute-start | bytes 786440 | tf_op jit(solution)/shard_map/ppermute | solution.py:447
  51.9 0.7 bitcast_dynamic-update-slice_fusion.5
  52.7 1.6 %shard_map.125 = f32[32,64,128]{2,1,0:T(8,128)} custom-call(s32[16]{0:T(128)S(1)} %copy-done.5, f32[32,72,128]{2,1,0:T(8,128)S(1)} %all-to-all-done.in_ref), custom_call_target="tpu_custom_call" | custom-call | flops 1000 | bytes 1000 | tf_op jit(solution)/shard_map/pallas_call | solution.py:73
  54.2 1.7 %bitcast_dynamic-update-slice_fusion.4 = f32[7,2,128,256]{3,2,1,0:T(8,128)} fusion(f32[7,2,128,256]{3,2,1,0:T(8,128)} %bitcast_dynamic-update-slice_fusion.5, f32[2,128,256]{2,1,0:T(8,128)} %collective-permute-done.3.refs_4_), kind=kLoop, calls=%fused_computation.5 | loop fusion | bytes 524288
  55.9 0.0 collective-permute-done.6.refs_0_
  55.9 0.8 collective-permute-done.7.refs_1_
  56.8 0.2 collective-permute-done.4.refs_5_
  56.9 0.0 collective-permute-done.5.refs_6_
  56.9 1.3 %collective-permute-start.8 = (f32[2,128,256]{2,1,0:T(8,128)S(1)}, f32[2,128,256]{2,1,0:T(8,128)S(1)}, u32[]{:S(2)}, u32[]{:S(2)}) collective-permute-start(f32[2,128,256]{2,1,0:T(8,128)S(1)} %collective-permute-done.4.refs_5_), channel_id=1, source_target_pairs={{0,8},{8,16},{16,24},{24,32},{32,40},{40,48},{48,56},{56,0},{1,9},... | collective-permute-start | bytes 786440 | tf_op jit(solution)/shard_map/ppermute | solution.py:452
  58.3 1.4 %collective-permute-start.9 = (f32[2,128,256]{2,1,0:T(8,128)S(1)}, f32[2,128,256]{2,1,0:T(8,128)S(1)}, u32[]{:S(2)}, u32[]{:S(2)}) collective-permute-start(f32[2,128,256]{2,1,0:T(8,128)S(1)} %collective-permute-done.5.refs_6_), channel_id=1, source_target_pairs={{8,0},{16,8},{24,16},{32,24},{40,32},{48,40},{56,48},{0,56},{9,1},... | collective-permute-start | bytes 786440 | tf_op jit(solution)/shard_map/ppermute | solution.py:453
  59.7 0.7 bitcast_dynamic-update-slice_fusion.3
  60.4 0.7 bitcast_dynamic-update-slice_fusion.2
  61.1 2.6 %collective-permute-done.8.refs_7_ = f32[2,128,256]{2,1,0:T(8,128)S(1)} collective-permute-done((f32[2,128,256]{2,1,0:T(8,128)S(1)}, f32[2,128,256]{2,1,0:T(8,128)S(1)}, u32[]{:S(2)}, u32[]{:S(2)}) %collective-permute-start.8) | collective-permute-done | bytes 262176 | tf_op jit(solution)/shard_map/ppermute | solution.py:452
  63.8 0.0 collective-permute-done.9.refs_8_
  63.8 0.8 bitcast_dynamic-update-slice_fusion.1
  64.6 0.7 bitcast_dynamic-update-slice_fusion
  65.3 3.3 %collective-permute-start.11 = (f32[7,2,128,256]{3,2,1,0:T(8,128)}, f32[7,2,128,256]{3,2,1,0:T(8,128)}, u32[]{:S(2)}, u32[]{:S(2)}) collective-permute-start(f32[7,2,128,256]{3,2,1,0:T(8,128)} %bitcast_dynamic-update-slice_fusion), channel_id=1, source_target_pairs={{0,4},{4,0},{1,5},{5,1},{2,6},{6,2},{3,7},{7,3},{8,12},{12,8},{9,1... | collective-permute-start | bytes 5505032 | tf_op jit(solution)/shard_map/ppermute | solution.py:461
  68.5 2.3 %collective-permute-start.10 = (f32[2,128,256]{2,1,0:T(8,128)S(1)}, f32[2,128,256]{2,1,0:T(8,128)S(1)}, u32[]{:S(2)}, u32[]{:S(2)}) collective-permute-start(f32[2,128,256]{2,1,0:T(8,128)S(1)} %collective-permute-done.8.refs_7_), channel_id=1, source_target_pairs={{0,8},{8,16},{16,24},{24,32},{32,40},{40,48},{48,56},{56,0},{1,9},... | collective-permute-start | bytes 786440 | tf_op jit(solution)/shard_map/ppermute | solution.py:455
  70.9 0.5 collective-permute-start.12
  71.4 0.0 copy-done.10
  71.4 7.9 %all-to-all-start.1 = ((f32[32,64,128]{2,1,0:T(8,128)}), f32[32,64,128]{2,1,0:T(8,128)}, u32[]{:S(2)}, u32[]{:S(2)}) async-start(f32[32,64,128]{2,1,0:T(8,128)} %shard_map.125), calls=%async_computation.1 | async-start | bytes 2097152 | tf_op jit(solution)/shard_map/all_to_all | solution.py:463
  79.4 0.0 collective-permute-done.10.refs_9_
  79.4 0.0 copy-start.13
  79.4 0.0 collective-permute-done.12.refs_11_
  79.4 0.0 collective-permute-done.11.refs_10_
  79.4 0.7 copy-done.13
  80.1 0.1 copy-done.14
  80.2 20.4 %shard_map.128 = (f32[128,1024]{1,0:T(8,128)}, f32[128,1024]{1,0:T(8,128)}) custom-call(s32[16]{0:T(128)} %lengths_ref.15, f32[128,1024]{1,0:T(8,128)} %collective-permute-done.6.refs_0_, f32[128,1024]{1,0:T(8,128)} %collective-permute-done.7.refs_1_, f32[2,128,256]{2,1,0:T(8,128)} %copy-done.7, f32[2,128,256]{2,1,0:T(8,128)} %copy-done.8, ...), custom_call_target="tpu_custom_call" | custom-call | flops 399999991808 | bytes 8000000 | tf_op jit(solution)/shard_map/pallas_call | solution.py:73
  100.6 1.9 %collective-permute-start.13 = (f32[128,1024]{1,0:T(8,128)}, f32[128,1024]{1,0:T(8,128)S(1)}, u32[]{:S(2)}, u32[]{:S(2)}) collective-permute-start(f32[128,1024]{1,0:T(8,128)} %get-tuple-element.49), channel_id=1, source_target_pairs={{0,0},{128,4},{4,64},{132,68},{64,128},{192,132},{68,192},{196,196... | collective-permute-start | bytes 1572872 | tf_op jit(solution)/shard_map/ppermute | solution.py:486
  102.5 3.3 %collective-permute-start.14 = (f32[128,1024]{1,0:T(8,128)}, f32[128,1024]{1,0:T(8,128)S(1)}, u32[]{:S(2)}, u32[]{:S(2)}) collective-permute-start(f32[128,1024]{1,0:T(8,128)} %get-tuple-element.50), channel_id=1, source_target_pairs={{64,0},{192,4},{68,64},{196,68},{0,128},{128,132},{4,192},{132,196... | collective-permute-start | bytes 1572872 | tf_op jit(solution)/shard_map/ppermute | solution.py:486
  105.8 0.0 all-to-all-done.1
  105.8 4.2 %shard_map.127 = f32[128,2048]{1,0:T(8,128)} custom-call(s32[16]{0:T(128)} %lengths_ref.15, f32[16,128]{1,0:T(8,128)} %rate_ref.5, f32[128,2048]{1,0:T(8,128)} %query_ref.2, f32[16,128,128]{2,1,0:T(8,128)} %bitcast.2.state_ref, f32[128,2048]{1,0:T(8,128)} %copy-done.3, f32[128,2048]{1,0:T(8,128)} %gate_ref.1, f32[1,2048]{1,0:T(1,128)} %bitcast.20), custom_call_target="tpu_custom_call" | custom-call | flops 1000 | bytes 1000 | tf_op jit(solution)/shard_map/pallas_call | solution.py:60
  109.9 8.7 %collective-permute-done.13.refs_0_ = f32[128,1024]{1,0:T(8,128)S(1)} collective-permute-done((f32[128,1024]{1,0:T(8,128)}, f32[128,1024]{1,0:T(8,128)S(1)}, u32[]{:S(2)}, u32[]{:S(2)}) %collective-permute-start.13) | collective-permute-done | bytes 524320 | tf_op jit(solution)/shard_map/ppermute | solution.py:486
  118.6 0.0 collective-permute-done.14.refs_1_
  118.6 1.6 %shard_map.129 = f32[128,2048]{1,0:T(8,128)} custom-call(s32[16]{0:T(128)S(1)} %copy-done.6, f32[128,1024]{1,0:T(8,128)S(1)} %collective-permute-done.13.refs_0_, f32[128,1024]{1,0:T(8,128)S(1)} %collective-permute-done.14.refs_1_), custom_call_target="tpu_custom_call" | custom-call | flops 1000 | bytes 1000 | tf_op jit(solution)/shard_map/pallas_call | solution.py:73
  (16 shorter events, 0.0 us)
Async XLA Ops:
  4.2 45.0 %all-to-all-start = ((f32[32,72,128]{2,1,0:T(8,128)}), f32[32,72,128]{2,1,0:T(8,128)S(1)}, u32[]{:S(2)}, u32[]{:S(2)}) async-start(f32[32,72,128]{2,1,0:T(8,128)} %shard_map.122), calls=%async_computation | async-start | bytes 2359296 | tf_op jit(solution)/shard_map/all_to_all | solution.py:418
  15.4 26.3 %copy-start = (f32[128,2048]{1,0:T(8,128)S(1)}, f32[128,2048]{1,0:T(8,128)}, u32[]{:S(2)}) copy-start(f32[128,2048]{1,0:T(8,128)} %key_ref.4) | copy-start | bytes 3145732
  15.5 26.3 %copy-start.1 = (f32[128,2048]{1,0:T(8,128)S(1)}, f32[128,2048]{1,0:T(8,128)}, u32[]{:S(2)}) copy-start(f32[128,2048]{1,0:T(8,128)} %value_ref.5) | copy-start | bytes 3145732
  15.5 26.3 %copy-start.4 = (f32[16,128]{1,0:T(8,128)S(1)}, f32[16,128]{1,0:T(8,128)}, u32[]{:S(2)}) copy-start(f32[16,128]{1,0:T(8,128)} %rate_ref.5) | copy-start | bytes 24580
  15.5 26.2 %copy-start.5 = (s32[16]{0:T(128)S(1)}, s32[16]{0:T(128)}, u32[]{:S(2)}) copy-start(s32[16]{0:T(128)} %lengths_ref.15) | copy-start | bytes 196
  17.7 9.9 %collective-permute-start.1 = (f32[128,256]{1,0:T(8,128)}, f32[128,256]{1,0:T(8,128)S(1)}, u32[]{:S(2)}, u32[]{:S(2)}) collective-permute-start(f32[128,256]{1,0:T(8,128)} %get-tuple-element.30), channel_id=1, source_target_pairs={{0,64},{4,192},{64,68},{68,196},{128,0},{132,128},{192,4},{196,132... | collective-permute-start | bytes 393224 | tf_op jit(solution)/shard_map/ppermute | solution.py:429
  21.3 8.3 %collective-permute-start = (f32[128,256]{1,0:T(8,128)}, f32[128,256]{1,0:T(8,128)S(1)}, u32[]{:S(2)}, u32[]{:S(2)}) collective-permute-start(f32[128,256]{1,0:T(8,128)} %get-tuple-element.29), channel_id=1, source_target_pairs={{0,0},{4,128},{64,4},{68,132},{128,64},{132,192},{192,68},{196,196... | collective-permute-start | bytes 393224 | tf_op jit(solution)/shard_map/ppermute | solution.py:429
  29.7 17.1 %copy-start.7 = (f32[2,128,256]{2,1,0:T(8,128)}, f32[2,128,256]{2,1,0:T(8,128)S(1)}, u32[]{:S(2)}) copy-start(f32[2,128,256]{2,1,0:T(8,128)S(1)} %pad_maximum_fusion.refs_2_) | copy-start | bytes 786436
  29.7 19.5 %collective-permute-start.2 = (f32[2,128,256]{2,1,0:T(8,128)S(1)}, f32[2,128,256]{2,1,0:T(8,128)S(1)}, u32[]{:S(2)}, u32[]{:S(2)}) collective-permute-start(f32[2,128,256]{2,1,0:T(8,128)S(1)} %pad_maximum_fusion.refs_2_), channel_id=1, source_target_pairs={{0,8},{8,16},{16,24},{24,32},{32,40},{40,48},{48,56},{56,0},{1,9},... | collective-permute-start | bytes 786440 | tf_op jit(solution)/shard_map/ppermute | solution.py:434
  30.5 18.7 %collective-permute-start.3 = (f32[2,128,256]{2,1,0:T(8,128)S(1)}, f32[2,128,256]{2,1,0:T(8,128)}, u32[]{:S(2)}, u32[]{:S(2)}) collective-permute-start(f32[2,128,256]{2,1,0:T(8,128)S(1)} %pad_maximum_fusion.refs_2_), channel_id=1, source_target_pairs={{8,0},{16,8},{24,16},{32,24},{40,32},{48,40},{56,48},{0,56},{9,1},... | collective-permute-start | bytes 786440 | tf_op jit(solution)/shard_map/ppermute | solution.py:435
  35.9 20.0 %collective-permute-start.6 = (f32[128,1024]{1,0:T(8,128)}, f32[128,1024]{1,0:T(8,128)}, u32[]{:S(2)}, u32[]{:S(2)}) collective-permute-start(f32[128,1024]{1,0:T(8,128)} %get-tuple-element.37), channel_id=1, source_target_pairs={{0,0},{4,128},{64,4},{68,132},{128,64},{132,192},{192,68},{196,196... | collective-permute-start | bytes 1572872 | tf_op jit(solution)/shard_map/ppermute | solution.py:441
  40.2 16.5 %collective-permute-start.7 = (f32[128,1024]{1,0:T(8,128)}, f32[128,1024]{1,0:T(8,128)}, u32[]{:S(2)}, u32[]{:S(2)}) collective-permute-start(f32[128,1024]{1,0:T(8,128)} %get-tuple-element.38), channel_id=1, source_target_pairs={{0,64},{4,192},{64,68},{68,196},{128,0},{132,128},{192,4},{196,132... | collective-permute-start | bytes 1572872 | tf_op jit(solution)/shard_map/ppermute | solution.py:441
  41.7 1.2 %copy-start.2 = (f32[128,2048]{1,0:T(8,128)S(1)}, f32[128,2048]{1,0:T(8,128)}, u32[]{:S(2)}) copy-start(f32[128,2048]{1,0:T(8,128)} %query_ref.2) | copy-start | bytes 3145732
  46.8 1.0 copy-start.3
  49.2 30.2 %copy-start.8 = (f32[2,128,256]{2,1,0:T(8,128)}, f32[2,128,256]{2,1,0:T(8,128)S(1)}, u32[]{:S(2)}) copy-start(f32[2,128,256]{2,1,0:T(8,128)S(1)} %collective-permute-done.2.refs_3_) | copy-start | bytes 786436
  49.2 7.7 %collective-permute-start.4 = (f32[2,128,256]{2,1,0:T(8,128)S(1)}, f32[2,128,256]{2,1,0:T(8,128)S(1)}, u32[]{:S(2)}, u32[]{:S(2)}) collective-permute-start(f32[2,128,256]{2,1,0:T(8,128)S(1)} %collective-permute-done.2.refs_3_), channel_id=1, source_target_pairs={{0,8},{8,16},{16,24},{24,32},{32,40},{40,48},{48,56},{56,0},{1,9},... | collective-permute-start | bytes 786440 | tf_op jit(solution)/shard_map/ppermute | solution.py:446
  49.3 7.7 %collective-permute-start.5 = (f32[2,128,256]{2,1,0:T(8,128)}, f32[2,128,256]{2,1,0:T(8,128)S(1)}, u32[]{:S(2)}, u32[]{:S(2)}) collective-permute-start(f32[2,128,256]{2,1,0:T(8,128)} %collective-permute-done.3.refs_4_), channel_id=1, source_target_pairs={{8,0},{16,8},{24,16},{32,24},{40,32},{48,40},{56,48},{0,56},{9,1},... | collective-permute-start | bytes 786440 | tf_op jit(solution)/shard_map/ppermute | solution.py:447
  56.9 14.5 %copy-start.9 = (f32[2,128,256]{2,1,0:T(8,128)}, f32[2,128,256]{2,1,0:T(8,128)S(1)}, u32[]{:S(2)}) copy-start(f32[2,128,256]{2,1,0:T(8,128)S(1)} %collective-permute-done.4.refs_5_) | copy-start | bytes 786436
  56.9 14.5 %copy-start.10 = (f32[2,128,256]{2,1,0:T(8,128)}, f32[2,128,256]{2,1,0:T(8,128)S(1)}, u32[]{:S(2)}) copy-start(f32[2,128,256]{2,1,0:T(8,128)S(1)} %collective-permute-done.5.refs_6_) | copy-start | bytes 786436
  56.9 6.8 %collective-permute-start.8 = (f32[2,128,256]{2,1,0:T(8,128)S(1)}, f32[2,128,256]{2,1,0:T(8,128)S(1)}, u32[]{:S(2)}, u32[]{:S(2)}) collective-permute-start(f32[2,128,256]{2,1,0:T(8,128)S(1)} %collective-permute-done.4.refs_5_), channel_id=1, source_target_pairs={{0,8},{8,16},{16,24},{24,32},{32,40},{40,48},{48,56},{56,0},{1,9},... | collective-permute-start | bytes 786440 | tf_op jit(solution)/shard_map/ppermute | solution.py:452
  58.3 5.5 %collective-permute-start.9 = (f32[2,128,256]{2,1,0:T(8,128)S(1)}, f32[2,128,256]{2,1,0:T(8,128)S(1)}, u32[]{:S(2)}, u32[]{:S(2)}) collective-permute-start(f32[2,128,256]{2,1,0:T(8,128)S(1)} %collective-permute-done.5.refs_6_), channel_id=1, source_target_pairs={{8,0},{16,8},{24,16},{32,24},{40,32},{48,40},{56,48},{0,56},{9,1},... | collective-permute-start | bytes 786440 | tf_op jit(solution)/shard_map/ppermute | solution.py:453
  63.8 15.7 %copy-start.11 = (f32[2,128,256]{2,1,0:T(8,128)}, f32[2,128,256]{2,1,0:T(8,128)S(1)}, u32[]{:S(2)}) copy-start(f32[2,128,256]{2,1,0:T(8,128)S(1)} %collective-permute-done.8.refs_7_) | copy-start | bytes 786436
  63.8 15.6 %copy-start.12 = (f32[2,128,256]{2,1,0:T(8,128)}, f32[2,128,256]{2,1,0:T(8,128)S(1)}, u32[]{:S(2)}) copy-start(f32[2,128,256]{2,1,0:T(8,128)S(1)} %collective-permute-done.9.refs_8_) | copy-start | bytes 786436
  65.3 14.1 %collective-permute-start.11 = (f32[7,2,128,256]{3,2,1,0:T(8,128)}, f32[7,2,128,256]{3,2,1,0:T(8,128)}, u32[]{:S(2)}, u32[]{:S(2)}) collective-permute-start(f32[7,2,128,256]{3,2,1,0:T(8,128)} %bitcast_dynamic-update-slice_fusion), channel_id=1, source_target_pairs={{0,4},{4,0},{1,5},{5,1},{2,6},{6,2},{3,7},{7,3},{8,12},{12,8},{9,1... | collective-permute-start | bytes 5505032 | tf_op jit(solution)/shard_map/ppermute | solution.py:461
  68.5 10.8 %collective-permute-start.10 = (f32[2,128,256]{2,1,0:T(8,128)S(1)}, f32[2,128,256]{2,1,0:T(8,128)S(1)}, u32[]{:S(2)}, u32[]{:S(2)}) collective-permute-start(f32[2,128,256]{2,1,0:T(8,128)S(1)} %collective-permute-done.8.refs_7_), channel_id=1, source_target_pairs={{0,8},{8,16},{16,24},{24,32},{32,40},{40,48},{48,56},{56,0},{1,9},... | collective-permute-start | bytes 786440 | tf_op jit(solution)/shard_map/ppermute | solution.py:455
  70.9 8.5 %collective-permute-start.12 = (f32[2,128,256]{2,1,0:T(8,128)S(1)}, f32[2,128,256]{2,1,0:T(8,128)S(1)}, u32[]{:S(2)}, u32[]{:S(2)}) collective-permute-start(f32[2,128,256]{2,1,0:T(8,128)S(1)} %collective-permute-done.9.refs_8_), channel_id=1, source_target_pairs={{0,60},{4,56},{8,4},{12,0},{16,12},{20,8},{24,20},{28,16},{32,28},... | collective-permute-start | bytes 786440 | tf_op jit(solution)/shard_map/ppermute | solution.py:459
  71.4 34.4 %all-to-all-start.1 = ((f32[32,64,128]{2,1,0:T(8,128)}), f32[32,64,128]{2,1,0:T(8,128)}, u32[]{:S(2)}, u32[]{:S(2)}) async-start(f32[32,64,128]{2,1,0:T(8,128)} %shard_map.125), calls=%async_computation.1 | async-start | bytes 2097152 | tf_op jit(solution)/shard_map/all_to_all | solution.py:463
  79.4 0.7 copy-start.13
  79.4 0.8 copy-start.14
  100.6 18.0 %collective-permute-start.13 = (f32[128,1024]{1,0:T(8,128)}, f32[128,1024]{1,0:T(8,128)S(1)}, u32[]{:S(2)}, u32[]{:S(2)}) collective-permute-start(f32[128,1024]{1,0:T(8,128)} %get-tuple-element.49), channel_id=1, source_target_pairs={{0,0},{128,4},{4,64},{132,68},{64,128},{192,132},{68,192},{196,196... | collective-permute-start | bytes 1572872 | tf_op jit(solution)/shard_map/ppermute | solution.py:486
  102.5 16.2 %collective-permute-start.14 = (f32[128,1024]{1,0:T(8,128)}, f32[128,1024]{1,0:T(8,128)S(1)}, u32[]{:S(2)}, u32[]{:S(2)}) collective-permute-start(f32[128,1024]{1,0:T(8,128)} %get-tuple-element.50), channel_id=1, source_target_pairs={{64,0},{192,4},{68,64},{196,68},{0,128},{128,132},{4,192},{132,196... | collective-permute-start | bytes 1572872 | tf_op jit(solution)/shard_map/ppermute | solution.py:486
  105.8 12.9 %copy-start.6 = (s32[16]{0:T(128)S(1)}, s32[16]{0:T(128)}, u32[]{:S(2)}) copy-start(s32[16]{0:T(128)} %lengths_ref.15) | copy-start | bytes 196
